TPU v7x, 32 devices: a whole 2x2x4 slice. The times are simulated.
32 devices in a mesh: rows: 8 (over y, x, core), cols: 4 (over z).
Axes of the slice: x: 2, y: 2, z: 4, core: 2. Of those that a mesh axis runs over, the one named last changes fastest.
Arguments:
- white_real: float32 [4096, 4096], P('rows', 'cols'), may hold values from -6 to 6
- white_imag: float32 [4096, 4096], P('rows', 'cols'), may hold values from -6 to 6
- covariates: bfloat16 [16, 4096, 4096], P(None, 'rows', 'cols'), may hold values from -6 to 6
- coefficients: float32 [16], replicated, may hold values from -0.9 to 0.9
- counts: int32 [4096, 4096], P('rows', 'cols'), may hold values from 0 to 5
- land_mask: int32 [4096, 4096], P('rows', 'cols'), may hold values from 0 to 1
- field_hyper: float32 [2], replicated, may hold values from 1 to 2
Outputs:
- step_real: float32 [4096, 4096], P('rows', 'cols')
- step_imag: float32 [4096, 4096], P('rows', 'cols')
- coef_grad: float32 [16], replicated
- objective: float32 [], replicated
All inputs are finite; a program needn't handle non-finite values.
Results may differ from a plain program's by a relative error of at most 0.0003.
Values sent between devices are 32-bit elements; how exact they have to be, the bound alone decides.
No kernel may reach another device: no remote copies, remote signals or barrier semaphores. Data moves between devices by JAX's collectives and lax.ppermute only.
A program may use at most 128 MiB of HBM per device.

v0:
```python
import math

import jax
import jax.numpy as jnp
from jax import lax
from jax.sharding import PartitionSpec as P

NG = 4096


lasso_weight = 0.02
ridge_weight = 0.1


def field_spectrum(field_hyper, wave_row, wave_col):
    amplitude = 0.2 * field_hyper[0]
    freq_range = field_hyper[1]
    radius = (wave_row[:, None] * wave_row[:, None] + wave_col[None, :] * wave_col[None, :]) / (
        freq_range * freq_range
    )
    return amplitude * (1.0 + NG / freq_range * jnp.power(1.0 + radius, -0.75))


def angle_table(left_len, right_len, modulus):
    product = lax.iota(jnp.int32, left_len)[:, None] * lax.iota(jnp.int32, right_len)[None, :]
    angles = (product % modulus).astype(jnp.float32) * (2.0 * math.pi / modulus)
    return (jnp.cos(angles), jnp.sin(angles))


def inverse_transform(pieces, want_real):
    highest = lax.Precision.HIGHEST
    components = pieces.shape[0]
    row_count = pieces.shape[1]
    length = pieces.shape[2]
    factor = 8
    others = length // factor
    shaped = pieces.reshape(components, row_count, others, factor)
    big_cos, big_sin = angle_table(others, others, others)

    def apply_big(table, block):
        return jnp.einsum("rnm,nk->rmk", block, table, precision=highest)

    if components == 2:
        real_mid = apply_big(big_cos, shaped[0]) - apply_big(big_sin, shaped[1])
        imag_mid = apply_big(big_sin, shaped[0]) + apply_big(big_cos, shaped[1])
    else:
        real_mid = apply_big(big_cos, shaped[0])
        imag_mid = apply_big(big_sin, shaped[0])
    tw_cos, tw_sin = angle_table(factor, others, length)
    real_tw = real_mid * tw_cos - imag_mid * tw_sin
    imag_tw = real_mid * tw_sin + imag_mid * tw_cos
    small_cos, small_sin = angle_table(factor, factor, factor)

    def apply_small(table, block):
        return jnp.einsum("rmk,mj->rjk", block, table, precision=highest)

    real_out = (apply_small(small_cos, real_tw) - apply_small(small_sin, imag_tw)).reshape(
        1, row_count, length
    )
    if want_real:
        return real_out
    imag_out = (apply_small(small_sin, real_tw) + apply_small(small_cos, imag_tw)).reshape(
        1, row_count, length
    )
    return jnp.concatenate([real_out, imag_out], axis=0)


def middle_step(spread):
    returned = lax.all_to_all(spread, "cols", split_axis=2, concat_axis=1, tiled=True)
    flipped = jnp.swapaxes(returned, 1, 2)
    return lax.all_to_all(flipped, "rows", split_axis=1, concat_axis=2, tiled=True)


def grid_transform(pieces, want_real):
    full_rows = lax.all_to_all(pieces, "cols", split_axis=1, concat_axis=2, tiled=True)
    halfway = inverse_transform(full_rows, False)
    columns = middle_step(halfway)
    second = inverse_transform(columns, want_real)
    blocks_out = lax.all_to_all(second, "rows", split_axis=2, concat_axis=1, tiled=True)
    return jnp.swapaxes(blocks_out, 1, 2) * (1.0 / NG)


def shards(white_real, white_imag, covariates, coefficients, counts, land_mask, field_hyper):
    highest = lax.Precision.HIGHEST
    rows_here = white_real.shape[0]
    cols_here = white_real.shape[1]
    freq_row = lax.axis_index("rows") * rows_here + lax.iota(jnp.int32, rows_here)
    freq_col = lax.axis_index("cols") * cols_here + lax.iota(jnp.int32, cols_here)
    wave_row = jnp.minimum(freq_row, NG - freq_row).astype(jnp.float32)
    wave_col = jnp.minimum(freq_col, NG - freq_col).astype(jnp.float32)
    spectrum = field_spectrum(field_hyper, wave_row, wave_col)
    scaled = jnp.stack([spectrum * white_real, spectrum * white_imag])
    latent = grid_transform(scaled, True)[0]
    cov_full = covariates.astype(jnp.float32)
    linear = jnp.einsum("j,jrc->rc", coefficients, cov_full, precision=highest)
    log_rate = linear + latent
    intensity = jnp.exp(log_rate)
    land_vals = land_mask.astype(jnp.float32)
    count_vals = counts.astype(jnp.float32)
    residual = land_vals * (intensity - count_vals)
    partial_coef = jnp.einsum("jrc,rc->j", cov_full, residual, precision=highest)
    partial_loss = jnp.sum(land_vals * (intensity - count_vals * log_rate)) + 0.5 * jnp.sum(
        white_real * white_real + white_imag * white_imag
    )
    adjoint = grid_transform(residual[None], False)
    total_coef, total_loss = lax.psum((partial_coef, partial_loss), ("rows", "cols"))
    per_cell = 1.0 / (NG * NG)
    coef_grad = (
        total_coef * per_cell + lasso_weight * jnp.sign(coefficients) + ridge_weight * coefficients
    )
    objective = (
        total_loss * per_cell
        + lasso_weight * jnp.sum(jnp.abs(coefficients))
        + 0.5 * ridge_weight * jnp.sum(coefficients * coefficients)
    )
    curvature = 1.0 + spectrum * spectrum
    step_real = (spectrum * adjoint[0] + white_real) / curvature
    step_imag = (white_imag - spectrum * adjoint[1]) / curvature
    return (step_real, step_imag, coef_grad, objective)


def solution(mesh):
    return jax.shard_map(
        shards,
        mesh=mesh,
        in_specs=(
            P("rows", "cols"),
            P("rows", "cols"),
            P(None, "rows", "cols"),
            P(),
            P("rows", "cols"),
            P("rows", "cols"),
            P(),
        ),
        out_specs=(P("rows", "cols"), P("rows", "cols"), P(), P()),
        check_vma=False,
    )
```

profile of v0, /device:TPU:0, one launch (start us, length us, event | category | flops | bytes accessed | tf_op | source)
XLA Modules:
  0.0 897.2 jit_solution(2084490301962304620)
XLA Ops:
  24.7 93.3 %all-to-all-done = f32[2,512,1024]{2,0,1:T(2,128)} async-done(((f32[2,512,1024]{2,0,1:T(2,128)}), f32[2,512,1024]{2,0,1:T(2,128)}, u32[]{:S(2)}, u32[]{:S(2)}) %all-to-all-start) | async-done | bytes 4194336 | tf_op jit(solution)/shard_map/all_to_all | solution.py:75
  127.7 10.2 %fusion.62 = f32[128,8,512]{2,0,1:T(8,128)} fusion(f32[128,512,8]{1,0,2:T(8,128)} %copy.151), kind=kOutput, calls=%fused_computation.88 | convolution fusion | flops 3224895488 | bytes 4194304 | tf_op jit(solution)/shard_map/rnm,nk->rmk/dot_general | solution.py:41
  137.9 8.4 fusion.74
  150.1 9.9 %convolution_subtract_fusion.2 = f32[128,8,512]{2,0,1:T(8,128)S(1)} fusion(f32[128,8,512]{2,0,1:T(8,128)} %fusion.74, f32[128,512,8]{1,0,2:T(8,128)S(1)} %copy.153), kind=kOutput, calls=%fused_computation.73 | convolution fusion | flops 3225419776 | bytes 6291456 | tf_op jit(solution)/shard_map/rnm,nk->rmk/dot_general | solution.py:41
  160.0 9.0 multiply_subtract_fusion.3
  192.5 95.3 %all_to_all.114 = f32[2,128,4096]{1,0,2:T(2,128)S(1)} all-to-all(f32[2,128,4096]{1,0,2:T(2,128)S(1)} %pad_maximum_fusion.1), channel_id=1, replica_groups=mesh['rows'=8,'cols'=4] {'cols'}, dimensions={2} | all-to-all | bytes 8388608 | tf_op jit(solution)/shard_map/all_to_all | solution.py:69
  302.8 52.9 %all_to_all.115 = f32[2,1024,512]{2,0,1:T(2,128)S(1)} all-to-all(f32[2,1024,512]{2,0,1:T(2,128)} %copy.164), channel_id=1, replica_groups=mesh['rows'=8,'cols'=4] {'rows'}, dimensions={1} | all-to-all | bytes 8388608 | tf_op jit(solution)/shard_map/all_to_all | solution.py:71
  362.9 10.3 %fusion.59 = f32[128,8,512]{2,0,1:T(8,128)} fusion(f32[128,512,8]{1,0,2:T(8,128)} %copy.167), kind=kOutput, calls=%fused_computation.85 | convolution fusion | flops 3224895488 | bytes 4194304 | tf_op jit(solution)/shard_map/rnm,nk->rmk/dot_general | solution.py:41
  373.2 8.4 fusion.71
  385.3 9.9 %convolution_subtract_fusion.1 = f32[128,8,512]{2,0,1:T(8,128)S(1)} fusion(f32[128,8,512]{2,0,1:T(8,128)} %fusion.71, f32[128,512,8]{1,0,2:T(8,128)S(1)} %copy.169), kind=kOutput, calls=%fused_computation.71 | convolution fusion | flops 3225419776 | bytes 6291456 | tf_op jit(solution)/shard_map/rnm,nk->rmk/dot_general | solution.py:41
  395.3 9.0 multiply_subtract_fusion.2
  416.1 22.7 %fusion = f32[1,512,1024]{2,0,1:T(1,128)} fusion(bf16[16,512,1024]{2,1,0:T(8,128)(2,1)} %param.9, f32[16]{0:T(128)S(1)} %copy-done.18), kind=kOutput, calls=%fused_computation.1 | convolution fusion | flops 100663296 | bytes 18874432 | tf_op jit(solution)/shard_map/j,jrc->rc/dot_general | solution.py:95
  449.4 48.1 %all_to_all.116 = f32[1,512,1024]{2,0,1:T(1,128)S(1)} all-to-all(f32[1,512,1024]{2,0,1:T(1,128)S(1)} %broadcast_in_dim.2), channel_id=1, replica_groups=mesh['rows'=8,'cols'=4] {'cols'}, dimensions={1} | all-to-all | bytes 4194304 | tf_op jit(solution)/shard_map/all_to_all | solution.py:75
  501.7 8.4 fusion.68
  510.1 8.9 multiply_subtract_fusion.1
  542.3 94.5 %all_to_all.117 = f32[2,128,4096]{1,0,2:T(2,128)S(1)} all-to-all(f32[2,128,4096]{1,0,2:T(2,128)S(1)} %pad_maximum_fusion.2), channel_id=1, replica_groups=mesh['rows'=8,'cols'=4] {'cols'}, dimensions={2} | all-to-all | bytes 8388608 | tf_op jit(solution)/shard_map/all_to_all | solution.py:69
  651.7 54.8 %all_to_all.118 = f32[2,1024,512]{2,0,1:T(2,128)S(1)} all-to-all(f32[2,1024,512]{2,0,1:T(2,128)} %copy.187), channel_id=1, replica_groups=mesh['rows'=8,'cols'=4] {'rows'}, dimensions={1} | all-to-all | bytes 8388608 | tf_op jit(solution)/shard_map/all_to_all | solution.py:71
  713.8 10.3 %fusion.54 = f32[128,8,512]{2,0,1:T(8,128)} fusion(f32[128,512,8]{1,0,2:T(8,128)} %copy.190), kind=kOutput, calls=%fused_computation.80 | convolution fusion | flops 3224895488 | bytes 4194304 | tf_op jit(solution)/shard_map/rnm,nk->rmk/dot_general | solution.py:41
  724.0 8.4 fusion.66
  736.2 9.9 %convolution_subtract_fusion = f32[128,8,512]{2,0,1:T(8,128)S(1)} fusion(f32[128,8,512]{2,0,1:T(8,128)} %fusion.66, f32[128,512,8]{1,0,2:T(8,128)S(1)} %copy.192), kind=kOutput, calls=%fused_computation.69 | convolution fusion | flops 3225419776 | bytes 6291456 | tf_op jit(solution)/shard_map/rnm,nk->rmk/dot_general | solution.py:41
  746.2 9.2 %multiply_subtract_fusion = (f32[128,8,512]{2,0,1:T(8,128)S(1)}, f32[128,8,512]{2,0,1:T(8,128)S(1)}) fusion(f32[128,8,512]{2,0,1:T(8,128)S(1)} %convolution_subtract_fusion, f32[8,512]{1,0:T(8,128)S(1)} %get-tuple-element.32, f32[8,512]{1,0:T(8,128)S(1)} %get-tuple-element.33, f32[128,8,512]{2,0,1:T(8,128)S(1)} %copy-done.7, f32[128,512,8]{1,0,2:T(8,128)S(1)} %copy.192), kind=kOutput, calls=%fused_computation.29 | convolution fusion | flops 3228565504 | bytes 10518528 | tf_op jit(solution)/shard_map/rnm,nk->rmk/dot_general | solution.py:41
  784.8 7.5 multiply_reduce_fusion
  792.3 41.6 %all-to-all-done.7 = f32[2,128,4096]{1,0,2:T(2,128)} async-done(((f32[2,128,4096]{1,0,2:T(2,128)}), f32[2,128,4096]{1,0,2:T(2,128)}, u32[]{:S(2)}, u32[]{:S(2)}) %all-to-all-start.7) | async-done | bytes 4194336 | tf_op jit(solution)/shard_map/all_to_all | solution.py:79
  854.8 38.0 %all-reduce = (f32[16]{0:T(128)S(1)}, f32[]{:T(128)}) all-reduce(f32[16]{0:T(128)S(1)} %multiply_reduce_fusion, f32[]{:T(128)S(6)} %add.265), channel_id=1, replica_groups=mesh['rows'=8,'cols'=4] {'rows','cols'}, use_global_device_ids=true, to_apply=%region_0.1 | all-reduce | flops 17 | bytes 136 | tf_op jit(solution)/shard_map/psum | solution.py:106
  (109 shorter events, 210.1 us)
Async XLA Ops:
  3.9 4.5 copy-start.16
  4.0 4.5 copy-start.14
  17.9 100.2 %all-to-all-start = ((f32[2,512,1024]{2,0,1:T(2,128)}), f32[2,512,1024]{2,0,1:T(2,128)}, u32[]{:S(2)}, u32[]{:S(2)}) async-start(f32[2,512,1024]{2,0,1:T(2,128)} %pad_maximum_fusion), calls=%async_computation | async-start | bytes 8388608 | tf_op jit(solution)/shard_map/all_to_all | solution.py:75
  127.7 10.3 %copy-start.10 = (f32[128,512,8]{1,0,2:T(8,128)S(1)}, f32[128,512,8]{1,0,2:T(8,128)}, u32[]{:S(2)}) copy-start(f32[128,512,8]{1,0,2:T(8,128)} %copy.151) | copy-start | bytes 6291460
  137.9 8.4 copy-start.3
  150.1 9.9 %copy-start.8 = (f32[128,8,512]{2,0,1:T(8,128)S(1)}, f32[128,8,512]{2,0,1:T(8,128)}, u32[]{:S(2)}) copy-start(f32[128,8,512]{2,0,1:T(8,128)} %fusion.62) | copy-start | bytes 6291460
  362.9 10.3 %copy-start.11 = (f32[128,512,8]{1,0,2:T(8,128)S(1)}, f32[128,512,8]{1,0,2:T(8,128)}, u32[]{:S(2)}) copy-start(f32[128,512,8]{1,0,2:T(8,128)} %copy.167) | copy-start | bytes 6291460
  373.2 8.4 copy-start.4
  385.3 9.9 %copy-start.9 = (f32[128,8,512]{2,0,1:T(8,128)S(1)}, f32[128,8,512]{2,0,1:T(8,128)}, u32[]{:S(2)}) copy-start(f32[128,8,512]{2,0,1:T(8,128)} %fusion.59) | copy-start | bytes 6291460
  411.9 4.2 copy-start.18
  411.9 30.7 %all-to-all-start.3 = ((f32[1,128,4096]{1,0,2:T(1,128)}), f32[1,128,4096]{1,0,2:T(1,128)S(1)}, u32[]{:S(2)}, u32[]{:S(2)}) async-start(f32[1,128,4096]{1,0,2:T(1,128)} %bitcast.209), calls=%async_computation.3 | async-start | bytes 4194304 | tf_op jit(solution)/shard_map/all_to_all | solution.py:79
  442.6 2.0 copy-start.6
  442.6 2.2 copy-start.13
  447.9 1.4 copy-start
  713.8 10.3 %copy-start.12 = (f32[128,512,8]{1,0,2:T(8,128)S(1)}, f32[128,512,8]{1,0,2:T(8,128)}, u32[]{:S(2)}) copy-start(f32[128,512,8]{1,0,2:T(8,128)} %copy.190) | copy-start | bytes 6291460
  724.0 8.4 copy-start.5
  736.2 10.0 %copy-start.7 = (f32[128,8,512]{2,0,1:T(8,128)S(1)}, f32[128,8,512]{2,0,1:T(8,128)}, u32[]{:S(2)}) copy-start(f32[128,8,512]{2,0,1:T(8,128)} %fusion.54) | copy-start | bytes 6291460
  780.1 4.7 copy-start.1
  780.1 53.8 %all-to-all-start.7 = ((f32[2,128,4096]{1,0,2:T(2,128)}), f32[2,128,4096]{1,0,2:T(2,128)}, u32[]{:S(2)}, u32[]{:S(2)}) async-start(f32[2,128,4096]{1,0,2:T(2,128)} %pad_maximum_fusion.3), calls=%async_computation.7 | async-start | bytes 8388608 | tf_op jit(solution)/shard_map/all_to_all | solution.py:79
  842.2 5.0 copy-start.2
  842.2 5.0 copy-start.15
  842.2 5.0 copy-start.17
where the time goes:
time: 906 us; the launch traced here: 897 us
  blocking collectives  384 us (42%)
  matrix products  197 us (22%)
  waiting for transfers between devices  139 us (15%)
  local copies, waits for them, and re-layouts  102 us (11%)
  other arithmetic  51 us (6%)
  starting transfers between devices  15.6 us (2%)
    all_to_all x2, blocking collectives, middle_step(): lax.all_to_all(spread, 'cols', split_axis=2, concat_axis=1, tiled=True)  190 us
    dot_general x14, matrix products, apply_big(): return jnp.einsum('rnm,nk->rmk', block, table, precision=highest)  130 us
    all_to_all x2, blocking collectives, middle_step(): lax.all_to_all(flipped, 'rows', split_axis=1, concat_axis=2, tiled=True)  108 us
    all_to_all x1, waiting for transfers between devices, grid_transform(): lax.all_to_all(pieces, 'cols', split_axis=1, concat_axis=2, tiled=True)  93.3 us
    all_to_all x1, blocking collectives, grid_transform(): lax.all_to_all(pieces, 'cols', split_axis=1, concat_axis=2, tiled=True)  48.1 us
    all_to_all x2, waiting for transfers between devices, grid_transform(): lax.all_to_all(second, 'rows', split_axis=2, concat_axis=1, tiled=True)  45.5 us
    dot_general x14, matrix products, apply_small(): return jnp.einsum('rmk,mj->rjk', block, table, precision=highest)  44.6 us
    psum x1, blocking collectives, shards(): lax.psum((partial_coef, partial_loss), ('rows', 'cols'))  38 us
  transfers between devices with their start and end apart: 3, of which 3 were waited for; matrix products, arithmetic and copies ran while one was open for 3% of the time, Pallas kernels for 0%

commit v1 on v0

--- a/solution.py
+++ b/solution.py
@@ -2,14 +2,565 @@
 
 import jax
 import jax.numpy as jnp
+import ml_dtypes
+import numpy as np
 from jax import lax
+from jax.experimental import pallas as pl
+from jax.experimental.pallas import tpu as pltpu
 from jax.sharding import PartitionSpec as P
 
 NG = 4096
-
+LANES = 128
+HALF = LANES // 2
+RADIX = 16
+DENSE = NG // RADIX
 
 lasso_weight = 0.02
 ridge_weight = 0.1
+
+
+def split3(values):
+    first = values.astype(ml_dtypes.bfloat16)
+    rest = values - first.astype(np.float64)
+    second = rest.astype(ml_dtypes.bfloat16)
+    rest = rest - second.astype(np.float64)
+    return first, second, rest.astype(ml_dtypes.bfloat16)
+
+
+def dense_table():
+    index = np.arange(DENSE)
+    angles = (index[:, None] * index[None, :] % DENSE) * (2.0 * np.pi / DENSE)
+    one, two, three = split3(np.concatenate([np.cos(angles), np.sin(angles)], axis=0))
+    return np.concatenate([one, one, one, two, two, three], axis=1)
+
+
+def twiddle_table():
+    angles = np.arange(DENSE)[:, None] * np.arange(RADIX)[None, :] * (2.0 * np.pi / NG)
+    table = np.zeros((DENSE, LANES), np.float32)
+    table[:, :RADIX] = np.cos(angles)
+    table[:, RADIX : 2 * RADIX] = np.sin(angles)
+    return table
+
+
+def half_sign():
+    lane = lax.broadcasted_iota(jnp.int32, (1, LANES), 1)
+    return jnp.where(lane < HALF, -1.0, 1.0).astype(jnp.float32)
+
+
+class Packed:
+    def __init__(self, sign):
+        self.sign = sign
+
+    def add(self, a, b):
+        return a + b
+
+    def sub(self, a, b):
+        return a - b
+
+    def turn(self, a):
+        return pltpu.roll(a, HALF, 1) * self.sign
+
+    def mul(self, a, c, s):
+        return a * c + self.turn(a) * s
+
+
+class Pairs:
+    def add(self, a, b):
+        return tuple(y if x is None else x if y is None else x + y for x, y in zip(a, b))
+
+    def sub(self, a, b):
+        return tuple((None if y is None else -y) if x is None else x if y is None else x - y for x, y in zip(a, b))
+
+    def turn(self, a):
+        return (None if a[1] is None else -a[1], a[0])
+
+    def mul(self, a, c, s):
+        re, im = a
+        if im is None:
+            return (re * c, re * s)
+        if re is None:
+            return (-(im * s), im * c)
+        return (re * c - im * s, re * s + im * c)
+
+
+def dft4(ops, z):
+    even, odd = ops.add(z[0], z[2]), ops.sub(z[0], z[2])
+    even2, turned = ops.add(z[1], z[3]), ops.turn(ops.sub(z[1], z[3]))
+    return [ops.add(even, even2), ops.add(odd, turned), ops.sub(even, even2), ops.sub(odd, turned)]
+
+
+def dft16(ops, z):
+    columns = []
+    for q in range(4):
+        column = dft4(ops, [z[4 * p + q] for p in range(4)])
+        for u in range(1, 4):
+            turns = q * u
+            if turns == 4:
+                column[u] = ops.turn(column[u])
+            elif turns:
+                angle = 2.0 * math.pi * turns / RADIX
+                column[u] = ops.mul(column[u], math.cos(angle), math.sin(angle))
+        columns.append(column)
+    out = [None] * RADIX
+    for u in range(4):
+        for v, value in enumerate(dft4(ops, [columns[q][u] for q in range(4)])):
+            out[u + 4 * v] = value
+    return out
+
+
+def dense_product(table, values):
+    one = values.astype(jnp.bfloat16)
+    rest = values - one.astype(jnp.float32)
+    two = rest.astype(jnp.bfloat16)
+    three = (rest - two.astype(jnp.float32)).astype(jnp.bfloat16)
+    parts = jnp.concatenate([one, two, three], axis=0)
+
+    def dot(left, right):
+        return jnp.dot(left, right, preferred_element_type=jnp.float32)
+
+    small = dot(table[:, 5 * DENSE :], parts[:DENSE]) + dot(table[:, 3 * DENSE : 5 * DENSE], parts[: 2 * DENSE])
+    return small + dot(table[:, : 3 * DENSE], parts)
+
+
+def spectrum_of(hyper, first_row, first_col, shape):
+    rows = lax.broadcasted_iota(jnp.int32, shape, 0) + first_row
+    cols = lax.broadcasted_iota(jnp.int32, shape, 1) + first_col
+    wave_row = jnp.minimum(rows, NG - rows).astype(jnp.float32)
+    wave_col = jnp.minimum(cols, NG - cols).astype(jnp.float32)
+    amplitude = 0.2 * hyper[0]
+    span = hyper[1]
+    base = 1.0 + (wave_row * wave_row + wave_col * wave_col) * (1.0 / (span * span))
+    return amplitude * (1.0 + (NG / span) / jnp.sqrt(base * jnp.sqrt(base)))
+
+
+def scale_kernel(count, place, hyper, real_ref, imag_ref, *outs):
+    height = real_ref.shape[0]
+    width = real_ref.shape[1]
+    me, first_row, first_col = place[0], place[1], place[2]
+    squares_ref = outs[-1]
+    lane = lax.broadcasted_iota(jnp.int32, (1, LANES), 1)
+    low = lane < HALF
+    step = 64
+    squares_ref[...] = jnp.zeros_like(squares_ref)
+    for k in range(count):
+        other = jnp.bitwise_xor(me, k)
+        start = pl.multiple_of(other * LANES, LANES)
+
+        def body(i, carry, k=k, start=start):
+            row = pl.multiple_of(i * step, step)
+            real = real_ref[pl.ds(row, step), pl.ds(start, LANES)]
+            imag = imag_ref[pl.ds(row, step), pl.ds(start, LANES)]
+            spec = spectrum_of(hyper, first_row + row, first_col + start, (step, LANES))
+            squares = (real * real + imag * imag).reshape(step // 8, 8, LANES)
+            squares_ref[...] += jnp.sum(squares, axis=0)
+            real, imag = spec * real, spec * imag
+            outs[k][pl.ds(row, step), :] = jnp.where(low, real, pltpu.roll(imag, HALF, 1))
+            outs[count + k][pl.ds(row, step), :] = jnp.where(low, pltpu.roll(real, HALF, 1), imag)
+            return carry
+
+        lax.fori_loop(0, height // step, body, 0)
+
+
+def first_axis_kernel(n_in, n_out, place, table_ref, twiddle_ref, *refs):
+    ins, outs, (work, done) = refs[:n_in], refs[n_in : n_in + n_out], refs[n_in + n_out :]
+    me = place[0]
+    sign = half_sign()
+    ops = Packed(sign)
+    if n_in > 1:
+        height = ins[0].shape[0]
+        for k in range(n_in):
+            start = pl.multiple_of(jnp.bitwise_xor(me, k) * height, height)
+            work[pl.ds(start, height), :] = ins[k][...]
+        source = work
+    else:
+        source = ins[0]
+    target = done if n_out > 1 else outs[0]
+    step = 16
+
+    def butterflies(i, carry):
+        row = pl.multiple_of(i * step, step)
+        z = dft16(ops, [source[pl.ds(row + DENSE * a, step), :] for a in range(RADIX)])
+        factors = twiddle_ref[pl.ds(row, step), :]
+        work[pl.ds(row, step), :] = z[0]
+        for x in range(1, RADIX):
+            cos = jnp.broadcast_to(factors[:, x : x + 1], (step, LANES))
+            sin = jnp.broadcast_to(factors[:, RADIX + x : RADIX + x + 1], (step, LANES))
+            work[pl.ds(row + DENSE * x, step), :] = ops.mul(z[x], cos, sin)
+        return carry
+
+    lax.fori_loop(0, DENSE // step, butterflies, 0)
+
+    def products(p, carry):
+        row = pl.multiple_of(p * 2 * DENSE, 2 * DENSE)
+        values = jnp.concatenate([work[pl.ds(row, DENSE), :], work[pl.ds(row + DENSE, DENSE), :]], axis=1)
+        both = dense_product(table_ref, values)
+        for h in range(2):
+            lanes = slice(h * LANES, (h + 1) * LANES)
+            value = both[:DENSE, lanes] + ops.turn(both[DENSE:, lanes])
+            target[pl.ds(2 * p + h, DENSE, stride=RADIX), :] = value
+        return carry
+
+    lax.fori_loop(0, RADIX // 2, products, 0)
+    if n_out > 1:
+        height = outs[0].shape[0]
+        for k in range(n_out):
+            start = pl.multiple_of(jnp.bitwise_xor(me, k) * height, height)
+            outs[k][...] = done[pl.ds(start, height), :]
+
+
+def second_axis_kernel(n_rows, n_cols, place, table_ref, twiddle_ref, *refs):
+    ins, outs, (real, imag, done) = refs[:2], refs[2 : 2 + n_cols], refs[2 + n_cols :]
+    me = place[1]
+    for r in range(n_rows):
+        for c in range(n_cols):
+            for j in range(2):
+                turned = ins[j][r * n_cols + c].T
+                row = (c * n_rows + r) * LANES + j * HALF
+                real[row : row + HALF, :] = turned[:HALF]
+                imag[row : row + HALF, :] = turned[HALF:]
+    ops = Pairs()
+    step = 8
+
+    def butterflies(i, carry):
+        row = pl.multiple_of(i * step, step)
+        where = [pl.ds(row + DENSE * a, step) for a in range(RADIX)]
+        z = dft16(ops, [(real[at, :], imag[at, :]) for at in where])
+        factors = twiddle_ref[pl.ds(row, step), :]
+        for x in range(RADIX):
+            value = z[x]
+            if x:
+                cos = jnp.broadcast_to(factors[:, x : x + 1], (step, LANES))
+                sin = jnp.broadcast_to(factors[:, RADIX + x : RADIX + x + 1], (step, LANES))
+                value = ops.mul(value, cos, sin)
+            real[where[x], :], imag[where[x], :] = value
+        return carry
+
+    lax.fori_loop(0, DENSE // step, butterflies, 0)
+
+    def products(p, carry):
+        row = pl.multiple_of(p * 2 * DENSE, 2 * DENSE)
+        here = [pl.ds(row, DENSE), pl.ds(row + DENSE, DENSE)]
+        one = dense_product(table_ref.at[:DENSE], jnp.concatenate([real[at, :] for at in here], axis=1))
+        two = dense_product(table_ref.at[DENSE:], jnp.concatenate([imag[at, :] for at in here], axis=1))
+        both = one - two
+        for h in range(2):
+            done[pl.ds(2 * p + h, DENSE, stride=RADIX), :] = both[:, h * LANES : (h + 1) * LANES]
+        return carry
+
+    lax.fori_loop(0, RADIX // 2, products, 0)
+    width = NG // n_cols
+    for k in range(n_cols):
+        start = jnp.bitwise_xor(me, k) * width
+        for t in range(width // LANES):
+            tile = done[pl.ds(pl.multiple_of(start + t * LANES, LANES), LANES), :]
+            outs[k][:, t * LANES : (t + 1) * LANES] = tile.T
+
+
+def second_axis_back_kernel(n_rows, n_cols, place, table_ref, twiddle_ref, *refs):
+    ins, outs, (real, imag, real_out, imag_out) = refs[:n_cols], refs[n_cols : n_cols + 2], refs[n_cols + 2 :]
+    me = place[1]
+    width = NG // n_cols
+    for k in range(n_cols):
+        start = jnp.bitwise_xor(me, k) * width
+        for t in range(width // LANES):
+            tile = ins[k][:, t * LANES : (t + 1) * LANES].T
+            real[pl.ds(pl.multiple_of(start + t * LANES, LANES), LANES), :] = tile
+    ops = Pairs()
+    step = 8
+
+    def butterflies(i, carry):
+        row = pl.multiple_of(i * step, step)
+        where = [pl.ds(row + DENSE * a, step) for a in range(RADIX)]
+        z = dft16(ops, [(real[at, :], None) for at in where])
+        factors = twiddle_ref[pl.ds(row, step), :]
+        for x in range(RADIX):
+            value = z[x]
+            if x:
+                cos = jnp.broadcast_to(factors[:, x : x + 1], (step, LANES))
+                sin = jnp.broadcast_to(factors[:, RADIX + x : RADIX + x + 1], (step, LANES))
+                value = ops.mul(value, cos, sin)
+            real[where[x], :] = value[0]
+            imag[where[x], :] = jnp.zeros((step, LANES), jnp.float32) if value[1] is None else value[1]
+        return carry
+
+    lax.fori_loop(0, DENSE // step, butterflies, 0)
+
+    def products(x, carry):
+        at = pl.ds(pl.multiple_of(x * DENSE, DENSE), DENSE)
+        both = dense_product(table_ref, jnp.concatenate([real[at, :], imag[at, :]], axis=1))
+        rows = pl.ds(x, DENSE, stride=RADIX)
+        real_out[rows, :] = both[:DENSE, :LANES] - both[DENSE:, LANES:]
+        imag_out[rows, :] = both[DENSE:, :LANES] + both[:DENSE, LANES:]
+        return carry
+
+    lax.fori_loop(0, RADIX, products, 0)
+    for r in range(n_rows):
+        for c in range(n_cols):
+            for j in range(2):
+                row = (c * n_rows + r) * LANES + j * HALF
+                tile = jnp.concatenate([real_out[row : row + HALF, :], imag_out[row : row + HALF, :]], axis=0)
+                outs[j][r * n_cols + c] = tile.T
+
+
+def cell_kernel(n_cov, place, coefficients, latent_ref, cov_ref, counts_ref, mask_ref, residual_ref, sums_ref):
+    @pl.when(pl.program_id(0) == 0)
+    def _():
+        sums_ref[...] = jnp.zeros_like(sums_ref)
+
+    height = latent_ref.shape[0]
+    width = latent_ref.shape[1]
+    step = 16
+
+    def fold(value):
+        return value[:8] + value[8:]
+
+    for row in range(0, height, step):
+        rows = slice(row, row + step)
+
+        def body(t, carry, rows=rows):
+            lanes = pl.ds(pl.multiple_of(t * LANES, LANES), LANES)
+            total = latent_ref[rows, lanes] * (1.0 / NG)
+            for j in range(n_cov):
+                total += coefficients[j] * cov_ref[j, rows, lanes].astype(jnp.float32)
+            intensity = jnp.exp(total)
+            land = mask_ref[rows, lanes].astype(jnp.float32)
+            count = counts_ref[rows, lanes].astype(jnp.float32)
+            residual = land * (intensity - count)
+            residual_ref[rows, lanes] = residual
+            for j in range(n_cov):
+                sums_ref[j] += fold(cov_ref[j, rows, lanes].astype(jnp.float32) * residual)
+            sums_ref[n_cov] += fold(land * (intensity - count * total))
+            return carry
+
+        lax.fori_loop(0, width // LANES, body, 0)
+
+
+def final_kernel(count, place, hyper, real_ref, imag_ref, *refs):
+    blocks, (step_real_ref, step_imag_ref) = refs[: 2 * count], refs[2 * count :]
+    height = real_ref.shape[0]
+    me, first_row, first_col = place[0], place[1], place[2]
+    lane = lax.broadcasted_iota(jnp.int32, (1, LANES), 1)
+    low = lane < HALF
+    step = 64
+    first_row = first_row + pl.program_id(0) * height
+    for k in range(count):
+        start = pl.multiple_of(jnp.bitwise_xor(me, k) * LANES, LANES)
+        for row in range(0, height, step):
+            rows = pl.ds(row, step)
+            lanes = pl.ds(start, LANES)
+            spec = spectrum_of(hyper, first_row + row, first_col + start, (step, LANES))
+            inverse = 1.0 / (1.0 + spec * spec)
+            spec = spec * (1.0 / NG)
+            one, two = blocks[k][rows, :], blocks[count + k][rows, :]
+            adjoint_real = jnp.where(low, one, pltpu.roll(two, HALF, 1))
+            adjoint_imag = jnp.where(low, pltpu.roll(one, HALF, 1), two)
+            step_real_ref[rows, lanes] = (spec * adjoint_real + real_ref[rows, lanes]) * inverse
+            step_imag_ref[rows, lanes] = (imag_ref[rows, lanes] - spec * adjoint_imag) * inverse
+
+
+SMEM = pl.BlockSpec(memory_space=pltpu.SMEM)
+VMEM = pl.BlockSpec(memory_space=pltpu.VMEM)
+
+
+def f32(*shape):
+    return jax.ShapeDtypeStruct(shape, jnp.float32)
+
+
+def params(mib):
+    return pltpu.CompilerParams(vmem_limit_bytes=mib << 20)
+
+
+def cost(flops, nbytes):
+    return pl.CostEstimate(flops=int(flops), bytes_accessed=int(nbytes), transcendentals=0)
+
+
+def call_scale(place, hyper, real, imag, n_rows):
+    def kernel(*refs):
+        scale_kernel(n_rows, *refs)
+
+    height = real.shape[0]
+    out = pl.pallas_call(
+        kernel,
+        name="scale",
+        out_shape=[f32(height, LANES)] * (2 * n_rows) + [f32(8, LANES)],
+        in_specs=[SMEM, SMEM, VMEM, VMEM],
+        out_specs=[VMEM] * (2 * n_rows + 1),
+        compiler_params=params(32),
+        cost_estimate=cost(4e9, 4 * 4 * real.size),
+    )(place, hyper, real, imag)
+    return out[:n_rows], out[n_rows : 2 * n_rows], out[-1]
+
+
+def call_first_axis(place, tables, ins, n_out):
+    n_in = len(ins)
+
+    def kernel(*refs):
+        first_axis_kernel(n_in, n_out, *refs)
+
+    return pl.pallas_call(
+        kernel,
+        name="first_axis",
+        out_shape=[f32(NG // n_out, LANES)] * n_out,
+        in_specs=[SMEM, VMEM, VMEM] + [VMEM] * n_in,
+        out_specs=[VMEM] * n_out,
+        scratch_shapes=[pltpu.VMEM((NG, LANES), jnp.float32)] * 2,
+        compiler_params=params(32),
+        cost_estimate=cost(5e9, 2 * 4 * NG * LANES),
+    )(place, *tables, *ins)
+
+
+def call_second_axis(place, tables, ins, n_rows, n_cols):
+    def kernel(*refs):
+        second_axis_kernel(n_rows, n_cols, *refs)
+
+    return pl.pallas_call(
+        kernel,
+        name="second_axis",
+        out_shape=[f32(LANES, NG // n_cols)] * n_cols,
+        in_specs=[SMEM, VMEM, VMEM, VMEM, VMEM],
+        out_specs=[VMEM] * n_cols,
+        scratch_shapes=[pltpu.VMEM((NG, LANES), jnp.float32)] * 3,
+        compiler_params=params(40),
+        cost_estimate=cost(8e9, 3 * 4 * NG * LANES),
+    )(place, *tables, *ins)
+
+
+def call_second_axis_back(place, tables, ins, n_rows, n_cols):
+    def kernel(*refs):
+        second_axis_back_kernel(n_rows, n_cols, *refs)
+
+    return pl.pallas_call(
+        kernel,
+        name="second_axis_back",
+        out_shape=[f32(n_rows * n_cols, LANES, LANES)] * 2,
+        in_specs=[SMEM, VMEM, VMEM] + [VMEM] * n_cols,
+        out_specs=[VMEM] * 2,
+        scratch_shapes=[pltpu.VMEM((NG, LANES), jnp.float32)] * 4,
+        compiler_params=params(40),
+        cost_estimate=cost(8e9, 3 * 4 * NG * LANES),
+    )(place, *tables, *ins)
+
+
+def call_cell(place, coefficients, latent, covariates, counts, mask, k):
+    n_cov = covariates.shape[0]
+    height, width = latent.shape
+    tile = 32
+    tiles = height // tile
+
+    def kernel(*refs):
+        cell_kernel(n_cov, *refs)
+
+    def part(i, place, coefficients):
+        return (jnp.bitwise_xor(place[3], k) * tiles + i, 0)
+
+    return pl.pallas_call(
+        kernel,
+        name="cell",
+        out_shape=[f32(height, width), f32(n_cov + 1, 8, LANES)],
+        grid_spec=pltpu.PrefetchScalarGridSpec(
+            num_scalar_prefetch=2,
+            grid=(tiles,),
+            in_specs=[
+                pl.BlockSpec((tile, width), lambda i, p, c: (i, 0)),
+                pl.BlockSpec((n_cov, tile, width), lambda i, p, c: (0, *part(i, p, c))),
+                pl.BlockSpec((tile, width), part),
+                pl.BlockSpec((tile, width), part),
+            ],
+            out_specs=[
+                pl.BlockSpec((tile, width), lambda i, p, c: (i, 0)),
+                pl.BlockSpec((n_cov + 1, 8, LANES), lambda i, p, c: (0, 0, 0)),
+            ],
+        ),
+        compiler_params=params(32),
+        cost_estimate=cost(4e9, height * width * (2 * n_cov + 16)),
+    )(place, coefficients, latent, covariates, counts, mask)
+
+
+def call_final(place, hyper, real, imag, blocks, n_rows):
+    height, width = real.shape
+    tile = 128
+
+    def kernel(*refs):
+        final_kernel(n_rows, *refs)
+
+    wide = pl.BlockSpec((tile, width), lambda i: (i, 0))
+    narrow = pl.BlockSpec((tile, LANES), lambda i: (i, 0))
+    return pl.pallas_call(
+        kernel,
+        name="final",
+        out_shape=[f32(height, width)] * 2,
+        grid=(height // tile,),
+        in_specs=[SMEM, SMEM, wide, wide] + [narrow] * (2 * n_rows),
+        out_specs=[wide, wide],
+        compiler_params=params(32),
+        cost_estimate=cost(4e9, 6 * 4 * real.size),
+    )(place, hyper, real, imag, *blocks)
+
+
+def exchange(blocks, axis):
+    count = len(blocks)
+    received = [blocks[0]] + [None] * (count - 1)
+    for k in range(count - 1, 0, -1):
+        received[k] = lax.ppermute(blocks[k], axis, [(i, i ^ k) for i in range(count)])
+    return received
+
+
+def sum_over(values, mesh_axes):
+    for axis, count in mesh_axes:
+        k = 1
+        while k < count:
+            values = values + lax.ppermute(values, axis, [(i, i ^ k) for i in range(count)])
+            k *= 2
+    return values
+
+
+def tiled_shards(n_rows, n_cols):
+    def run(white_real, white_imag, covariates, coefficients, counts, land_mask, field_hyper):
+        height, width = white_real.shape
+        n_cov = covariates.shape[0]
+        my_row, my_col = lax.axis_index("rows"), lax.axis_index("cols")
+        place = jnp.stack([my_row, my_row * height, my_col * width, my_col]).astype(jnp.int32)
+        spots = jnp.stack([my_row, my_col]).astype(jnp.int32)
+        tables = (jnp.asarray(dense_table()), jnp.asarray(twiddle_table()))
+
+        *packed, squares = call_scale(place, field_hyper, white_real, white_imag, n_rows)
+        lines = []
+        for j in range(2):
+            columns = exchange(packed[j], "rows")
+            (spread,) = call_first_axis(spots, tables, columns, 1)
+            spread = spread.reshape(n_rows * n_cols, LANES, LANES)
+            lines.append(lax.all_to_all(spread, ("rows", "cols"), 0, 0))
+        latent = exchange(call_second_axis(spots, tables, lines, n_rows, n_cols), "cols")
+
+        residuals, sums = [], 0.0
+        for k in range(n_cols):
+            residual, part = call_cell(place, coefficients, latent[k], covariates, counts, land_mask, k)
+            residuals.append(residual)
+            sums = sums + part
+        back = exchange(residuals, "cols")
+        spread = call_second_axis_back(spots, tables, back, n_rows, n_cols)
+        blocks = []
+        for j in range(2):
+            lines = lax.all_to_all(spread[j], ("rows", "cols"), 0, 0).reshape(NG, LANES)
+            blocks += exchange(call_first_axis(spots, tables, [lines], n_rows), "rows")
+
+        sums = jnp.sum(sums, axis=(1, 2))
+        own_loss = sums[n_cov] + 0.5 * jnp.sum(squares)
+        own = jnp.concatenate([sums[:n_cov], jnp.broadcast_to(own_loss, (LANES - n_cov,))])
+        totals = sum_over(own, (("rows", n_rows), ("cols", n_cols)))
+        per_cell = 1.0 / (NG * NG)
+        coef_grad = (
+            totals[:n_cov] * per_cell + lasso_weight * jnp.sign(coefficients) + ridge_weight * coefficients
+        )
+        objective = (
+            totals[n_cov] * per_cell
+            + lasso_weight * jnp.sum(jnp.abs(coefficients))
+            + 0.5 * ridge_weight * jnp.sum(coefficients * coefficients)
+        )
+        step_real, step_imag = call_final(place, field_hyper, white_real, white_imag, blocks, n_rows)
+        return (step_real, step_imag, coef_grad, objective)
+
+    return run
 
 
 def field_spectrum(field_hyper, wave_row, wave_col):
@@ -120,8 +671,10 @@
 
 
 def solution(mesh):
+    n_rows, n_cols = mesh.shape["rows"], mesh.shape["cols"]
+    tiled = n_rows * n_cols * LANES == NG and not n_rows & (n_rows - 1) and not n_cols & (n_cols - 1)
     return jax.shard_map(
-        shards,
+        tiled_shards(n_rows, n_cols) if tiled else shards,
         mesh=mesh,
         in_specs=(
             P("rows", "cols"),

time: 906 us -> 493 us (0.54)
  blocking collectives: 384 us -> 109 us
  matrix products: 197 us -> 0 us
  Pallas kernels: 0 us -> 106 us
  local copies, waits for them, and re-layouts: 102 us -> 38.5 us
  other arithmetic: 51 us -> 2.14 us
  starting transfers between devices: 15.6 us -> 54 us
  waiting for transfers between devices: 139 us -> 176 us
    all_to_all x5 -> x2, blocking collectives: 346 us -> 109 us  [the longest x1 58.7 us: run(): lines = lax.all_to_all(spread[j], ('rows', 'cols'), 0, 0).reshape(NG, LANES)]
    dot_general x29 -> x0, matrix products: 197 us -> none  [the longest x14 130 us: apply_big(): return jnp.einsum('rnm,nk->rmk', block, table, precision=highest)]
    ppermute x0 -> x39, waiting for transfers between devices: none -> 176 us  [the longest x34 148 us: exchange(): lax.ppermute(blocks[k], axis, [(i, i ^ k) for i in range(count)])]
    all_to_all x3 -> x2, waiting for transfers between devices: 139 us -> 0.01 us  [the longest x1 0.01 us: run(): lines.append(lax.all_to_all(spread, ('rows', 'cols'), 0, 0))]
    pallas_call x0 -> x12, Pallas kernels: none -> 106 us  [the longest x4 47.2 us: call_first_axis(): pl.pallas_call(kernel, name='first_axis', out_shape=[f32(NG // n_out, LAN...]
    ppermute x0 -> x39, starting transfers between devices: none -> 43.1 us  [the longest x34 34.7 us: exchange(): lax.ppermute(blocks[k], axis, [(i, i ^ k) for i in range(count)])]
    psum x1 -> x0, blocking collectives: 38 us -> none  [shards(): lax.psum((partial_coef, partial_loss), ('rows', 'cols'))]
    unnamed x39 -> x78, local copies, waits for them, and re-layouts: 0.72 us -> 37.3 us
  transfers between devices with their start and end apart: 3 -> 41, of which waited for: 3 -> 17; matrix products, arithmetic and copies ran while one was open for 3% -> 1% of each run, Pallas kernels for 0% -> 10%
where the time goes in v1:
time: 493 us; the launch traced here: 491 us
  waiting for transfers between devices  176 us (36%)
  blocking collectives  109 us (22%)
  Pallas kernels  106 us (22%)
  starting transfers between devices  54 us (11%)
  local copies, waits for them, and re-layouts  38.5 us (8%)
  between operations  5.32 us (1%)
    ppermute x34, waiting for transfers between devices, exchange(): lax.ppermute(blocks[k], axis, [(i, i ^ k) for i in range(count)])  148 us
    all_to_all x1, blocking collectives, run(): lines = lax.all_to_all(spread[j], ('rows', 'cols'), 0, 0).reshape(NG, LANES)  58.7 us
    all_to_all x1, blocking collectives, run(): lines.append(lax.all_to_all(spread, ('rows', 'cols'), 0, 0))  50.8 us
    pallas_call x4, Pallas kernels, call_first_axis(): pl.pallas_call(kernel, name='first_axis', out_shape=[f32(NG // n_out, LAN...  47.2 us
    unnamed x78, local copies, waits for them, and re-layouts  37.3 us
    ppermute x34, starting transfers between devices, exchange(): lax.ppermute(blocks[k], axis, [(i, i ^ k) for i in range(count)])  34.7 us
    ppermute x5, waiting for transfers between devices, sum_over(): lax.ppermute(values, axis, [(i, i ^ k) for i in range(count)])  28.4 us
    pallas_call x1, Pallas kernels, call_second_axis_back(): pl.pallas_call(kernel, name='second_axis_back', out_shape=[f32(n_rows * n...  16.6 us
  transfers between devices with their start and end apart: 41, of which 17 were waited for; matrix products, arithmetic and copies ran while one was open for 1% of the time, Pallas kernels for 10%

profile of v1, /device:TPU:0, one launch (start us, length us, event | category | flops | bytes accessed | tf_op | source)
XLA Modules:
  0.0 491.5 jit_solution(14872532647388062162)
XLA Ops:
  4.6 10.5 %scale.1 = (f32[512,128]{1,0:T(8,128)S(1)}, f32[512,128]{1,0:T(8,128)S(1)}, f32[512,128]{1,0:T(8,128)S(1)}, f32[512,128]{1,0:T(8,128)S(1)}, f32[512,128]{1,0:T(8...) custom-call(s32[4]{0:T(128)S(1)} %pad_add_fusion.refs_0_, ...), custom_call_target="tpu_custom_call" | custom-call | flops 4000000000 | bytes 8388608 | tf_op jit(solution)/shard_map/scale/pallas_call | solution.py:382
  31.1 12.3 %collective-permute-done.4.refs_8_ = f32[512,128]{1,0:T(8,128)S(1)} collective-permute-done((f32[512,128]{1,0:T(8,128)S(1)}, f32[512,128]{1,0:T(8,128)S(1)}, u32[]{:S(2)}, u32[]{:S(2)}) %collective-permute-start.4) | collective-permute-done | bytes 262176 | tf_op jit(solution)/shard_map/ppermute | solution.py:504
  43.5 11.3 %first_axis.4 = f32[4096,128]{1,0:T(8,128)S(1)} custom-call(s32[2]{0:T(128)S(1)} %pad_add_fusion.1.refs_0_, bf16[512,1536]{1,0:T(8,128)(2,1)S(1)} %copy-done.23, f32[256,128]{1,0:T(8,128)S(1)} %copy-done.29, f32[512,128]{1,0:T(8,128)S(1)} %get-tuple-element.53.refs_3_, f32[512,128]{1,0:T(8,128)S(1)} %collective-permute-done.refs_4_, ...), custom_call_target="tpu_custom_call" | custom-call | flops 5000000000 | bytes 4194304 | tf_op jit(solution)/shard_map/first_axis/pallas_call | solution.py:400
  56.2 6.2 %all-to-all-start = ((f32[32,128,128]{2,1,0:T(8,128)}), f32[32,128,128]{2,1,0:T(8,128)S(1)}, u32[]{:S(2)}, u32[]{:S(2)}) async-start(f32[32,128,128]{2,1,0:T(8,128)} %bitcast.13), calls=%async_computation | async-start | bytes 4194304 | tf_op jit(solution)/shard_map/all_to_all | solution.py:532
  68.8 18.1 %collective-permute-done.8.refs_5_ = f32[512,128]{1,0:T(8,128)S(1)} collective-permute-done((f32[512,128]{1,0:T(8,128)}, f32[512,128]{1,0:T(8,128)S(1)}, u32[]{:S(2)}, u32[]{:S(2)}) %collective-permute-start.8) | collective-permute-done | bytes 262176 | tf_op jit(solution)/shard_map/ppermute | solution.py:504
  86.9 7.4 %collective-permute-done.9.refs_6_ = f32[512,128]{1,0:T(8,128)S(1)} collective-permute-done((f32[512,128]{1,0:T(8,128)S(1)}, f32[512,128]{1,0:T(8,128)S(1)}, u32[]{:S(2)}, u32[]{:S(2)}) %collective-permute-start.9) | collective-permute-done | bytes 262176 | tf_op jit(solution)/shard_map/ppermute | solution.py:504
  94.3 11.0 %collective-permute-done.12.refs_9_ = f32[512,128]{1,0:T(8,128)S(1)} collective-permute-done((f32[512,128]{1,0:T(8,128)S(1)}, f32[512,128]{1,0:T(8,128)S(1)}, u32[]{:S(2)}, u32[]{:S(2)}) %collective-permute-start.12) | collective-permute-done | bytes 262176 | tf_op jit(solution)/shard_map/ppermute | solution.py:504
  105.3 7.2 %collective-permute-done.13.refs_10_ = f32[512,128]{1,0:T(8,128)S(1)} collective-permute-done((f32[512,128]{1,0:T(8,128)S(1)}, f32[512,128]{1,0:T(8,128)S(1)}, u32[]{:S(2)}, u32[]{:S(2)}) %collective-permute-start.13) | collective-permute-done | bytes 262176 | tf_op jit(solution)/shard_map/ppermute | solution.py:504
  115.8 11.3 %first_axis.5 = f32[4096,128]{1,0:T(8,128)S(1)} custom-call(s32[2]{0:T(128)S(1)} %pad_add_fusion.1.refs_0_, bf16[512,1536]{1,0:T(8,128)(2,1)S(1)} %copy-done.24, f32[256,128]{1,0:T(8,128)S(1)} %copy-done.30, f32[512,128]{1,0:T(8,128)S(1)} %copy-done.38, f32[512,128]{1,0:T(8,128)S(1)} %collective-permute-done.7.refs_4_, ...), custom_call_target="tpu_custom_call" | custom-call | flops 5000000000 | bytes 4194304 | tf_op jit(solution)/shard_map/first_axis/pallas_call | solution.py:400
  128.5 50.8 %all_to_all.20.refs_4_ = f32[32,128,128]{2,1,0:T(8,128)S(1)} all-to-all(f32[32,128,128]{2,1,0:T(8,128)} %bitcast.14), channel_id=1, replica_groups=mesh['rows'=8,'cols'=4] {'rows','cols'}, dimensions={0} | all-to-all | bytes 4194304 | tf_op jit(solution)/shard_map/all_to_all | solution.py:532
  179.3 11.4 %second_axis.1 = (f32[128,1024]{1,0:T(8,128)S(1)}, f32[128,1024]{1,0:T(8,128)S(1)}, f32[128,1024]{1,0:T(8,128)S(1)}, f32[128,1024]{1,0:T(8,128)S(1)}) custom-call(s32[2]{0:T(128)S(1)} %pad_add_fusion.1.refs_0_, bf16[512,1536]{1,0:T(8,128)(2,1)S(1)} %copy-done.25, f32[256,128]{1,0:T(8,128)S(1)} %copy-done.30, f32[32,128,128]{2,1,0:T(8,128)S(1)} %all-to-all-done.refs_3_, ...), custom_call_target="tpu_custom_call" | custom-call | flops 8000000000 | bytes 6291456 | tf_op jit(solution)/shard_map/second_axis/pallas_call | solution.py:416
  196.3 19.6 %collective-permute-done.14.refs_2_ = f32[128,1024]{1,0:T(8,128)S(1)} collective-permute-done((f32[128,1024]{1,0:T(8,128)S(1)}, f32[128,1024]{1,0:T(8,128)S(1)}, u32[]{:S(2)}, u32[]{:S(2)}) %collective-permute-start.14) | collective-permute-done | bytes 524320 | tf_op jit(solution)/shard_map/ppermute | solution.py:504
  216.0 5.8 %copy-done = bf16[16,512,1024]{2,1,0:T(8,128)(2,1)S(1)} copy-done((bf16[16,512,1024]{2,1,0:T(8,128)(2,1)S(1)}, bf16[16,512,1024]{2,1,0:T(8,128)(2,1)}, u32[]{:S(2)}) %copy-start) | copy-done | bytes 16777240
  225.5 6.6 %collective-permute-done.16.refs_2_ = f32[128,1024]{1,0:T(8,128)S(1)} collective-permute-done((f32[128,1024]{1,0:T(8,128)S(1)}, f32[128,1024]{1,0:T(8,128)S(1)}, u32[]{:S(2)}, u32[]{:S(2)}) %collective-permute-start.16) | collective-permute-done | bytes 524320 | tf_op jit(solution)/shard_map/ppermute | solution.py:504
  240.4 5.8 %copy-done.1 = bf16[16,512,1024]{2,1,0:T(8,128)(2,1)S(1)} copy-done((bf16[16,512,1024]{2,1,0:T(8,128)(2,1)S(1)}, bf16[16,512,1024]{2,1,0:T(8,128)(2,1)}, u32[]{:S(2)}) %copy-start.1) | copy-done | bytes 16777240
  249.9 27.1 %collective-permute-done.17.refs_5_ = f32[128,1024]{1,0:T(8,128)S(1)} collective-permute-done((f32[128,1024]{1,0:T(8,128)S(1)}, f32[128,1024]{1,0:T(8,128)S(1)}, u32[]{:S(2)}, u32[]{:S(2)}) %collective-permute-start.17) | collective-permute-done | bytes 524320 | tf_op jit(solution)/shard_map/ppermute | solution.py:504
  278.5 16.6 %second_axis_back.1 = (f32[32,128,128]{2,1,0:T(8,128)S(1)}, f32[32,128,128]{2,1,0:T(8,128)S(1)}) custom-call(s32[2]{0:T(128)S(1)} %pad_add_fusion.1.refs_0_, bf16[512,1536]{1,0:T(8,128)(2,1)S(1)} %copy-done.26, f32[256,128]{1,0:T(8,128)S(1)} %copy-done.31, f32[128,1024]{1,0:T(8,128)S(1)} %get-tuple-element.70.refs_3_, ...), custom_call_target="tpu_custom_call" | custom-call | flops 8000000000 | bytes 6291456 | tf_op jit(solution)/shard_map/second_axis_back/pallas_call | solution.py:432
  295.0 58.7 %all_to_all.21 = f32[32,128,128]{2,1,0:T(8,128)} all-to-all(f32[32,128,128]{2,1,0:T(8,128)S(1)} %get-tuple-element.86), channel_id=1, replica_groups=mesh['rows'=8,'cols'=4] {'rows','cols'}, dimensions={0} | all-to-all | bytes 4194304 | tf_op jit(solution)/shard_map/all_to_all | solution.py:544
  363.9 8.8 %collective-permute-done.35 = f32[128]{0:T(128)S(1)} collective-permute-done((f32[128]{0:T(128)S(1)}, f32[128]{0:T(128)S(1)}, u32[]{:S(2)}, u32[]{:S(2)}) %collective-permute-start.35) | collective-permute-done | bytes 544 | tf_op jit(solution)/shard_map/ppermute | solution.py:512
  376.6 16.5 %collective-permute-done.37 = f32[128]{0:T(128)S(1)} collective-permute-done((f32[128]{0:T(128)S(1)}, f32[128]{0:T(128)S(1)}, u32[]{:S(2)}, u32[]{:S(2)}) %collective-permute-start.37) | collective-permute-done | bytes 544 | tf_op jit(solution)/shard_map/ppermute | solution.py:512
  400.9 12.3 %first_axis.7 = (f32[512,128]{1,0:T(8,128)S(1)}, f32[512,128]{1,0:T(8,128)}, f32[512,128]{1,0:T(8,128)}, f32[512,128]{1,0:T(8,128)}, f32[512,128]{1,0:T(8,128)},...) custom-call(s32[2]{0:T(128)S(1)} %pad_add_fusion.1.refs_0_, ...), custom_call_target="tpu_custom_call" | custom-call | flops 5000000000 | bytes 4194304 | tf_op jit(solution)/shard_map/first_axis/pallas_call | solution.py:400
  421.7 12.3 %first_axis.6 = (f32[512,128]{1,0:T(8,128)S(1)}, f32[512,128]{1,0:T(8,128)S(1)}, f32[512,128]{1,0:T(8,128)S(1)}, f32[512,128]{1,0:T(8,128)}, f32[512,128]{1,0:T(...) custom-call(s32[2]{0:T(128)S(1)} %pad_add_fusion.1.refs_0_, ...), custom_call_target="tpu_custom_call" | custom-call | flops 5000000000 | bytes 4194304 | tf_op jit(solution)/shard_map/first_axis/pallas_call | solution.py:400
  438.7 15.5 %collective-permute-done.31.refs_17_ = f32[512,128]{1,0:T(8,128)S(1)} collective-permute-done((f32[512,128]{1,0:T(8,128)S(1)}, f32[512,128]{1,0:T(8,128)S(1)}, u32[]{:S(2)}, u32[]{:S(2)}) %collective-permute-start.31) | collective-permute-done | bytes 262176 | tf_op jit(solution)/shard_map/ppermute | solution.py:504
  463.2 12.5 %collective-permute-done.23.refs_8_ = f32[512,128]{1,0:T(8,128)S(1)} collective-permute-done((f32[512,128]{1,0:T(8,128)}, f32[512,128]{1,0:T(8,128)S(1)}, u32[]{:S(2)}, u32[]{:S(2)}) %collective-permute-start.23) | collective-permute-done | bytes 262176 | tf_op jit(solution)/shard_map/ppermute | solution.py:504
  (163 shorter events, 110.6 us)
Async XLA Ops:
  20.6 22.9 %collective-permute-start.4 = (f32[512,128]{1,0:T(8,128)S(1)}, f32[512,128]{1,0:T(8,128)S(1)}, u32[]{:S(2)}, u32[]{:S(2)}) collective-permute-start(f32[512,128]{1,0:T(8,128)S(1)} %get-tuple-element.58), channel_id=1, source_target_pairs={{0,20},{4,16},{8,28},{12,24},{16,4},{20,0},{24,12},{28,8},{1,21},{... | collective-permute-start | bytes 786440 | tf_op jit(solution)/shard_map/ppermute | solution.py:504
  20.6 22.9 %collective-permute-start.5 = (f32[512,128]{1,0:T(8,128)S(1)}, f32[512,128]{1,0:T(8,128)S(1)}, u32[]{:S(2)}, u32[]{:S(2)}) collective-permute-start(f32[512,128]{1,0:T(8,128)S(1)} %get-tuple-element.59), channel_id=1, source_target_pairs={{0,24},{4,28},{8,16},{12,20},{16,8},{20,12},{24,0},{28,4},{1,25},{... | collective-permute-start | bytes 786440 | tf_op jit(solution)/shard_map/ppermute | solution.py:504
  56.2 72.3 %all-to-all-start = ((f32[32,128,128]{2,1,0:T(8,128)}), f32[32,128,128]{2,1,0:T(8,128)S(1)}, u32[]{:S(2)}, u32[]{:S(2)}) async-start(f32[32,128,128]{2,1,0:T(8,128)} %bitcast.13), calls=%async_computation | async-start | bytes 4194304 | tf_op jit(solution)/shard_map/all_to_all | solution.py:532
  62.8 24.2 %collective-permute-start.8 = (f32[512,128]{1,0:T(8,128)}, f32[512,128]{1,0:T(8,128)S(1)}, u32[]{:S(2)}, u32[]{:S(2)}) collective-permute-start(f32[512,128]{1,0:T(8,128)} %copy-done.13), channel_id=1, source_target_pairs={{0,8},{4,12},{8,0},{12,4},{16,24},{20,28},{24,16},{28,20},{1,9},{5... | collective-permute-start | bytes 786440 | tf_op jit(solution)/shard_map/ppermute | solution.py:504
  64.4 29.9 %collective-permute-start.9 = (f32[512,128]{1,0:T(8,128)S(1)}, f32[512,128]{1,0:T(8,128)S(1)}, u32[]{:S(2)}, u32[]{:S(2)}) collective-permute-start(f32[512,128]{1,0:T(8,128)S(1)} %get-tuple-element.64), channel_id=1, source_target_pairs={{0,12},{4,8},{8,4},{12,0},{16,28},{20,24},{24,20},{28,16},{1,13},{... | collective-permute-start | bytes 786440 | tf_op jit(solution)/shard_map/ppermute | solution.py:504
  64.4 29.9 %collective-permute-start.10 = (f32[512,128]{1,0:T(8,128)S(1)}, f32[512,128]{1,0:T(8,128)S(1)}, u32[]{:S(2)}, u32[]{:S(2)}) collective-permute-start(f32[512,128]{1,0:T(8,128)S(1)} %get-tuple-element.65), channel_id=1, source_target_pairs={{0,16},{4,20},{8,24},{12,28},{16,0},{20,4},{24,8},{28,12},{1,17},{... | collective-permute-start | bytes 786440 | tf_op jit(solution)/shard_map/ppermute | solution.py:504
  66.1 28.2 %collective-permute-start.11 = (f32[512,128]{1,0:T(8,128)S(1)}, f32[512,128]{1,0:T(8,128)S(1)}, u32[]{:S(2)}, u32[]{:S(2)}) collective-permute-start(f32[512,128]{1,0:T(8,128)S(1)} %get-tuple-element.66), channel_id=1, source_target_pairs={{0,20},{4,16},{8,28},{12,24},{16,4},{20,0},{24,12},{28,8},{1,21},{... | collective-permute-start | bytes 786440 | tf_op jit(solution)/shard_map/ppermute | solution.py:504
  66.3 39.1 %collective-permute-start.12 = (f32[512,128]{1,0:T(8,128)S(1)}, f32[512,128]{1,0:T(8,128)S(1)}, u32[]{:S(2)}, u32[]{:S(2)}) collective-permute-start(f32[512,128]{1,0:T(8,128)S(1)} %get-tuple-element.67), channel_id=1, source_target_pairs={{0,24},{4,28},{8,16},{12,20},{16,8},{20,12},{24,0},{28,4},{1,25},{... | collective-permute-start | bytes 786440 | tf_op jit(solution)/shard_map/ppermute | solution.py:504
  86.9 25.6 %collective-permute-start.13 = (f32[512,128]{1,0:T(8,128)S(1)}, f32[512,128]{1,0:T(8,128)S(1)}, u32[]{:S(2)}, u32[]{:S(2)}) collective-permute-start(f32[512,128]{1,0:T(8,128)S(1)} %get-tuple-element.68), channel_id=1, source_target_pairs={{0,28},{4,24},{8,20},{12,16},{16,12},{20,8},{24,4},{28,0},{1,29},{... | collective-permute-start | bytes 786440 | tf_op jit(solution)/shard_map/ppermute | solution.py:504
  190.7 25.2 %collective-permute-start.14 = (f32[128,1024]{1,0:T(8,128)S(1)}, f32[128,1024]{1,0:T(8,128)S(1)}, u32[]{:S(2)}, u32[]{:S(2)}) collective-permute-start(f32[128,1024]{1,0:T(8,128)S(1)} %get-tuple-element.71), channel_id=1, source_target_pairs={{0,1},{1,0},{2,3},{3,2},{4,5},{5,4},{6,7},{7,6},{8,9},{9,8},{10,11... | collective-permute-start | bytes 1572872 | tf_op jit(solution)/shard_map/ppermute | solution.py:504
  193.9 38.2 %collective-permute-start.16 = (f32[128,1024]{1,0:T(8,128)S(1)}, f32[128,1024]{1,0:T(8,128)S(1)}, u32[]{:S(2)}, u32[]{:S(2)}) collective-permute-start(f32[128,1024]{1,0:T(8,128)S(1)} %get-tuple-element.73), channel_id=1, source_target_pairs={{0,2},{1,3},{2,0},{3,1},{4,6},{5,7},{6,4},{7,5},{8,10},{9,11},{10,... | collective-permute-start | bytes 1572872 | tf_op jit(solution)/shard_map/ppermute | solution.py:504
  194.5 41.4 %collective-permute-start.18 = (f32[128,1024]{1,0:T(8,128)S(1)}, f32[128,1024]{1,0:T(8,128)S(1)}, u32[]{:S(2)}, u32[]{:S(2)}) collective-permute-start(f32[128,1024]{1,0:T(8,128)S(1)} %get-tuple-element.75), channel_id=1, source_target_pairs={{0,3},{1,2},{2,1},{3,0},{4,7},{5,6},{6,5},{7,4},{8,11},{9,10},{10,... | collective-permute-start | bytes 1572872 | tf_op jit(solution)/shard_map/ppermute | solution.py:504
  225.5 24.4 %collective-permute-start.15 = (f32[128,1024]{1,0:T(8,128)S(1)}, f32[128,1024]{1,0:T(8,128)S(1)}, u32[]{:S(2)}, u32[]{:S(2)}) collective-permute-start(f32[128,1024]{1,0:T(8,128)S(1)} %get-tuple-element.72), channel_id=1, source_target_pairs={{0,1},{1,0},{2,3},{3,2},{4,5},{5,4},{6,7},{7,6},{8,9},{9,8},{10,11... | collective-permute-start | bytes 1572872 | tf_op jit(solution)/shard_map/ppermute | solution.py:504
  235.8 41.2 %collective-permute-start.17 = (f32[128,1024]{1,0:T(8,128)S(1)}, f32[128,1024]{1,0:T(8,128)S(1)}, u32[]{:S(2)}, u32[]{:S(2)}) collective-permute-start(f32[128,1024]{1,0:T(8,128)S(1)} %get-tuple-element.74), channel_id=1, source_target_pairs={{0,2},{1,3},{2,0},{3,1},{4,6},{5,7},{6,4},{7,5},{8,10},{9,11},{10,... | collective-permute-start | bytes 1572872 | tf_op jit(solution)/shard_map/ppermute | solution.py:504
  239.7 37.4 %collective-permute-start.19 = (f32[128,1024]{1,0:T(8,128)S(1)}, f32[128,1024]{1,0:T(8,128)S(1)}, u32[]{:S(2)}, u32[]{:S(2)}) collective-permute-start(f32[128,1024]{1,0:T(8,128)S(1)} %get-tuple-element.76), channel_id=1, source_target_pairs={{0,3},{1,2},{2,1},{3,0},{4,7},{5,6},{6,5},{7,4},{8,11},{9,10},{10,... | collective-permute-start | bytes 1572872 | tf_op jit(solution)/shard_map/ppermute | solution.py:504
  353.7 65.6 %all-to-all-start.2 = ((f32[32,128,128]{2,1,0:T(8,128)}), f32[32,128,128]{2,1,0:T(8,128)S(1)}, u32[]{:S(2)}, u32[]{:S(2)}) async-start(f32[32,128,128]{2,1,0:T(8,128)} %copy-done.4), calls=%async_computation.2 | async-start | bytes 4194304 | tf_op jit(solution)/shard_map/all_to_all | solution.py:544
  393.0 41.6 %collective-permute-start.38 = (f32[128]{0:T(128)S(1)}, f32[128]{0:T(128)S(1)}, u32[]{:S(2)}, u32[]{:S(2)}) collective-permute-start(f32[128]{0:T(128)S(1)} %add.48), channel_id=1, source_target_pairs={{0,2},{1,3},{2,0},{3,1},{4,6},{5,7},{6,4},{7,5},{8,10},{9,11},{10,... | collective-permute-start | bytes 1544 | tf_op jit(solution)/shard_map/ppermute | solution.py:512
  416.0 20.6 %collective-permute-start.28 = (f32[512,128]{1,0:T(8,128)}, f32[512,128]{1,0:T(8,128)S(1)}, u32[]{:S(2)}, u32[]{:S(2)}) collective-permute-start(f32[512,128]{1,0:T(8,128)} %get-tuple-element.89), channel_id=1, source_target_pairs={{0,8},{4,12},{8,0},{12,4},{16,24},{20,28},{24,16},{28,20},{1,9},{5... | collective-permute-start | bytes 786440 | tf_op jit(solution)/shard_map/ppermute | solution.py:504
  416.9 20.7 %collective-permute-start.29 = (f32[512,128]{1,0:T(8,128)}, f32[512,128]{1,0:T(8,128)S(1)}, u32[]{:S(2)}, u32[]{:S(2)}) collective-permute-start(f32[512,128]{1,0:T(8,128)} %get-tuple-element.90), channel_id=1, source_target_pairs={{0,12},{4,8},{8,4},{12,0},{16,28},{20,24},{24,20},{28,16},{1,13},{... | collective-permute-start | bytes 786440 | tf_op jit(solution)/shard_map/ppermute | solution.py:504
  434.8 20.3 %collective-permute-start.32 = (f32[512,128]{1,0:T(8,128)S(1)}, f32[512,128]{1,0:T(8,128)S(1)}, u32[]{:S(2)}, u32[]{:S(2)}) collective-permute-start(f32[512,128]{1,0:T(8,128)S(1)} %copy-done.18), channel_id=1, source_target_pairs={{0,24},{4,28},{8,16},{12,20},{16,8},{20,12},{24,0},{28,4},{1,25},{... | collective-permute-start | bytes 786440 | tf_op jit(solution)/shard_map/ppermute | solution.py:504
  455.1 20.6 %collective-permute-start.23 = (f32[512,128]{1,0:T(8,128)}, f32[512,128]{1,0:T(8,128)S(1)}, u32[]{:S(2)}, u32[]{:S(2)}) collective-permute-start(f32[512,128]{1,0:T(8,128)} %get-tuple-element.82), channel_id=1, source_target_pairs={{0,16},{4,20},{8,24},{12,28},{16,0},{20,4},{24,8},{28,12},{1,17},{... | collective-permute-start | bytes 786440 | tf_op jit(solution)/shard_map/ppermute | solution.py:504
  455.6 24.2 %collective-permute-start.24 = (f32[512,128]{1,0:T(8,128)}, f32[512,128]{1,0:T(8,128)S(1)}, u32[]{:S(2)}, u32[]{:S(2)}) collective-permute-start(f32[512,128]{1,0:T(8,128)} %get-tuple-element.83), channel_id=1, source_target_pairs={{0,20},{4,16},{8,28},{12,24},{16,4},{20,0},{24,12},{28,8},{1,21},{... | collective-permute-start | bytes 786440 | tf_op jit(solution)/shard_map/ppermute | solution.py:504
  456.7 23.2 %collective-permute-start.25 = (f32[512,128]{1,0:T(8,128)}, f32[512,128]{1,0:T(8,128)}, u32[]{:S(2)}, u32[]{:S(2)}) collective-permute-start(f32[512,128]{1,0:T(8,128)} %get-tuple-element.84), channel_id=1, source_target_pairs={{0,24},{4,28},{8,16},{12,20},{16,8},{20,12},{24,0},{28,4},{1,25},{... | collective-permute-start | bytes 786440 | tf_op jit(solution)/shard_map/ppermute | solution.py:504
  457.8 22.1 %collective-permute-start.26 = (f32[512,128]{1,0:T(8,128)S(1)}, f32[512,128]{1,0:T(8,128)}, u32[]{:S(2)}, u32[]{:S(2)}) collective-permute-start(f32[512,128]{1,0:T(8,128)S(1)} %get-tuple-element.85), channel_id=1, source_target_pairs={{0,28},{4,24},{8,20},{12,16},{16,12},{20,8},{24,4},{28,0},{1,29},{... | collective-permute-start | bytes 786440 | tf_op jit(solution)/shard_map/ppermute | solution.py:504
  (56 other events, 760.9 us)

commit v2 on v1

v2 whole, which is shorter than its diff:
```python
import math

import jax
import jax.numpy as jnp
import ml_dtypes
import numpy as np
from jax import lax
from jax.experimental import pallas as pl
from jax.experimental.pallas import tpu as pltpu
from jax.sharding import PartitionSpec as P

NG = 4096
LANES = 128
HALF = LANES // 2
RADIX = 16
DENSE = NG // RADIX

lasso_weight = 0.02
ridge_weight = 0.1


def split3(values):
    first = values.astype(ml_dtypes.bfloat16)
    rest = values - first.astype(np.float64)
    second = rest.astype(ml_dtypes.bfloat16)
    rest = rest - second.astype(np.float64)
    return first, second, rest.astype(ml_dtypes.bfloat16)


def dense_table():
    index = np.arange(DENSE)
    angles = (index[:, None] * index[None, :] % DENSE) * (2.0 * np.pi / DENSE)
    quarters = index.reshape(4, DENSE // 4)
    columns = [np.concatenate([quarters[j], quarters[j + 2]]) for j in range(2)]
    full = np.concatenate([part[:, at] for at in columns for part in (np.cos(angles), -np.sin(angles))], axis=1)
    return np.concatenate(split3(full), axis=1)


def twiddle_table():
    angles = np.arange(DENSE)[None, :] * np.array([1.0, 4.0])[:, None] * (2.0 * np.pi / NG)
    return np.stack([np.cos(angles[0]), np.sin(angles[0]), np.cos(angles[1]), np.sin(angles[1])]).astype(np.float32)


class Pairs:
    def add(self, a, b):
        return tuple(y if x is None else x if y is None else x + y for x, y in zip(a, b))

    def sub(self, a, b):
        return tuple((None if y is None else -y) if x is None else x if y is None else x - y for x, y in zip(a, b))

    def turn(self, a):
        return (None if a[1] is None else -a[1], a[0])

    def mul(self, a, c, s):
        re, im = a
        if im is None:
            return (re * c, re * s)
        if re is None:
            return (-(im * s), im * c)
        return (re * c - im * s, re * s + im * c)


def dft4(ops, z):
    even, odd = ops.add(z[0], z[2]), ops.sub(z[0], z[2])
    even2, turned = ops.add(z[1], z[3]), ops.turn(ops.sub(z[1], z[3]))
    return [ops.add(even, even2), ops.add(odd, turned), ops.sub(even, even2), ops.sub(odd, turned)]


def dft16(ops, z):
    columns = []
    for q in range(4):
        column = dft4(ops, [z[4 * p + q] for p in range(4)])
        for u in range(1, 4):
            turns = q * u
            if turns == 4:
                column[u] = ops.turn(column[u])
            elif turns:
                angle = 2.0 * math.pi * turns / RADIX
                column[u] = ops.mul(column[u], math.cos(angle), math.sin(angle))
        columns.append(column)
    out = [None] * RADIX
    for u in range(4):
        for v, value in enumerate(dft4(ops, [columns[q][u] for q in range(4)])):
            out[u + 4 * v] = value
    return out


def bf16_parts(values):
    one = values.astype(jnp.bfloat16)
    rest = values - one.astype(jnp.float32)
    two = rest.astype(jnp.bfloat16)
    return [one, two, (rest - two.astype(jnp.float32)).astype(jnp.bfloat16)]


def dense_product(table, first, parts):
    one, two, three = parts
    depth = one.shape[0]

    def dot(part, right):
        start = 2 * DENSE * part + first
        return jnp.dot(table[:, start : start + depth], right, preferred_element_type=jnp.float32)

    small = (dot(2, one) + dot(0, three)) + dot(1, two)
    return (small + (dot(1, one) + dot(0, two))) + dot(0, one)


def powers(twiddle_ref, row, step):
    ops = Pairs()
    w = [None] * RADIX
    at = pl.ds(row, step)
    w[1] = (twiddle_ref[0, at, :], twiddle_ref[1, at, :])
    w[4] = (twiddle_ref[2, at, :], twiddle_ref[3, at, :])
    w[2] = ops.mul(w[1], *w[1])
    w[3] = ops.mul(w[2], *w[1])
    for x in (5, 6, 7):
        w[x] = ops.mul(w[4], *w[x - 4])
    w[8] = ops.mul(w[4], *w[4])
    for x in range(9, RADIX):
        w[x] = ops.mul(w[8], *w[x - 8])
    return w


def butterflies(load, re_ref, im_ref, twiddle_ref, halves=(0, 1)):
    ops = Pairs()
    step = 8
    quarter = DENSE // 4
    for at, j in enumerate(halves):

        def body(i, carry, at=at, j=j):
            slow = i // (quarter // step)
            inner = pl.multiple_of((i % (quarter // step)) * step, step)
            z = dft16(ops, [load(a, 2 * slow + j, inner) for a in range(RADIX)])
            w = powers(twiddle_ref, pl.multiple_of((2 * slow + j) * quarter + inner, step), step)
            for x in range(RADIX):
                re, im = ops.mul(z[x], *w[x]) if x else z[x]
                rows = pl.ds(pl.multiple_of((x * len(halves) + at) * 2 * quarter + i * step, step), step)
                re_ref[rows, :] = re
                im_ref[rows, :] = jnp.zeros((step, LANES), jnp.float32) if im is None else im
            return carry

        lax.fori_loop(0, 2 * quarter // step, body, 0, unroll=4)


def stacked(re_ref, im_ref, x, n_halves):
    half = DENSE // 2
    out = []
    for h in range(n_halves):
        rows = pl.ds(pl.multiple_of((x * n_halves + h) * half, half), half)
        out += [re_ref[rows, :], im_ref[rows, :]]
    return out


def real_products(re_ref, im_ref, table_ref, target, halves=(0, 1)):
    def body(p, carry):
        pair = [jnp.concatenate(stacked(re_ref, im_ref, 2 * p + h, len(halves)), axis=0) for h in range(2)]
        both = dense_product(table_ref, halves[0] * DENSE, bf16_parts(jnp.concatenate(pair, axis=1)))
        for h in range(2):
            target[pl.ds(2 * p + h, DENSE, stride=RADIX), :] = both[:, h * LANES : (h + 1) * LANES]
        return carry

    lax.fori_loop(0, RADIX // 2, body, 0, unroll=4)


def spectrum_of(hyper, first_row, first_col, shape, cols=None):
    rows = lax.broadcasted_iota(jnp.int32, shape, 0) + first_row
    cols = (lax.broadcasted_iota(jnp.int32, shape, 1) if cols is None else cols) + first_col
    wave_row = jnp.minimum(rows, NG - rows).astype(jnp.float32)
    wave_col = jnp.minimum(cols, NG - cols).astype(jnp.float32)
    amplitude = 0.2 * hyper[0]
    span = hyper[1]
    base = 1.0 + (wave_row * wave_row + wave_col * wave_col) * (1.0 / (span * span))
    return amplitude * (1.0 + (NG / span) / jnp.sqrt(base * jnp.sqrt(base)))


def scale_kernel(count, j, place, hyper, real_ref, imag_ref, *outs):
    height = real_ref.shape[0]
    me, first_col = place[0], place[2]
    first_row = place[1] + pl.program_id(0) * height
    lane = lax.broadcasted_iota(jnp.int32, (1, LANES), 1)
    low = lane < HALF
    step = 64
    total = jnp.zeros((8, LANES), jnp.float32)
    for k in range(count):
        start = pl.multiple_of(jnp.bitwise_xor(me, k) * LANES, LANES)
        for row in range(0, height, step):
            real = real_ref[pl.ds(row, step), pl.ds(start, LANES)]
            imag = imag_ref[pl.ds(row, step), pl.ds(start, LANES)]
            squares = real * real + imag * imag
            squares = jnp.where(low, squares, 0.0) if j == 0 else jnp.where(low, 0.0, squares)
            total += jnp.sum(squares.reshape(step // 8, 8, LANES), axis=0)
            if j == 0:
                value = jnp.where(low, real, pltpu.roll(imag, HALF, 1))
            else:
                value = jnp.where(low, pltpu.roll(real, HALF, 1), imag)
            cols = jnp.bitwise_and(lax.broadcasted_iota(jnp.int32, (step, LANES), 1), HALF - 1)
            spec = spectrum_of(hyper, first_row + row, first_col + start + j * HALF, (step, LANES), cols)
            outs[k][pl.ds(row, step), :] = spec * value
    outs[-1][...] = total


def first_axis_kernel(n_in, n_out, place, table_ref, twiddle_ref, *refs):
    ins, outs, (one, two, done) = refs[:n_in], refs[n_in : n_in + n_out], refs[n_in + n_out :]
    me = place[0]
    lane = lax.broadcasted_iota(jnp.int32, (8, LANES), 1)
    sign = jnp.where(lane < HALF, 1.0, -1.0).astype(jnp.float32)
    if n_in > 1:
        height = ins[0].shape[0]
        for k in range(n_in):
            start = pl.multiple_of(jnp.bitwise_xor(me, k) * height, height)
            done[pl.ds(start, height), :] = ins[k][...]
        source = done
    else:
        source = ins[0]
    target = done if n_out > 1 else outs[0]

    def load(a, quarter, inner):
        row = pl.multiple_of(a * DENSE + quarter * (DENSE // 4) + inner, 8)
        value = source[pl.ds(row, 8), :]
        return (value, pltpu.roll(value, HALF, 1) * sign)

    butterflies(load, one, two, twiddle_ref)
    real_products(one, two, table_ref, target)
    if n_out > 1:
        height = outs[0].shape[0]
        for k in range(n_out):
            start = pl.multiple_of(jnp.bitwise_xor(me, k) * height, height)
            outs[k][...] = done[pl.ds(start, height), :]


def second_axis_kernel(n_rows, n_cols, j, place, table_ref, twiddle_ref, *refs):
    lines, refs = refs[0], refs[1:]
    last = j == 1
    if last:
        before, outs, (real, imag, done) = refs[0], refs[1 : 1 + n_cols], refs[1 + n_cols :]
    else:
        done, real, imag = refs
    me = place[1]
    for r in range(n_rows):
        for c in range(n_cols):
            turned = lines[r * n_cols + c].T
            row = (c * n_rows + r) * HALF
            real[row : row + HALF, :] = turned[:HALF]
            imag[row : row + HALF, :] = turned[HALF:]

    def load(a, quarter, inner):
        rows = pl.ds(pl.multiple_of(2 * a * HALF + (quarter // 2) * HALF + inner, 8), 8)
        return (real[rows, :], imag[rows, :])

    butterflies(load, real, imag, twiddle_ref, (j,))
    real_products(real, imag, table_ref, done, (j,))
    if not last:
        return
    width = NG // n_cols
    for k in range(n_cols):
        start = jnp.bitwise_xor(me, k) * width
        rows = pl.ds(pl.multiple_of(start, LANES), width)
        outs[k][...] = done[rows, :] + before[rows, :]


def second_axis_back_kernel(n_rows, n_cols, place, table_ref, twiddle_ref, *refs):
    ins, outs, (real, imag, real_out, imag_out) = refs[:n_cols], refs[n_cols : n_cols + 2], refs[n_cols + 2 :]
    source = real_out
    me = place[1]
    width = NG // n_cols
    for k in range(n_cols):
        start = jnp.bitwise_xor(me, k) * width
        source[pl.ds(pl.multiple_of(start, LANES), width), :] = ins[k][...]

    def load(a, quarter, inner):
        return (source[pl.ds(pl.multiple_of(a * DENSE + quarter * (DENSE // 4) + inner, 8), 8), :], None)

    butterflies(load, real, imag, twiddle_ref)

    def products(x, carry):
        pieces = [bf16_parts(piece) for piece in stacked(real, imag, x, 2)]
        parts = []
        for re0, im0, re1, im1 in zip(*pieces):
            left = jnp.concatenate([re0, im0, re1, im1], axis=0)
            right = jnp.concatenate([im0, -re0, im1, -re1], axis=0)
            parts.append(jnp.concatenate([left, right], axis=1))
        both = dense_product(table_ref, 0, parts)
        rows = pl.ds(x, DENSE, stride=RADIX)
        real_out[rows, :] = both[:, :LANES]
        imag_out[rows, :] = both[:, LANES:]
        return carry

    lax.fori_loop(0, RADIX, products, 0, unroll=4)
    for r in range(n_rows):
        for c in range(n_cols):
            for j in range(2):
                row = (c * n_rows + r) * LANES + j * HALF
                tile = jnp.concatenate([real_out[row : row + HALF, :], imag_out[row : row + HALF, :]], axis=0)
                outs[j][r * n_cols + c] = tile.T


def cell_kernel(n_cov, place, coefficients, latent_ref, cov_ref, counts_ref, mask_ref, residual_ref, sums_ref, values):
    @pl.when(pl.program_id(0) == 0)
    def _():
        sums_ref[...] = jnp.zeros_like(sums_ref)

    width = latent_ref.shape[0]
    step = 16
    for t in range(0, width, LANES):
        values[:, t : t + LANES] = latent_ref[t : t + LANES, :].T

    def fold(value):
        return value[:8] + value[8:]

    for row in range(0, LANES, step):
        rows = slice(row, row + step)

        def body(t, carry, rows=rows):
            lanes = pl.ds(pl.multiple_of(t * LANES, LANES), LANES)
            total = values[rows, lanes] * (1.0 / NG)
            for j in range(n_cov):
                total += coefficients[j] * cov_ref[j, rows, lanes].astype(jnp.float32)
            intensity = jnp.exp(total)
            land = mask_ref[rows, lanes].astype(jnp.float32)
            count = counts_ref[rows, lanes].astype(jnp.float32)
            residual = land * (intensity - count)
            values[rows, lanes] = residual
            for j in range(n_cov):
                sums_ref[j] += fold(cov_ref[j, rows, lanes].astype(jnp.float32) * residual)
            sums_ref[n_cov] += fold(land * (intensity - count * total))
            return carry

        lax.fori_loop(0, width // LANES, body, 0)
    for t in range(0, width, LANES):
        residual_ref[t : t + LANES, :] = values[:, t : t + LANES].T


def final_kernel(count, place, hyper, real_ref, imag_ref, *refs):
    blocks, (step_real_ref, step_imag_ref) = refs[: 2 * count], refs[2 * count :]
    height = real_ref.shape[0]
    me, first_row, first_col = place[0], place[1], place[2]
    lane = lax.broadcasted_iota(jnp.int32, (1, LANES), 1)
    low = lane < HALF
    step = 64
    first_row = first_row + pl.program_id(0) * height
    for k in range(count):
        start = pl.multiple_of(jnp.bitwise_xor(me, k) * LANES, LANES)
        for row in range(0, height, step):
            rows = pl.ds(row, step)
            lanes = pl.ds(start, LANES)
            spec = spectrum_of(hyper, first_row + row, first_col + start, (step, LANES))
            inverse = 1.0 / (1.0 + spec * spec)
            spec = spec * (1.0 / NG)
            one, two = blocks[k][rows, :], blocks[count + k][rows, :]
            adjoint_real = jnp.where(low, one, pltpu.roll(two, HALF, 1))
            adjoint_imag = jnp.where(low, pltpu.roll(one, HALF, 1), two)
            step_real_ref[rows, lanes] = (spec * adjoint_real + real_ref[rows, lanes]) * inverse
            step_imag_ref[rows, lanes] = (imag_ref[rows, lanes] - spec * adjoint_imag) * inverse


SMEM = pl.BlockSpec(memory_space=pltpu.SMEM)
VMEM = pl.BlockSpec(memory_space=pltpu.VMEM)


def f32(*shape):
    return jax.ShapeDtypeStruct(shape, jnp.float32)


def params(mib):
    return pltpu.CompilerParams(vmem_limit_bytes=mib << 20)


def cost(flops, nbytes):
    return pl.CostEstimate(flops=int(flops), bytes_accessed=int(nbytes), transcendentals=0)


def call_scale(place, hyper, real, imag, n_rows, j):
    height, width = real.shape
    tile = 128

    def kernel(*refs):
        scale_kernel(n_rows, j, *refs)

    wide = pl.BlockSpec((tile, width), lambda i: (i, 0))
    narrow = pl.BlockSpec((tile, LANES), lambda i: (i, 0))
    *out, squares = pl.pallas_call(
        kernel,
        name="scale",
        out_shape=[f32(height, LANES)] * n_rows + [f32(8 * height // tile, LANES)],
        grid=(height // tile,),
        in_specs=[SMEM, SMEM, wide, wide],
        out_specs=[narrow] * n_rows + [pl.BlockSpec((8, LANES), lambda i: (i, 0))],
        compiler_params=params(60),
        cost_estimate=cost(2e9, 3 * 4 * real.size),
    )(place, hyper, real, imag)
    return out, jnp.sum(squares)


def call_first_axis(place, tables, ins, n_out):
    n_in = len(ins)

    def kernel(*refs):
        first_axis_kernel(n_in, n_out, *refs)

    return pl.pallas_call(
        kernel,
        name="first_axis",
        out_shape=[f32(NG // n_out, LANES)] * n_out,
        in_specs=[SMEM, VMEM, VMEM] + [VMEM] * n_in,
        out_specs=[VMEM] * n_out,
        scratch_shapes=[pltpu.VMEM((NG, LANES), jnp.float32)] * 3,
        compiler_params=params(32),
        cost_estimate=cost(5e10, 2 * 4 * NG * LANES),
    )(place, *tables, *ins)


def call_second_axis(place, tables, lines, before, n_rows, n_cols):
    j = len(before)

    def kernel(*refs):
        second_axis_kernel(n_rows, n_cols, j, *refs)

    scratch = [pltpu.VMEM((NG // 2, LANES), jnp.float32)] * 2
    return pl.pallas_call(
        kernel,
        name="second_axis",
        out_shape=[f32(NG // n_cols, LANES)] * n_cols if j else f32(NG, LANES),
        in_specs=[SMEM, VMEM, VMEM, VMEM] + [VMEM] * j,
        out_specs=[VMEM] * n_cols if j else VMEM,
        scratch_shapes=scratch + [pltpu.VMEM((NG, LANES), jnp.float32)] * j,
        compiler_params=params(32),
        cost_estimate=cost(5e10, 3 * 4 * NG * LANES),
    )(place, *tables, lines, *before)


def call_second_axis_back(place, tables, ins, n_rows, n_cols):
    def kernel(*refs):
        second_axis_back_kernel(n_rows, n_cols, *refs)

    return pl.pallas_call(
        kernel,
        name="second_axis_back",
        out_shape=[f32(n_rows * n_cols, LANES, LANES)] * 2,
        in_specs=[SMEM, VMEM, VMEM] + [VMEM] * n_cols,
        out_specs=[VMEM] * 2,
        scratch_shapes=[pltpu.VMEM((NG, LANES), jnp.float32)] * 4,
        compiler_params=params(40),
        cost_estimate=cost(5e10, 3 * 4 * NG * LANES),
    )(place, *tables, *ins)


def call_cell(place, coefficients, latent, covariates, counts, mask, k):
    n_cov = covariates.shape[0]
    width = latent.shape[0]
    tile = 256

    def kernel(*refs):
        cell_kernel(n_cov, *refs)

    def part(i, place, coefficients):
        return (jnp.bitwise_xor(place[3], k), i)

    lines = pl.BlockSpec((tile, LANES), lambda i, p, c: (i, 0))
    return pl.pallas_call(
        kernel,
        name="cell",
        out_shape=[f32(width, LANES), f32(n_cov + 1, 8, LANES)],
        grid_spec=pltpu.PrefetchScalarGridSpec(
            num_scalar_prefetch=2,
            grid=(width // tile,),
            in_specs=[
                lines,
                pl.BlockSpec((n_cov, LANES, tile), lambda i, p, c: (0, *part(i, p, c))),
                pl.BlockSpec((LANES, tile), part),
                pl.BlockSpec((LANES, tile), part),
            ],
            out_specs=[lines, pl.BlockSpec((n_cov + 1, 8, LANES), lambda i, p, c: (0, 0, 0))],
            scratch_shapes=[pltpu.VMEM((LANES, tile), jnp.float32)],
        ),
        compiler_params=params(32),
        cost_estimate=cost(2e10, width * LANES * (2 * n_cov + 16)),
    )(place, coefficients, latent, covariates, counts, mask)


def call_final(place, hyper, real, imag, blocks, n_rows):
    height, width = real.shape
    tile = 128

    def kernel(*refs):
        final_kernel(n_rows, *refs)

    wide = pl.BlockSpec((tile, width), lambda i: (i, 0))
    narrow = pl.BlockSpec((tile, LANES), lambda i: (i, 0))
    return pl.pallas_call(
        kernel,
        name="final",
        out_shape=[f32(height, width)] * 2,
        grid=(height // tile,),
        in_specs=[SMEM, SMEM, wide, wide] + [narrow] * (2 * n_rows),
        out_specs=[wide, wide],
        compiler_params=params(60),
        cost_estimate=cost(4e9, 6 * 4 * real.size),
    )(place, hyper, real, imag, *blocks)


def exchange(blocks, axis):
    count = len(blocks)
    received = [blocks[0]] + [None] * (count - 1)
    for k in range(count - 1, 0, -1):
        received[k] = lax.ppermute(blocks[k], axis, [(i, i ^ k) for i in range(count)])
    return received


def doubled(values, axis, count, steps):
    for step in steps:
        values = values + lax.ppermute(values, axis, [(i, i ^ (1 << step)) for i in range(count)])
    return values


def tiled_shards(n_rows, n_cols):
    def run(white_real, white_imag, covariates, coefficients, counts, land_mask, field_hyper):
        height, width = white_real.shape
        n_cov = covariates.shape[0]
        my_row, my_col = lax.axis_index("rows"), lax.axis_index("cols")
        place = jnp.stack([my_row, my_row * height, my_col * width, my_col]).astype(jnp.int32)
        spots = jnp.stack([my_row, my_col]).astype(jnp.int32)
        twiddles = jnp.broadcast_to(jnp.asarray(twiddle_table())[:, :, None], (4, DENSE, LANES))
        tables = (jnp.asarray(dense_table()), twiddles)

        partial, squares = (), 0.0
        for j in range(2):
            scaled, part = call_scale(place, field_hyper, white_real, white_imag, n_rows, j)
            squares = squares + part
            if j:
                columns[1], *scaled = lax.optimization_barrier((columns[1], *scaled))
            columns = exchange(scaled, "rows")
            (spread,) = call_first_axis(spots, tables, columns, 1)
            spread = spread.reshape(n_rows * n_cols, LANES, LANES)
            lines = lax.all_to_all(spread, ("rows", "cols"), 0, 0)
            if j:
                latent = exchange(call_second_axis(spots, tables, lines, partial, n_rows, n_cols), "cols")
            else:
                partial = (call_second_axis(spots, tables, lines, partial, n_rows, n_cols),)

        residuals, sums = [], 0.0
        for k in range(n_cols):
            residual, part = call_cell(place, coefficients, latent[k], covariates, counts, land_mask, k)
            residuals.append(residual)
            sums = sums + part
        back = exchange(residuals, "cols")
        sums = jnp.sum(sums, axis=(1, 2))
        own_loss = sums[n_cov] + 0.5 * squares
        own = jnp.concatenate([sums[:n_cov], jnp.broadcast_to(own_loss, (LANES - n_cov,))])
        row_steps, col_steps = n_rows.bit_length() - 1, n_cols.bit_length() - 1
        totals = doubled(doubled(own, "rows", n_rows, range(row_steps)), "cols", n_cols, range(col_steps))
        spread = call_second_axis_back(spots, tables, back, n_rows, n_cols)
        blocks = []
        for j in range(2):
            lines = lax.all_to_all(spread[j], ("rows", "cols"), 0, 0).reshape(NG, LANES)
            if j:
                lines, *blocks = lax.optimization_barrier((lines, *blocks))
            else:
                lines, totals = lax.optimization_barrier((lines, totals))
            blocks += exchange(call_first_axis(spots, tables, [lines], n_rows), "rows")

        per_cell = 1.0 / (NG * NG)
        coef_grad = (
            totals[:n_cov] * per_cell + lasso_weight * jnp.sign(coefficients) + ridge_weight * coefficients
        )
        objective = (
            totals[n_cov] * per_cell
            + lasso_weight * jnp.sum(jnp.abs(coefficients))
            + 0.5 * ridge_weight * jnp.sum(coefficients * coefficients)
        )
        step_real, step_imag = call_final(place, field_hyper, white_real, white_imag, blocks, n_rows)
        return (step_real, step_imag, coef_grad, objective)

    return run


def field_spectrum(field_hyper, wave_row, wave_col):
    amplitude = 0.2 * field_hyper[0]
    freq_range = field_hyper[1]
    radius = (wave_row[:, None] * wave_row[:, None] + wave_col[None, :] * wave_col[None, :]) / (
        freq_range * freq_range
    )
    return amplitude * (1.0 + NG / freq_range * jnp.power(1.0 + radius, -0.75))


def angle_table(left_len, right_len, modulus):
    product = lax.iota(jnp.int32, left_len)[:, None] * lax.iota(jnp.int32, right_len)[None, :]
    angles = (product % modulus).astype(jnp.float32) * (2.0 * math.pi / modulus)
    return (jnp.cos(angles), jnp.sin(angles))


def inverse_transform(pieces, want_real):
    highest = lax.Precision.HIGHEST
    components = pieces.shape[0]
    row_count = pieces.shape[1]
    length = pieces.shape[2]
    factor = 8
    others = length // factor
    shaped = pieces.reshape(components, row_count, others, factor)
    big_cos, big_sin = angle_table(others, others, others)

    def apply_big(table, block):
        return jnp.einsum("rnm,nk->rmk", block, table, precision=highest)

    if components == 2:
        real_mid = apply_big(big_cos, shaped[0]) - apply_big(big_sin, shaped[1])
        imag_mid = apply_big(big_sin, shaped[0]) + apply_big(big_cos, shaped[1])
    else:
        real_mid = apply_big(big_cos, shaped[0])
        imag_mid = apply_big(big_sin, shaped[0])
    tw_cos, tw_sin = angle_table(factor, others, length)
    real_tw = real_mid * tw_cos - imag_mid * tw_sin
    imag_tw = real_mid * tw_sin + imag_mid * tw_cos
    small_cos, small_sin = angle_table(factor, factor, factor)

    def apply_small(table, block):
        return jnp.einsum("rmk,mj->rjk", block, table, precision=highest)

    real_out = (apply_small(small_cos, real_tw) - apply_small(small_sin, imag_tw)).reshape(
        1, row_count, length
    )
    if want_real:
        return real_out
    imag_out = (apply_small(small_sin, real_tw) + apply_small(small_cos, imag_tw)).reshape(
        1, row_count, length
    )
    return jnp.concatenate([real_out, imag_out], axis=0)


def middle_step(spread):
    returned = lax.all_to_all(spread, "cols", split_axis=2, concat_axis=1, tiled=True)
    flipped = jnp.swapaxes(returned, 1, 2)
    return lax.all_to_all(flipped, "rows", split_axis=1, concat_axis=2, tiled=True)


def grid_transform(pieces, want_real):
    full_rows = lax.all_to_all(pieces, "cols", split_axis=1, concat_axis=2, tiled=True)
    halfway = inverse_transform(full_rows, False)
    columns = middle_step(halfway)
    second = inverse_transform(columns, want_real)
    blocks_out = lax.all_to_all(second, "rows", split_axis=2, concat_axis=1, tiled=True)
    return jnp.swapaxes(blocks_out, 1, 2) * (1.0 / NG)


def shards(white_real, white_imag, covariates, coefficients, counts, land_mask, field_hyper):
    highest = lax.Precision.HIGHEST
    rows_here = white_real.shape[0]
    cols_here = white_real.shape[1]
    freq_row = lax.axis_index("rows") * rows_here + lax.iota(jnp.int32, rows_here)
    freq_col = lax.axis_index("cols") * cols_here + lax.iota(jnp.int32, cols_here)
    wave_row = jnp.minimum(freq_row, NG - freq_row).astype(jnp.float32)
    wave_col = jnp.minimum(freq_col, NG - freq_col).astype(jnp.float32)
    spectrum = field_spectrum(field_hyper, wave_row, wave_col)
    scaled = jnp.stack([spectrum * white_real, spectrum * white_imag])
    latent = grid_transform(scaled, True)[0]
    cov_full = covariates.astype(jnp.float32)
    linear = jnp.einsum("j,jrc->rc", coefficients, cov_full, precision=highest)
    log_rate = linear + latent
    intensity = jnp.exp(log_rate)
    land_vals = land_mask.astype(jnp.float32)
    count_vals = counts.astype(jnp.float32)
    residual = land_vals * (intensity - count_vals)
    partial_coef = jnp.einsum("jrc,rc->j", cov_full, residual, precision=highest)
    partial_loss = jnp.sum(land_vals * (intensity - count_vals * log_rate)) + 0.5 * jnp.sum(
        white_real * white_real + white_imag * white_imag
    )
    adjoint = grid_transform(residual[None], False)
    total_coef, total_loss = lax.psum((partial_coef, partial_loss), ("rows", "cols"))
    per_cell = 1.0 / (NG * NG)
    coef_grad = (
        total_coef * per_cell + lasso_weight * jnp.sign(coefficients) + ridge_weight * coefficients
    )
    objective = (
        total_loss * per_cell
        + lasso_weight * jnp.sum(jnp.abs(coefficients))
        + 0.5 * ridge_weight * jnp.sum(coefficients * coefficients)
    )
    curvature = 1.0 + spectrum * spectrum
    step_real = (spectrum * adjoint[0] + white_real) / curvature
    step_imag = (white_imag - spectrum * adjoint[1]) / curvature
    return (step_real, step_imag, coef_grad, objective)


def solution(mesh):
    n_rows, n_cols = mesh.shape["rows"], mesh.shape["cols"]
    tiled = n_rows * n_cols * LANES == NG and not n_rows & (n_rows - 1) and not n_cols & (n_cols - 1)
    return jax.shard_map(
        tiled_shards(n_rows, n_cols) if tiled else shards,
        mesh=mesh,
        in_specs=(
            P("rows", "cols"),
            P("rows", "cols"),
            P(None, "rows", "cols"),
            P(),
            P("rows", "cols"),
            P("rows", "cols"),
            P(),
        ),
        out_specs=(P("rows", "cols"), P("rows", "cols"), P(), P()),
        check_vma=False,
    )
```

time: 493 us -> 425 us (0.86)
  blocking collectives: 109 us -> 0 us
  waiting for transfers between devices: 176 us -> 232 us
  local copies, waits for them, and re-layouts: 38.5 us -> 22 us
  Pallas kernels: 106 us -> 92.6 us
  starting transfers between devices: 54 us -> 67.3 us
    all_to_all x2 -> x0, blocking collectives: 109 us -> none  [the longest x1 58.7 us: run(): lines = lax.all_to_all(spread[j], ('rows', 'cols'), 0, 0).reshape(NG, LANES)]
    all_to_all x1 -> x2, waiting for transfers between devices: 0.01 us -> 56.9 us  [run(): lines = lax.all_to_all(spread, ('rows', 'cols'), 0, 0)]
    ppermute x34, waiting for transfers between devices: 148 us -> 116 us  [exchange(): lax.ppermute(blocks[k], axis, [(i, i ^ k) for i in range(count)])]
    all_to_all x1 -> x2, waiting for transfers between devices: 0.01 us -> 22.8 us  [run(): lines = lax.all_to_all(spread[j], ('rows', 'cols'), 0, 0).reshape(NG, LANES)]
    unnamed x78 -> x80, local copies, waits for them, and re-layouts: 37.3 us -> 20.7 us
    pallas_call x4, Pallas kernels: 47.2 us -> 31.2 us  [call_first_axis(): pl.pallas_call(kernel, name='first_axis', out_shape=[f32(NG // n_out, LAN...]
    all_to_all x1 -> x2, starting transfers between devices: 4.63 us -> 15.2 us  [run(): lines = lax.all_to_all(spread[j], ('rows', 'cols'), 0, 0).reshape(NG, LANES)]
    ppermute x5, waiting for transfers between devices: 28.4 us -> 36.8 us  [doubled(): lax.ppermute(values, axis, [(i, i ^ 1 << step) for i in range(count)])]
  transfers between devices with their start and end apart: 41 -> 43, of which waited for: 17 -> 20; matrix products, arithmetic and copies ran while one was open for 1% -> 1% of each run, Pallas kernels for 10% -> 13%
where the time goes in v2:
time: 425 us; the launch traced here: 424 us
  waiting for transfers between devices  232 us (55%)
  Pallas kernels  92.6 us (22%)
  starting transfers between devices  67.3 us (16%)
  local copies, waits for them, and re-layouts  22 us (5%)
  between operations  6.16 us (1%)
    ppermute x34, waiting for transfers between devices, exchange(): lax.ppermute(blocks[k], axis, [(i, i ^ k) for i in range(count)])  116 us
    all_to_all x2, waiting for transfers between devices, run(): lines = lax.all_to_all(spread, ('rows', 'cols'), 0, 0)  56.9 us
    ppermute x5, waiting for transfers between devices, doubled(): lax.ppermute(values, axis, [(i, i ^ 1 << step) for i in range(count)])  36.8 us
    ppermute x34, starting transfers between devices, exchange(): lax.ppermute(blocks[k], axis, [(i, i ^ k) for i in range(count)])  34.2 us
    pallas_call x4, Pallas kernels, call_first_axis(): pl.pallas_call(kernel, name='first_axis', out_shape=[f32(NG // n_out, LAN...  31.2 us
    all_to_all x2, waiting for transfers between devices, run(): lines = lax.all_to_all(spread[j], ('rows', 'cols'), 0, 0).reshape(NG, LANES)  22.8 us
    unnamed x80, local copies, waits for them, and re-layouts  20.7 us
    pallas_call x4, Pallas kernels, call_cell(): pl.pallas_call(kernel, name='cell', out_shape=[f32(width, LANES), f32(n_c...  20.1 us
  transfers between devices with their start and end apart: 43, of which 20 were waited for; matrix products, arithmetic and copies ran while one was open for 1% of the time, Pallas kernels for 13%

profile of v2, /device:TPU:0, one launch (start us, length us, event | category | flops | bytes accessed | tf_op | source)
XLA Modules:
  0.0 423.6 jit_solution(16825196790785055300)
XLA Ops:
  1.2 5.4 %scale.2 = (f32[512,128]{1,0:T(8,128)}, f32[512,128]{1,0:T(8,128)}, f32[512,128]{1,0:T(8,128)}, f32[512,128]{1,0:T(8,128)}, f32[512,128]{1,0:T(8,128)}, /*index=...) custom-call(s32[4]{0:T(128)} %pad_add_fusion.refs_0_, f32[2]{0:T(128)} %refs_1_.20, ...), custom_call_target="tpu_custom_call" | custom-call | flops 2000000000 | bytes 6291456 | tf_op jit(solution)/shard_map/scale/pallas_call | solution.py:380
  11.7 5.5 %scale.3 = (f32[512,128]{1,0:T(8,128)}, f32[512,128]{1,0:T(8,128)}, f32[512,128]{1,0:T(8,128)}, f32[512,128]{1,0:T(8,128)}, f32[512,128]{1,0:T(8,128)}, /*index=...) custom-call(s32[4]{0:T(128)} %pad_add_fusion.refs_0_, f32[2]{0:T(128)} %refs_1_.20, ...), custom_call_target="tpu_custom_call" | custom-call | flops 2000000000 | bytes 6291456 | tf_op jit(solution)/shard_map/scale/pallas_call | solution.py:380
  24.9 9.9 %collective-permute-done.11.refs_8_ = f32[512,128]{1,0:T(8,128)S(1)} collective-permute-done((f32[512,128]{1,0:T(8,128)}, f32[512,128]{1,0:T(8,128)S(1)}, u32[]{:S(2)}, u32[]{:S(2)}) %collective-permute-start.11) | collective-permute-done | bytes 262176 | tf_op jit(solution)/shard_map/ppermute | solution.py:504
  41.6 7.1 %first_axis.5 = f32[4096,128]{1,0:T(8,128)S(1)} custom-call(s32[2]{0:T(128)S(1)} %pad_add_fusion.1.refs_0_, bf16[256,1536]{1,0:T(8,128)(2,1)S(1)} %copy-done.9, f32[4,256,128]{2,1,0:T(8,128)S(1)} %broadcast_in_dim.2.refs_2_, f32[512,128]{1,0:T(8,128)S(1)} %copy-done.16, f32[512,128]{1,0:T(8,128)S(1)} %collective-permute-done.refs_4_, ...), custom_call_target="tpu_custom_call" | custom-call | flops 49999998976 | bytes 4194304 | tf_op jit(solution)/shard_map/first_axis/pallas_call | solution.py:399
  57.7 17.5 %collective-permute-done.5.refs_8_ = f32[512,128]{1,0:T(8,128)} collective-permute-done((f32[512,128]{1,0:T(8,128)}, f32[512,128]{1,0:T(8,128)}, u32[]{:S(2)}, u32[]{:S(2)}) %collective-permute-start.5) | collective-permute-done | bytes 262176 | tf_op jit(solution)/shard_map/ppermute | solution.py:504
  77.3 7.8 %first_axis.4 = f32[4096,128]{1,0:T(8,128)S(1)} custom-call(s32[2]{0:T(128)S(1)} %pad_add_fusion.1.refs_0_, bf16[256,1536]{1,0:T(8,128)(2,1)S(1)} %copy-done.10, f32[4,256,128]{2,1,0:T(8,128)S(1)} %broadcast_in_dim.2.refs_2_, f32[512,128]{1,0:T(8,128)S(1)} %copy-done.15, f32[512,128]{1,0:T(8,128)S(1)} %collective-permute-done.1.refs_4_, ...), custom_call_target="tpu_custom_call" | custom-call | flops 49999998976 | bytes 4194304 | tf_op jit(solution)/shard_map/first_axis/pallas_call | solution.py:399
  86.4 16.1 %all-to-all-done.1.refs_3_ = f32[32,128,128]{2,1,0:T(8,128)S(1)} async-done(((f32[32,128,128]{2,1,0:T(8,128)}), f32[32,128,128]{2,1,0:T(8,128)S(1)}, u32[]{:S(2)}, u32[]{:S(2)}) %all-to-all-start.1) | async-done | bytes 2097184 | tf_op jit(solution)/shard_map/all_to_all | solution.py:533
  112.8 40.9 %all-to-all-done.refs_3_ = f32[32,128,128]{2,1,0:T(8,128)} async-done(((f32[32,128,128]{2,1,0:T(8,128)}), f32[32,128,128]{2,1,0:T(8,128)}, u32[]{:S(2)}, u32[]{:S(2)}) %all-to-all-start) | async-done | bytes 2097184 | tf_op jit(solution)/shard_map/all_to_all | solution.py:533
  155.2 5.9 %second_axis.3 = (f32[1024,128]{1,0:T(8,128)S(1)}, f32[1024,128]{1,0:T(8,128)S(1)}, f32[1024,128]{1,0:T(8,128)S(1)}, f32[1024,128]{1,0:T(8,128)S(1)}) custom-call(s32[2]{0:T(128)S(1)} %pad_add_fusion.1.refs_0_, bf16[256,1536]{1,0:T(8,128)(2,1)S(1)} %copy-done.11, f32[4,256,128]{2,1,0:T(8,128)S(1)} %broadcast_in_dim.2.refs_2_, ...), custom_call_target="tpu_custom_call" | custom-call | flops 49999998976 | bytes 6291456 | tf_op jit(solution)/shard_map/second_axis/pallas_call | solution.py:418
  167.4 19.0 %collective-permute-done.14.refs_2_ = f32[1024,128]{1,0:T(8,128)S(1)} collective-permute-done((f32[1024,128]{1,0:T(8,128)S(1)}, f32[1024,128]{1,0:T(8,128)S(1)}, u32[]{:S(2)}, u32[]{:S(2)}) %collective-permute-start.14) | collective-permute-done | bytes 524320 | tf_op jit(solution)/shard_map/ppermute | solution.py:504
  186.4 5.8 %copy-done.6 = bf16[16,512,1024]{2,1,0:T(8,128)(2,1)S(1)} copy-done((bf16[16,512,1024]{2,1,0:T(8,128)(2,1)S(1)}, bf16[16,512,1024]{2,1,0:T(8,128)(2,1)}, u32[]{:S(2)}) %copy-start.6) | copy-done | bytes 16777240
  197.3 5.9 %collective-permute-done.16.refs_2_ = f32[1024,128]{1,0:T(8,128)S(1)} collective-permute-done((f32[1024,128]{1,0:T(8,128)S(1)}, f32[1024,128]{1,0:T(8,128)S(1)}, u32[]{:S(2)}, u32[]{:S(2)}) %collective-permute-start.16) | collective-permute-done | bytes 524320 | tf_op jit(solution)/shard_map/ppermute | solution.py:504
  219.0 29.2 %collective-permute-done.17.refs_5_ = f32[1024,128]{1,0:T(8,128)S(1)} collective-permute-done((f32[1024,128]{1,0:T(8,128)S(1)}, f32[1024,128]{1,0:T(8,128)S(1)}, u32[]{:S(2)}, u32[]{:S(2)}) %collective-permute-start.17) | collective-permute-done | bytes 524320 | tf_op jit(solution)/shard_map/ppermute | solution.py:504
  248.2 12.9 %second_axis_back.1 = (f32[32,128,128]{2,1,0:T(8,128)S(1)}, f32[32,128,128]{2,1,0:T(8,128)}) custom-call(s32[2]{0:T(128)S(1)} %pad_add_fusion.1.refs_0_, bf16[256,1536]{1,0:T(8,128)(2,1)S(1)} %copy-done.12, f32[4,256,128]{2,1,0:T(8,128)S(1)} %broadcast_in_dim.2.refs_2_, f32[1024,128]{1,0:T(8,128)S(1)} %get-tuple-element.98.refs_3_, ...), custom_call_target="tpu_custom_call" | custom-call | flops 49999998976 | bytes 6291456 | tf_op jit(solution)/shard_map/second_axis_back/pallas_call | solution.py:434
  262.4 11.5 %all-to-all-start.3 = ((f32[32,128,128]{2,1,0:T(8,128)}), f32[32,128,128]{2,1,0:T(8,128)S(1)}, u32[]{:S(2)}, u32[]{:S(2)}) async-start(f32[32,128,128]{2,1,0:T(8,128)} %copy-done), calls=%async_computation.3 | async-start | bytes 4194304 | tf_op jit(solution)/shard_map/all_to_all | solution.py:553
  280.8 7.5 %collective-permute-done.21 = f32[128]{0:T(128)S(1)} collective-permute-done((f32[128]{0:T(128)S(1)}, f32[128]{0:T(128)S(1)}, u32[]{:S(2)}, u32[]{:S(2)}) %collective-permute-start.21) | collective-permute-done | bytes 544 | tf_op jit(solution)/shard_map/ppermute | solution.py:510
  292.2 16.6 %collective-permute-done.23 = f32[128]{0:T(128)S(1)} collective-permute-done((f32[128]{0:T(128)S(1)}, f32[128]{0:T(128)S(1)}, u32[]{:S(2)}, u32[]{:S(2)}) %collective-permute-start.23) | collective-permute-done | bytes 544 | tf_op jit(solution)/shard_map/ppermute | solution.py:510
  313.6 9.6 %collective-permute-done.24 = f32[128]{0:T(128)S(1)} collective-permute-done((f32[128]{0:T(128)S(1)}, f32[128]{0:T(128)S(1)}, u32[]{:S(2)}, u32[]{:S(2)}) %collective-permute-start.24) | collective-permute-done | bytes 544 | tf_op jit(solution)/shard_map/ppermute | solution.py:510
  328.1 8.0 %first_axis.6 = (f32[512,128]{1,0:T(8,128)S(1)}, f32[512,128]{1,0:T(8,128)S(1)}, f32[512,128]{1,0:T(8,128)S(1)}, f32[512,128]{1,0:T(8,128)}, f32[512,128]{1,0:T(...) custom-call(s32[2]{0:T(128)S(1)} %pad_add_fusion.1.refs_0_, ...), custom_call_target="tpu_custom_call" | custom-call | flops 49999998976 | bytes 4194304 | tf_op jit(solution)/shard_map/first_axis/pallas_call | solution.py:399
  342.7 8.0 %collective-permute-done.26.refs_6_ = f32[512,128]{1,0:T(8,128)S(1)} collective-permute-done((f32[512,128]{1,0:T(8,128)S(1)}, f32[512,128]{1,0:T(8,128)S(1)}, u32[]{:S(2)}, u32[]{:S(2)}) %collective-permute-start.26) | collective-permute-done | bytes 262176 | tf_op jit(solution)/shard_map/ppermute | solution.py:504
  351.4 22.8 %all-to-all-done.2 = f32[32,128,128]{2,1,0:T(8,128)} async-done(((f32[32,128,128]{2,1,0:T(8,128)}), f32[32,128,128]{2,1,0:T(8,128)}, u32[]{:S(2)}, u32[]{:S(2)}) %all-to-all-start.2) | async-done | bytes 2097184 | tf_op jit(solution)/shard_map/all_to_all | solution.py:553
  378.7 8.2 %first_axis.7 = (f32[512,128]{1,0:T(8,128)S(1)}, f32[512,128]{1,0:T(8,128)S(1)}, f32[512,128]{1,0:T(8,128)S(1)}, f32[512,128]{1,0:T(8,128)S(1)}, f32[512,128]{1,...) custom-call(s32[2]{0:T(128)S(1)} %pad_add_fusion.1.refs_0_, ...), custom_call_target="tpu_custom_call" | custom-call | flops 49999998976 | bytes 4194304 | tf_op jit(solution)/shard_map/first_axis/pallas_call | solution.py:399
  401.5 13.1 %collective-permute-done.36.refs_17_ = f32[512,128]{1,0:T(8,128)S(1)} collective-permute-done((f32[512,128]{1,0:T(8,128)S(1)}, f32[512,128]{1,0:T(8,128)S(1)}, u32[]{:S(2)}, u32[]{:S(2)}) %collective-permute-start.36) | collective-permute-done | bytes 262176 | tf_op jit(solution)/shard_map/ppermute | solution.py:504
  415.5 7.0 %final.1 = (f32[512,1024]{1,0:T(8,128)}, f32[512,1024]{1,0:T(8,128)}) custom-call(s32[4]{0:T(128)} %pad_add_fusion.refs_0_, f32[2]{0:T(128)} %refs_1_.20, f32[512,1024]{1,0:T(8,128)} %refs_2_.5, f32[512,1024]{1,0:T(8,128)} %refs_3_.13, f32[512,128]{1,0:T(8,128)} %copy-done.17, f32[512,128]{1,0:T(8,128)} %copy-done.24, f32[512,128]{1,0:T(8,128)} %copy-done.25, ...), custom_call_target="tpu_custom_call" | custom-call | flops 4000000000 | bytes 12582912 | tf_op jit(solution)/shard_map/final/pallas_call | solution.py:488
  (171 shorter events, 116.1 us)
Async XLA Ops:
  11.6 23.2 %collective-permute-start.11 = (f32[512,128]{1,0:T(8,128)}, f32[512,128]{1,0:T(8,128)S(1)}, u32[]{:S(2)}, u32[]{:S(2)}) collective-permute-start(f32[512,128]{1,0:T(8,128)} %get-tuple-element.94), channel_id=1, source_target_pairs={{0,20},{4,16},{8,28},{12,24},{16,4},{20,0},{24,12},{28,8},{1,21},{... | collective-permute-start | bytes 786440 | tf_op jit(solution)/shard_map/ppermute | solution.py:504
  17.2 19.7 %collective-permute-start.12 = (f32[512,128]{1,0:T(8,128)S(1)}, f32[512,128]{1,0:T(8,128)S(1)}, u32[]{:S(2)}, u32[]{:S(2)}) collective-permute-start(f32[512,128]{1,0:T(8,128)S(1)} %copy-done.36), channel_id=1, source_target_pairs={{0,24},{4,28},{8,16},{12,20},{16,8},{20,12},{24,0},{28,4},{1,25},{... | collective-permute-start | bytes 786440 | tf_op jit(solution)/shard_map/ppermute | solution.py:504
  34.8 20.1 %collective-permute-start.3 = (f32[512,128]{1,0:T(8,128)}, f32[512,128]{1,0:T(8,128)S(1)}, u32[]{:S(2)}, u32[]{:S(2)}) collective-permute-start(f32[512,128]{1,0:T(8,128)} %get-tuple-element.85), channel_id=1, source_target_pairs={{0,12},{4,8},{8,4},{12,0},{16,28},{20,24},{24,20},{28,16},{1,13},{... | collective-permute-start | bytes 786440 | tf_op jit(solution)/shard_map/ppermute | solution.py:504
  36.9 20.8 %collective-permute-start.4 = (f32[512,128]{1,0:T(8,128)}, f32[512,128]{1,0:T(8,128)}, u32[]{:S(2)}, u32[]{:S(2)}) collective-permute-start(f32[512,128]{1,0:T(8,128)} %get-tuple-element.86), channel_id=1, source_target_pairs={{0,16},{4,20},{8,24},{12,28},{16,0},{20,4},{24,8},{28,12},{1,17},{... | collective-permute-start | bytes 786440 | tf_op jit(solution)/shard_map/ppermute | solution.py:504
  38.4 36.8 %collective-permute-start.5 = (f32[512,128]{1,0:T(8,128)}, f32[512,128]{1,0:T(8,128)}, u32[]{:S(2)}, u32[]{:S(2)}) collective-permute-start(f32[512,128]{1,0:T(8,128)} %get-tuple-element.87), channel_id=1, source_target_pairs={{0,20},{4,16},{8,28},{12,24},{16,4},{20,0},{24,12},{28,8},{1,21},{... | collective-permute-start | bytes 786440 | tf_op jit(solution)/shard_map/ppermute | solution.py:504
  38.4 36.8 %collective-permute-start.6 = (f32[512,128]{1,0:T(8,128)}, f32[512,128]{1,0:T(8,128)}, u32[]{:S(2)}, u32[]{:S(2)}) collective-permute-start(f32[512,128]{1,0:T(8,128)} %get-tuple-element.88), channel_id=1, source_target_pairs={{0,24},{4,28},{8,16},{12,20},{16,8},{20,12},{24,0},{28,4},{1,25},{... | collective-permute-start | bytes 786440 | tf_op jit(solution)/shard_map/ppermute | solution.py:504
  39.6 35.6 %collective-permute-start.7 = (f32[512,128]{1,0:T(8,128)}, f32[512,128]{1,0:T(8,128)}, u32[]{:S(2)}, u32[]{:S(2)}) collective-permute-start(f32[512,128]{1,0:T(8,128)} %get-tuple-element.89), channel_id=1, source_target_pairs={{0,28},{4,24},{8,20},{12,16},{16,12},{20,8},{24,4},{28,0},{1,29},{... | collective-permute-start | bytes 786440 | tf_op jit(solution)/shard_map/ppermute | solution.py:504
  50.1 52.4 %all-to-all-start.1 = ((f32[32,128,128]{2,1,0:T(8,128)}), f32[32,128,128]{2,1,0:T(8,128)S(1)}, u32[]{:S(2)}, u32[]{:S(2)}) async-start(f32[32,128,128]{2,1,0:T(8,128)} %bitcast.12), calls=%async_computation.1 | async-start | bytes 4194304 | tf_op jit(solution)/shard_map/all_to_all | solution.py:533
  102.5 51.2 %all-to-all-start = ((f32[32,128,128]{2,1,0:T(8,128)}), f32[32,128,128]{2,1,0:T(8,128)}, u32[]{:S(2)}, u32[]{:S(2)}) async-start(f32[32,128,128]{2,1,0:T(8,128)} %bitcast.13), calls=%async_computation | async-start | bytes 4194304 | tf_op jit(solution)/shard_map/all_to_all | solution.py:533
  161.2 25.2 %collective-permute-start.14 = (f32[1024,128]{1,0:T(8,128)S(1)}, f32[1024,128]{1,0:T(8,128)S(1)}, u32[]{:S(2)}, u32[]{:S(2)}) collective-permute-start(f32[1024,128]{1,0:T(8,128)S(1)} %get-tuple-element.99), channel_id=1, source_target_pairs={{0,1},{1,0},{2,3},{3,2},{4,5},{5,4},{6,7},{7,6},{8,9},{9,8},{10,11... | collective-permute-start | bytes 1572872 | tf_op jit(solution)/shard_map/ppermute | solution.py:504
  165.0 38.2 %collective-permute-start.16 = (f32[1024,128]{1,0:T(8,128)S(1)}, f32[1024,128]{1,0:T(8,128)S(1)}, u32[]{:S(2)}, u32[]{:S(2)}) collective-permute-start(f32[1024,128]{1,0:T(8,128)S(1)} %get-tuple-element.101), channel_id=1, source_target_pairs={{0,2},{1,3},{2,0},{3,1},{4,6},{5,7},{6,4},{7,5},{8,10},{9,11},{10,... | collective-permute-start | bytes 1572872 | tf_op jit(solution)/shard_map/ppermute | solution.py:504
  165.1 43.2 %collective-permute-start.18 = (f32[1024,128]{1,0:T(8,128)S(1)}, f32[1024,128]{1,0:T(8,128)S(1)}, u32[]{:S(2)}, u32[]{:S(2)}) collective-permute-start(f32[1024,128]{1,0:T(8,128)S(1)} %get-tuple-element.103), channel_id=1, source_target_pairs={{0,3},{1,2},{2,1},{3,0},{4,7},{5,6},{6,5},{7,4},{8,11},{9,10},{10,... | collective-permute-start | bytes 1572872 | tf_op jit(solution)/shard_map/ppermute | solution.py:504
  197.2 21.8 %collective-permute-start.15 = (f32[1024,128]{1,0:T(8,128)S(1)}, f32[1024,128]{1,0:T(8,128)S(1)}, u32[]{:S(2)}, u32[]{:S(2)}) collective-permute-start(f32[1024,128]{1,0:T(8,128)S(1)} %get-tuple-element.100), channel_id=1, source_target_pairs={{0,1},{1,0},{2,3},{3,2},{4,5},{5,4},{6,7},{7,6},{8,9},{9,8},{10,11... | collective-permute-start | bytes 1572872 | tf_op jit(solution)/shard_map/ppermute | solution.py:504
  208.2 39.9 %collective-permute-start.17 = (f32[1024,128]{1,0:T(8,128)S(1)}, f32[1024,128]{1,0:T(8,128)S(1)}, u32[]{:S(2)}, u32[]{:S(2)}) collective-permute-start(f32[1024,128]{1,0:T(8,128)S(1)} %get-tuple-element.102), channel_id=1, source_target_pairs={{0,2},{1,3},{2,0},{3,1},{4,6},{5,7},{6,4},{7,5},{8,10},{9,11},{10,... | collective-permute-start | bytes 1572872 | tf_op jit(solution)/shard_map/ppermute | solution.py:504
  213.4 34.8 %collective-permute-start.19 = (f32[1024,128]{1,0:T(8,128)S(1)}, f32[1024,128]{1,0:T(8,128)S(1)}, u32[]{:S(2)}, u32[]{:S(2)}) collective-permute-start(f32[1024,128]{1,0:T(8,128)S(1)} %get-tuple-element.104), channel_id=1, source_target_pairs={{0,3},{1,2},{2,1},{3,0},{4,7},{5,6},{6,5},{7,4},{8,11},{9,10},{10,... | collective-permute-start | bytes 1572872 | tf_op jit(solution)/shard_map/ppermute | solution.py:504
  262.4 60.9 %all-to-all-start.3 = ((f32[32,128,128]{2,1,0:T(8,128)}), f32[32,128,128]{2,1,0:T(8,128)S(1)}, u32[]{:S(2)}, u32[]{:S(2)}) async-start(f32[32,128,128]{2,1,0:T(8,128)} %copy-done), calls=%async_computation.3 | async-start | bytes 4194304 | tf_op jit(solution)/shard_map/all_to_all | solution.py:553
  323.3 51.0 %all-to-all-start.2 = ((f32[32,128,128]{2,1,0:T(8,128)}), f32[32,128,128]{2,1,0:T(8,128)}, u32[]{:S(2)}, u32[]{:S(2)}) async-start(f32[32,128,128]{2,1,0:T(8,128)} %get-tuple-element.105), calls=%async_computation.2 | async-start | bytes 4194304 | tf_op jit(solution)/shard_map/all_to_all | solution.py:553
  338.3 35.9 %collective-permute-start.27 = (f32[512,128]{1,0:T(8,128)}, f32[512,128]{1,0:T(8,128)S(1)}, u32[]{:S(2)}, u32[]{:S(2)}) collective-permute-start(f32[512,128]{1,0:T(8,128)} %get-tuple-element.117), channel_id=1, source_target_pairs={{0,12},{4,8},{8,4},{12,0},{16,28},{20,24},{24,20},{28,16},{1,13},{... | collective-permute-start | bytes 786440 | tf_op jit(solution)/shard_map/ppermute | solution.py:504
  338.7 35.6 %collective-permute-start.28 = (f32[512,128]{1,0:T(8,128)}, f32[512,128]{1,0:T(8,128)S(1)}, u32[]{:S(2)}, u32[]{:S(2)}) collective-permute-start(f32[512,128]{1,0:T(8,128)} %get-tuple-element.118), channel_id=1, source_target_pairs={{0,16},{4,20},{8,24},{12,28},{16,0},{20,4},{24,8},{28,12},{1,17},{... | collective-permute-start | bytes 786440 | tf_op jit(solution)/shard_map/ppermute | solution.py:504
  340.0 34.2 %collective-permute-start.29 = (f32[512,128]{1,0:T(8,128)S(1)}, f32[512,128]{1,0:T(8,128)S(1)}, u32[]{:S(2)}, u32[]{:S(2)}) collective-permute-start(f32[512,128]{1,0:T(8,128)S(1)} %get-tuple-element.119), channel_id=1, source_target_pairs={{0,20},{4,16},{8,28},{12,24},{16,4},{20,0},{24,12},{28,8},{1,21},{... | collective-permute-start | bytes 786440 | tf_op jit(solution)/shard_map/ppermute | solution.py:504
  340.3 34.0 %collective-permute-start.30 = (f32[512,128]{1,0:T(8,128)S(1)}, f32[512,128]{1,0:T(8,128)S(1)}, u32[]{:S(2)}, u32[]{:S(2)}) collective-permute-start(f32[512,128]{1,0:T(8,128)S(1)} %get-tuple-element.120), channel_id=1, source_target_pairs={{0,24},{4,28},{8,16},{12,20},{16,8},{20,12},{24,0},{28,4},{1,25},{... | collective-permute-start | bytes 786440 | tf_op jit(solution)/shard_map/ppermute | solution.py:504
  351.4 25.5 %collective-permute-start.31 = (f32[512,128]{1,0:T(8,128)S(1)}, f32[512,128]{1,0:T(8,128)S(1)}, u32[]{:S(2)}, u32[]{:S(2)}) collective-permute-start(f32[512,128]{1,0:T(8,128)S(1)} %get-tuple-element.121), channel_id=1, source_target_pairs={{0,28},{4,24},{8,20},{12,16},{16,12},{20,8},{24,4},{28,0},{1,29},{... | collective-permute-start | bytes 786440 | tf_op jit(solution)/shard_map/ppermute | solution.py:504
  390.3 24.3 %collective-permute-start.36 = (f32[512,128]{1,0:T(8,128)S(1)}, f32[512,128]{1,0:T(8,128)S(1)}, u32[]{:S(2)}, u32[]{:S(2)}) collective-permute-start(f32[512,128]{1,0:T(8,128)S(1)} %get-tuple-element.136), channel_id=1, source_target_pairs={{0,20},{4,16},{8,28},{12,24},{16,4},{20,0},{24,12},{28,8},{1,21},{... | collective-permute-start | bytes 786440 | tf_op jit(solution)/shard_map/ppermute | solution.py:504
  391.3 23.3 %collective-permute-start.37 = (f32[512,128]{1,0:T(8,128)S(1)}, f32[512,128]{1,0:T(8,128)S(1)}, u32[]{:S(2)}, u32[]{:S(2)}) collective-permute-start(f32[512,128]{1,0:T(8,128)S(1)} %get-tuple-element.137), channel_id=1, source_target_pairs={{0,24},{4,28},{8,16},{12,20},{16,8},{20,12},{24,0},{28,4},{1,25},{... | collective-permute-start | bytes 786440 | tf_op jit(solution)/shard_map/ppermute | solution.py:504
  (59 other events, 759.5 us)

commit v3 on v2

--- a/solution.py
+++ b/solution.py
@@ -168,8 +168,8 @@
     wave_col = jnp.minimum(cols, NG - cols).astype(jnp.float32)
     amplitude = 0.2 * hyper[0]
     span = hyper[1]
-    base = 1.0 + (wave_row * wave_row + wave_col * wave_col) * (1.0 / (span * span))
-    return amplitude * (1.0 + (NG / span) / jnp.sqrt(base * jnp.sqrt(base)))
+    root = lax.rsqrt(1.0 + (wave_row * wave_row + wave_col * wave_col) * (1.0 / (span * span)))
+    return amplitude + (amplitude * (NG / span)) * (root * root * lax.rsqrt(root))
 
 
 def scale_kernel(count, j, place, hyper, real_ref, imag_ref, *outs):
@@ -231,7 +231,9 @@
     lines, refs = refs[0], refs[1:]
     last = j == 1
     if last:
-        before, outs, (real, imag, done) = refs[0], refs[1 : 1 + n_cols], refs[1 + n_cols :]
+        outs, (real, imag, done, before, arrived) = refs[1 : 1 + n_cols], refs[1 + n_cols :]
+        copy = pltpu.make_async_copy(refs[0], before, arrived)
+        copy.start()
     else:
         done, real, imag = refs
     me = place[1]
@@ -250,6 +252,7 @@
     real_products(real, imag, table_ref, done, (j,))
     if not last:
         return
+    copy.wait()
     width = NG // n_cols
     for k in range(n_cols):
         start = jnp.bitwise_xor(me, k) * width
@@ -419,9 +422,9 @@
         kernel,
         name="second_axis",
         out_shape=[f32(NG // n_cols, LANES)] * n_cols if j else f32(NG, LANES),
-        in_specs=[SMEM, VMEM, VMEM, VMEM] + [VMEM] * j,
+        in_specs=[SMEM, VMEM, VMEM, VMEM] + [pl.BlockSpec(memory_space=pl.ANY)] * j,
         out_specs=[VMEM] * n_cols if j else VMEM,
-        scratch_shapes=scratch + [pltpu.VMEM((NG, LANES), jnp.float32)] * j,
+        scratch_shapes=scratch + ([pltpu.VMEM((NG, LANES), jnp.float32)] * 2 + [pltpu.SemaphoreType.DMA]) * j,
         compiler_params=params(32),
         cost_estimate=cost(5e10, 3 * 4 * NG * LANES),
     )(place, *tables, lines, *before)
@@ -497,18 +500,23 @@
     )(place, hyper, real, imag, *blocks)
 
 
+def send(values, axis, count, k):
+    return lax.ppermute(values, axis, [(i, i ^ k) for i in range(count)])
+
+
 def exchange(blocks, axis):
     count = len(blocks)
     received = [blocks[0]] + [None] * (count - 1)
     for k in range(count - 1, 0, -1):
-        received[k] = lax.ppermute(blocks[k], axis, [(i, i ^ k) for i in range(count)])
+        received[k] = send(blocks[k], axis, count, k)
     return received
 
 
-def doubled(values, axis, count, steps):
-    for step in steps:
-        values = values + lax.ppermute(values, axis, [(i, i ^ (1 << step)) for i in range(count)])
-    return values
+def sum_over(values, axis, count):
+    terms = exchange([values] * count, axis)
+    while len(terms) > 1:
+        terms = [terms[i] + terms[i + 1] for i in range(0, len(terms), 2)]
+    return terms[0]
 
 
 def tiled_shards(n_rows, n_cols):
@@ -532,21 +540,28 @@
             spread = spread.reshape(n_rows * n_cols, LANES, LANES)
             lines = lax.all_to_all(spread, ("rows", "cols"), 0, 0)
             if j:
-                latent = exchange(call_second_axis(spots, tables, lines, partial, n_rows, n_cols), "cols")
+                latent = list(call_second_axis(spots, tables, lines, partial, n_rows, n_cols))
             else:
                 partial = (call_second_axis(spots, tables, lines, partial, n_rows, n_cols),)
 
-        residuals, sums = [], 0.0
-        for k in range(n_cols):
-            residual, part = call_cell(place, coefficients, latent[k], covariates, counts, land_mask, k)
-            residuals.append(residual)
-            sums = sums + part
-        back = exchange(residuals, "cols")
+        residuals, sums, own, far = [None] * n_cols, 0.0, latent[0], n_cols - 1
+        arrived = {0: own, far: send(latent[far], "cols", n_cols, far)}
+        for k in range(1, far):
+            if k > 1:
+                arrived[far], latent[k] = lax.optimization_barrier((arrived[far], latent[k]))
+            arrived[k] = send(latent[k], "cols", n_cols, k)
+        before = None
+        for k in (far, *range(1, far), 0):
+            values = arrived[k]
+            if before is not None:
+                values, _ = lax.optimization_barrier((values, residuals[before]))
+            residuals[k], part = call_cell(place, coefficients, values, covariates, counts, land_mask, k)
+            sums, before = sums + part, k
+        back = [residuals[0]] + [send(residuals[k], "cols", n_cols, k) for k in range(1, n_cols)]
         sums = jnp.sum(sums, axis=(1, 2))
         own_loss = sums[n_cov] + 0.5 * squares
         own = jnp.concatenate([sums[:n_cov], jnp.broadcast_to(own_loss, (LANES - n_cov,))])
-        row_steps, col_steps = n_rows.bit_length() - 1, n_cols.bit_length() - 1
-        totals = doubled(doubled(own, "rows", n_rows, range(row_steps)), "cols", n_cols, range(col_steps))
+        totals = sum_over(sum_over(own, "rows", n_rows), "cols", n_cols)
         spread = call_second_axis_back(spots, tables, back, n_rows, n_cols)
         blocks = []
         for j in range(2):

time: 425 us -> 425 us (level)
  starting transfers between devices: 67.3 us -> 71.6 us
    ppermute x39 -> x44, starting transfers between devices: 42.8 us -> 54.9 us  [send(): return lax.ppermute(values, axis, [(i, i ^ k) for i in range(count)])]
    all_to_all x2, starting transfers between devices: 15.2 us -> 7.34 us  [run(): lines = lax.all_to_all(spread[j], ('rows', 'cols'), 0, 0).reshape(NG, LANES)]
    ppermute x39 -> x44, waiting for transfers between devices: 153 us -> 150 us  [send(): return lax.ppermute(values, axis, [(i, i ^ k) for i in range(count)])]
  transfers between devices with their start and end apart: 43 -> 48, of which waited for: 20 -> 19; matrix products, arithmetic and copies ran while one was open for 1% -> 1% of each run, Pallas kernels for 13% -> 12%
where the time goes in v3:
time: 425 us; the launch traced here: 424 us
  waiting for transfers between devices  230 us (54%)
  Pallas kernels  90.5 us (21%)
  starting transfers between devices  71.6 us (17%)
  local copies, waits for them, and re-layouts  22 us (5%)
  between operations  6.19 us (1%)
    ppermute x44, waiting for transfers between devices, send(): return lax.ppermute(values, axis, [(i, i ^ k) for i in range(count)])  150 us
    all_to_all x2, waiting for transfers between devices, run(): lines = lax.all_to_all(spread, ('rows', 'cols'), 0, 0)  56.9 us
    ppermute x44, starting transfers between devices, send(): return lax.ppermute(values, axis, [(i, i ^ k) for i in range(count)])  54.9 us
    pallas_call x4, Pallas kernels, call_first_axis(): pl.pallas_call(kernel, name='first_axis', out_shape=[f32(NG // n_out, LAN...  31.2 us
    all_to_all x2, waiting for transfers between devices, run(): lines = lax.all_to_all(spread[j], ('rows', 'cols'), 0, 0).reshape(NG, LANES)  22.8 us
    unnamed x80, local copies, waits for them, and re-layouts  20.7 us
    pallas_call x4, Pallas kernels, call_cell(): pl.pallas_call(kernel, name='cell', out_shape=[f32(width, LANES), f32(n_c...  20.1 us
    pallas_call x1, Pallas kernels, call_second_axis_back(): pl.pallas_call(kernel, name='second_axis_back', out_shape=[f32(n_rows * n...  12.9 us
  transfers between devices with their start and end apart: 48, of which 19 were waited for; matrix products, arithmetic and copies ran while one was open for 1% of the time, Pallas kernels for 12%

profile of v3, /device:TPU:0, one launch (start us, length us, event | category | flops | bytes accessed | tf_op | source)
XLA Modules:
  0.0 423.9 jit_solution(16973057846236886165)
XLA Ops:
  24.2 9.9 %collective-permute-done.11.refs_8_ = f32[512,128]{1,0:T(8,128)S(1)} collective-permute-done((f32[512,128]{1,0:T(8,128)}, f32[512,128]{1,0:T(8,128)S(1)}, u32[]{:S(2)}, u32[]{:S(2)}) %collective-permute-start.11) | collective-permute-done | bytes 262176 | tf_op jit(solution)/shard_map/ppermute | solution.py:504
  40.9 7.2 %first_axis.5 = f32[4096,128]{1,0:T(8,128)S(1)} custom-call(s32[2]{0:T(128)S(1)} %pad_add_fusion.1.refs_0_, bf16[256,1536]{1,0:T(8,128)(2,1)S(1)} %copy-done.9, f32[4,256,128]{2,1,0:T(8,128)S(1)} %broadcast_in_dim.2.refs_2_, f32[512,128]{1,0:T(8,128)S(1)} %copy-done.16, f32[512,128]{1,0:T(8,128)S(1)} %collective-permute-done.refs_4_, ...), custom_call_target="tpu_custom_call" | custom-call | flops 49999998976 | bytes 4194304 | tf_op jit(solution)/shard_map/first_axis/pallas_call | solution.py:402
  57.0 17.5 %collective-permute-done.5.refs_8_ = f32[512,128]{1,0:T(8,128)} collective-permute-done((f32[512,128]{1,0:T(8,128)}, f32[512,128]{1,0:T(8,128)}, u32[]{:S(2)}, u32[]{:S(2)}) %collective-permute-start.5) | collective-permute-done | bytes 262176 | tf_op jit(solution)/shard_map/ppermute | solution.py:504
  76.6 7.8 %first_axis.4 = f32[4096,128]{1,0:T(8,128)S(1)} custom-call(s32[2]{0:T(128)S(1)} %pad_add_fusion.1.refs_0_, bf16[256,1536]{1,0:T(8,128)(2,1)S(1)} %copy-done.10, f32[4,256,128]{2,1,0:T(8,128)S(1)} %broadcast_in_dim.2.refs_2_, f32[512,128]{1,0:T(8,128)S(1)} %copy-done.15, f32[512,128]{1,0:T(8,128)S(1)} %collective-permute-done.1.refs_4_, ...), custom_call_target="tpu_custom_call" | custom-call | flops 49999998976 | bytes 4194304 | tf_op jit(solution)/shard_map/first_axis/pallas_call | solution.py:402
  85.7 16.1 %all-to-all-done.1.refs_3_ = f32[32,128,128]{2,1,0:T(8,128)S(1)} async-done(((f32[32,128,128]{2,1,0:T(8,128)}), f32[32,128,128]{2,1,0:T(8,128)S(1)}, u32[]{:S(2)}, u32[]{:S(2)}) %all-to-all-start.1) | async-done | bytes 2097184 | tf_op jit(solution)/shard_map/all_to_all | solution.py:541
  112.1 40.9 %all-to-all-done.refs_3_ = f32[32,128,128]{2,1,0:T(8,128)} async-done(((f32[32,128,128]{2,1,0:T(8,128)}), f32[32,128,128]{2,1,0:T(8,128)}, u32[]{:S(2)}, u32[]{:S(2)}) %all-to-all-start) | async-done | bytes 2097184 | tf_op jit(solution)/shard_map/all_to_all | solution.py:541
  154.6 6.1 %second_axis.3 = (f32[1024,128]{1,0:T(8,128)S(1)}, f32[1024,128]{1,0:T(8,128)S(1)}, f32[1024,128]{1,0:T(8,128)S(1)}, f32[1024,128]{1,0:T(8,128)S(1)}) custom-call(s32[2]{0:T(128)S(1)} %pad_add_fusion.1.refs_0_, bf16[256,1536]{1,0:T(8,128)(2,1)S(1)} %copy-done.11, f32[4,256,128]{2,1,0:T(8,128)S(1)} %broadcast_in_dim.2.refs_2_, ...), custom_call_target="tpu_custom_call" | custom-call | flops 49999998976 | bytes 6291456 | tf_op jit(solution)/shard_map/second_axis/pallas_call | solution.py:421
  164.5 12.4 %collective-permute-done.14.refs_2_ = f32[1024,128]{1,0:T(8,128)S(1)} collective-permute-done((f32[1024,128]{1,0:T(8,128)S(1)}, f32[1024,128]{1,0:T(8,128)S(1)}, u32[]{:S(2)}, u32[]{:S(2)}) %collective-permute-start.14) | collective-permute-done | bytes 524320 | tf_op jit(solution)/shard_map/ppermute | solution.py:504
  176.9 12.0 %collective-permute-start.15 = (f32[1024,128]{1,0:T(8,128)S(1)}, f32[1024,128]{1,0:T(8,128)S(1)}, u32[]{:S(2)}, u32[]{:S(2)}) collective-permute-start(f32[1024,128]{1,0:T(8,128)S(1)} %get-tuple-element.105), channel_id=1, source_target_pairs={{0,2},{1,3},{2,0},{3,1},{4,6},{5,7},{6,4},{7,5},{8,10},{9,11},{10,... | collective-permute-start | bytes 1572872 | tf_op jit(solution)/shard_map/ppermute | solution.py:504
  188.9 5.8 %copy-done.6 = bf16[16,512,1024]{2,1,0:T(8,128)(2,1)S(1)} copy-done((bf16[16,512,1024]{2,1,0:T(8,128)(2,1)S(1)}, bf16[16,512,1024]{2,1,0:T(8,128)(2,1)}, u32[]{:S(2)}) %copy-start.6) | copy-done | bytes 16777240
  201.6 5.0 %cell.5 = (f32[1024,128]{1,0:T(8,128)S(1)}, f32[17,8,128]{2,1,0:T(8,128)S(1)}) custom-call(s32[4]{0:T(128)S(1)} %copy-done.5, f32[16]{0:T(128)S(1)} %copy-done.3, f32[1024,128]{1,0:T(8,128)S(1)} %collective-permute-done.16.refs_2_, bf16[16,512,1024]{2,1,0:T(8,128)(2,1)S(1)} %copy-done.6, s32[512,1024]{1,0:T(8,128)S(1)} %copy-done.7, s32[512,1024]{1,0:T(8,128)S(1)} %copy-done.8), custom_call_target="tpu_custom_call" | custom-call | flops 20000000000 | bytes 6291456 | tf_op jit(solution)/shard_map/cell/pallas_call | solution.py:461
  206.7 17.5 %collective-permute-done.15.refs_2_ = f32[1024,128]{1,0:T(8,128)S(1)} collective-permute-done((f32[1024,128]{1,0:T(8,128)S(1)}, f32[1024,128]{1,0:T(8,128)S(1)}, u32[]{:S(2)}, u32[]{:S(2)}) %collective-permute-start.15) | collective-permute-done | bytes 524320 | tf_op jit(solution)/shard_map/ppermute | solution.py:504
  224.2 5.0 %cell.6 = (f32[1024,128]{1,0:T(8,128)S(1)}, f32[17,8,128]{2,1,0:T(8,128)S(1)}) custom-call(s32[4]{0:T(128)S(1)} %copy-done.5, f32[16]{0:T(128)S(1)} %copy-done.3, f32[1024,128]{1,0:T(8,128)S(1)} %collective-permute-done.15.refs_2_, bf16[16,512,1024]{2,1,0:T(8,128)(2,1)S(1)} %copy-done.6, s32[512,1024]{1,0:T(8,128)S(1)} %copy-done.7, s32[512,1024]{1,0:T(8,128)S(1)} %copy-done.8), custom_call_target="tpu_custom_call" | custom-call | flops 20000000000 | bytes 6291456 | tf_op jit(solution)/shard_map/cell/pallas_call | solution.py:461
  229.3 5.0 %cell.7 = (f32[1024,128]{1,0:T(8,128)S(1)}, f32[17,8,128]{2,1,0:T(8,128)S(1)}) custom-call(s32[4]{0:T(128)S(1)} %copy-done.5, f32[16]{0:T(128)S(1)} %copy-done.3, f32[1024,128]{1,0:T(8,128)S(1)} %get-tuple-element.113.refs_2_, bf16[16,512,1024]{2,1,0:T(8,128)(2,1)S(1)} %copy-done.6, s32[512,1024]{1,0:T(8,128)S(1)} %copy-done.7, s32[512,1024]{1,0:T(8,128)S(1)} %copy-done.8), custom_call_target="tpu_custom_call" | custom-call | flops 20000000000 | bytes 6291456 | tf_op jit(solution)/shard_map/cell/pallas_call | solution.py:461
  234.4 22.5 %collective-permute-done.18.refs_5_ = f32[1024,128]{1,0:T(8,128)S(1)} collective-permute-done((f32[1024,128]{1,0:T(8,128)S(1)}, f32[1024,128]{1,0:T(8,128)S(1)}, u32[]{:S(2)}, u32[]{:S(2)}) %collective-permute-start.18) | collective-permute-done | bytes 524320 | tf_op jit(solution)/shard_map/ppermute | solution.py:504
  256.9 12.9 %second_axis_back.1 = (f32[32,128,128]{2,1,0:T(8,128)S(1)}, f32[32,128,128]{2,1,0:T(8,128)}) custom-call(s32[2]{0:T(128)S(1)} %pad_add_fusion.1.refs_0_, bf16[256,1536]{1,0:T(8,128)(2,1)S(1)} %copy-done.12, f32[4,256,128]{2,1,0:T(8,128)S(1)} %broadcast_in_dim.2.refs_2_, f32[1024,128]{1,0:T(8,128)S(1)} %get-tuple-element.114.refs_3_, ...), custom_call_target="tpu_custom_call" | custom-call | flops 49999998976 | bytes 6291456 | tf_op jit(solution)/shard_map/second_axis_back/pallas_call | solution.py:437
  285.0 6.3 %collective-permute-done.25 = f32[128]{0:T(128)S(1)} collective-permute-done((f32[128]{0:T(128)S(1)}, f32[128]{0:T(128)S(1)}, u32[]{:S(2)}, u32[]{:S(2)}) %collective-permute-start.25) | collective-permute-done | bytes 544 | tf_op jit(solution)/shard_map/ppermute | solution.py:504
  297.9 26.3 %collective-permute-done.28 = f32[128]{0:T(128)S(1)} collective-permute-done((f32[128]{0:T(128)S(1)}, f32[128]{0:T(128)S(1)}, u32[]{:S(2)}, u32[]{:S(2)}) %collective-permute-start.28) | collective-permute-done | bytes 544 | tf_op jit(solution)/shard_map/ppermute | solution.py:504
  329.1 8.0 %first_axis.6 = (f32[512,128]{1,0:T(8,128)S(1)}, f32[512,128]{1,0:T(8,128)S(1)}, f32[512,128]{1,0:T(8,128)S(1)}, f32[512,128]{1,0:T(8,128)}, f32[512,128]{1,0:T(...) custom-call(s32[2]{0:T(128)S(1)} %pad_add_fusion.1.refs_0_, ...), custom_call_target="tpu_custom_call" | custom-call | flops 49999998976 | bytes 4194304 | tf_op jit(solution)/shard_map/first_axis/pallas_call | solution.py:402
  343.7 8.0 %collective-permute-done.31.refs_6_ = f32[512,128]{1,0:T(8,128)S(1)} collective-permute-done((f32[512,128]{1,0:T(8,128)S(1)}, f32[512,128]{1,0:T(8,128)S(1)}, u32[]{:S(2)}, u32[]{:S(2)}) %collective-permute-start.31) | collective-permute-done | bytes 262176 | tf_op jit(solution)/shard_map/ppermute | solution.py:504
  352.4 22.8 %all-to-all-done.2 = f32[32,128,128]{2,1,0:T(8,128)} async-done(((f32[32,128,128]{2,1,0:T(8,128)}), f32[32,128,128]{2,1,0:T(8,128)}, u32[]{:S(2)}, u32[]{:S(2)}) %all-to-all-start.2) | async-done | bytes 2097184 | tf_op jit(solution)/shard_map/all_to_all | solution.py:568
  379.7 8.2 %first_axis.7 = (f32[512,128]{1,0:T(8,128)S(1)}, f32[512,128]{1,0:T(8,128)S(1)}, f32[512,128]{1,0:T(8,128)S(1)}, f32[512,128]{1,0:T(8,128)S(1)}, f32[512,128]{1,...) custom-call(s32[2]{0:T(128)S(1)} %pad_add_fusion.1.refs_0_, ...), custom_call_target="tpu_custom_call" | custom-call | flops 49999998976 | bytes 4194304 | tf_op jit(solution)/shard_map/first_axis/pallas_call | solution.py:402
  402.4 13.1 %collective-permute-done.41.refs_17_ = f32[512,128]{1,0:T(8,128)S(1)} collective-permute-done((f32[512,128]{1,0:T(8,128)S(1)}, f32[512,128]{1,0:T(8,128)S(1)}, u32[]{:S(2)}, u32[]{:S(2)}) %collective-permute-start.41) | collective-permute-done | bytes 262176 | tf_op jit(solution)/shard_map/ppermute | solution.py:504
  416.4 6.3 %final.1 = (f32[512,1024]{1,0:T(8,128)}, f32[512,1024]{1,0:T(8,128)}) custom-call(s32[4]{0:T(128)} %pad_add_fusion.refs_0_, f32[2]{0:T(128)} %refs_1_.20, f32[512,1024]{1,0:T(8,128)} %refs_2_.5, f32[512,1024]{1,0:T(8,128)} %refs_3_.13, f32[512,128]{1,0:T(8,128)} %copy-done.17, f32[512,128]{1,0:T(8,128)} %copy-done.24, f32[512,128]{1,0:T(8,128)} %copy-done.25, ...), custom_call_target="tpu_custom_call" | custom-call | flops 4000000000 | bytes 12582912 | tf_op jit(solution)/shard_map/final/pallas_call | solution.py:491
  (178 shorter events, 115.1 us)
Async XLA Ops:
  10.9 23.2 %collective-permute-start.11 = (f32[512,128]{1,0:T(8,128)}, f32[512,128]{1,0:T(8,128)S(1)}, u32[]{:S(2)}, u32[]{:S(2)}) collective-permute-start(f32[512,128]{1,0:T(8,128)} %get-tuple-element.99), channel_id=1, source_target_pairs={{0,20},{4,16},{8,28},{12,24},{16,4},{20,0},{24,12},{28,8},{1,21},{... | collective-permute-start | bytes 786440 | tf_op jit(solution)/shard_map/ppermute | solution.py:504
  36.2 20.8 %collective-permute-start.4 = (f32[512,128]{1,0:T(8,128)}, f32[512,128]{1,0:T(8,128)}, u32[]{:S(2)}, u32[]{:S(2)}) collective-permute-start(f32[512,128]{1,0:T(8,128)} %get-tuple-element.91), channel_id=1, source_target_pairs={{0,16},{4,20},{8,24},{12,28},{16,0},{20,4},{24,8},{28,12},{1,17},{... | collective-permute-start | bytes 786440 | tf_op jit(solution)/shard_map/ppermute | solution.py:504
  37.8 36.8 %collective-permute-start.5 = (f32[512,128]{1,0:T(8,128)}, f32[512,128]{1,0:T(8,128)}, u32[]{:S(2)}, u32[]{:S(2)}) collective-permute-start(f32[512,128]{1,0:T(8,128)} %get-tuple-element.92), channel_id=1, source_target_pairs={{0,20},{4,16},{8,28},{12,24},{16,4},{20,0},{24,12},{28,8},{1,21},{... | collective-permute-start | bytes 786440 | tf_op jit(solution)/shard_map/ppermute | solution.py:504
  37.8 36.8 %collective-permute-start.6 = (f32[512,128]{1,0:T(8,128)}, f32[512,128]{1,0:T(8,128)}, u32[]{:S(2)}, u32[]{:S(2)}) collective-permute-start(f32[512,128]{1,0:T(8,128)} %get-tuple-element.93), channel_id=1, source_target_pairs={{0,24},{4,28},{8,16},{12,20},{16,8},{20,12},{24,0},{28,4},{1,25},{... | collective-permute-start | bytes 786440 | tf_op jit(solution)/shard_map/ppermute | solution.py:504
  39.0 35.6 %collective-permute-start.7 = (f32[512,128]{1,0:T(8,128)}, f32[512,128]{1,0:T(8,128)}, u32[]{:S(2)}, u32[]{:S(2)}) collective-permute-start(f32[512,128]{1,0:T(8,128)} %get-tuple-element.94), channel_id=1, source_target_pairs={{0,28},{4,24},{8,20},{12,16},{16,12},{20,8},{24,4},{28,0},{1,29},{... | collective-permute-start | bytes 786440 | tf_op jit(solution)/shard_map/ppermute | solution.py:504
  49.4 52.4 %all-to-all-start.1 = ((f32[32,128,128]{2,1,0:T(8,128)}), f32[32,128,128]{2,1,0:T(8,128)S(1)}, u32[]{:S(2)}, u32[]{:S(2)}) async-start(f32[32,128,128]{2,1,0:T(8,128)} %bitcast.12), calls=%async_computation.1 | async-start | bytes 4194304 | tf_op jit(solution)/shard_map/all_to_all | solution.py:541
  101.8 51.2 %all-to-all-start = ((f32[32,128,128]{2,1,0:T(8,128)}), f32[32,128,128]{2,1,0:T(8,128)}, u32[]{:S(2)}, u32[]{:S(2)}) async-start(f32[32,128,128]{2,1,0:T(8,128)} %bitcast.13), calls=%async_computation | async-start | bytes 4194304 | tf_op jit(solution)/shard_map/all_to_all | solution.py:541
  164.1 37.5 %collective-permute-start.16 = (f32[1024,128]{1,0:T(8,128)S(1)}, f32[1024,128]{1,0:T(8,128)S(1)}, u32[]{:S(2)}, u32[]{:S(2)}) collective-permute-start(f32[1024,128]{1,0:T(8,128)S(1)} %get-tuple-element.106), channel_id=1, source_target_pairs={{0,1},{1,0},{2,3},{3,2},{4,5},{5,4},{6,7},{7,6},{8,9},{9,8},{10,11... | collective-permute-start | bytes 1572872 | tf_op jit(solution)/shard_map/ppermute | solution.py:504
  176.9 47.2 %collective-permute-start.15 = (f32[1024,128]{1,0:T(8,128)S(1)}, f32[1024,128]{1,0:T(8,128)S(1)}, u32[]{:S(2)}, u32[]{:S(2)}) collective-permute-start(f32[1024,128]{1,0:T(8,128)S(1)} %get-tuple-element.105), channel_id=1, source_target_pairs={{0,2},{1,3},{2,0},{3,1},{4,6},{5,7},{6,4},{7,5},{8,10},{9,11},{10,... | collective-permute-start | bytes 1572872 | tf_op jit(solution)/shard_map/ppermute | solution.py:504
  199.7 34.7 %collective-permute-start.19 = (f32[1024,128]{1,0:T(8,128)S(1)}, f32[1024,128]{1,0:T(8,128)S(1)}, u32[]{:S(2)}, u32[]{:S(2)}) collective-permute-start(f32[1024,128]{1,0:T(8,128)S(1)} %get-tuple-element.108), channel_id=1, source_target_pairs={{0,3},{1,2},{2,1},{3,0},{4,7},{5,6},{6,5},{7,4},{8,11},{9,10},{10,... | collective-permute-start | bytes 1572872 | tf_op jit(solution)/shard_map/ppermute | solution.py:504
  206.6 27.8 %collective-permute-start.17 = (f32[1024,128]{1,0:T(8,128)S(1)}, f32[1024,128]{1,0:T(8,128)S(1)}, u32[]{:S(2)}, u32[]{:S(2)}) collective-permute-start(f32[1024,128]{1,0:T(8,128)S(1)} %get-tuple-element.110), channel_id=1, source_target_pairs={{0,1},{1,0},{2,3},{3,2},{4,5},{5,4},{6,7},{7,6},{8,9},{9,8},{10,11... | collective-permute-start | bytes 1572872 | tf_op jit(solution)/shard_map/ppermute | solution.py:504
  229.2 27.7 %collective-permute-start.18 = (f32[1024,128]{1,0:T(8,128)S(1)}, f32[1024,128]{1,0:T(8,128)S(1)}, u32[]{:S(2)}, u32[]{:S(2)}) collective-permute-start(f32[1024,128]{1,0:T(8,128)S(1)} %get-tuple-element.112), channel_id=1, source_target_pairs={{0,2},{1,3},{2,0},{3,1},{4,6},{5,7},{6,4},{7,5},{8,10},{9,11},{10,... | collective-permute-start | bytes 1572872 | tf_op jit(solution)/shard_map/ppermute | solution.py:504
  271.2 53.1 %all-to-all-start.3 = ((f32[32,128,128]{2,1,0:T(8,128)}), f32[32,128,128]{2,1,0:T(8,128)S(1)}, u32[]{:S(2)}, u32[]{:S(2)}) async-start(f32[32,128,128]{2,1,0:T(8,128)} %copy-done), calls=%async_computation.3 | async-start | bytes 4194304 | tf_op jit(solution)/shard_map/all_to_all | solution.py:568
  294.3 29.9 %collective-permute-start.28 = (f32[128]{0:T(128)S(1)}, f32[128]{0:T(128)S(1)}, u32[]{:S(2)}, u32[]{:S(2)}) collective-permute-start(f32[128]{0:T(128)S(1)} %add_add_fusion.1), channel_id=1, source_target_pairs={{0,2},{1,3},{2,0},{3,1},{4,6},{5,7},{6,4},{7,5},{8,10},{9,11},{10,... | collective-permute-start | bytes 1544 | tf_op jit(solution)/shard_map/ppermute | solution.py:504
  294.4 29.8 %collective-permute-start.29 = (f32[128]{0:T(128)S(1)}, f32[128]{0:T(128)S(1)}, u32[]{:S(2)}, u32[]{:S(2)}) collective-permute-start(f32[128]{0:T(128)S(1)} %add_add_fusion.1), channel_id=1, source_target_pairs={{0,3},{1,2},{2,1},{3,0},{4,7},{5,6},{6,5},{7,4},{8,11},{9,10},{10,... | collective-permute-start | bytes 1544 | tf_op jit(solution)/shard_map/ppermute | solution.py:504
  296.9 27.3 %collective-permute-start.27 = (f32[128]{0:T(128)S(1)}, f32[128]{0:T(128)S(1)}, u32[]{:S(2)}, u32[]{:S(2)}) collective-permute-start(f32[128]{0:T(128)S(1)} %add_add_fusion.1), channel_id=1, source_target_pairs={{0,1},{1,0},{2,3},{3,2},{4,5},{5,4},{6,7},{7,6},{8,9},{9,8},{10,11... | collective-permute-start | bytes 1544 | tf_op jit(solution)/shard_map/ppermute | solution.py:504
  324.2 51.0 %all-to-all-start.2 = ((f32[32,128,128]{2,1,0:T(8,128)}), f32[32,128,128]{2,1,0:T(8,128)}, u32[]{:S(2)}, u32[]{:S(2)}) async-start(f32[32,128,128]{2,1,0:T(8,128)} %get-tuple-element.115), calls=%async_computation.2 | async-start | bytes 4194304 | tf_op jit(solution)/shard_map/all_to_all | solution.py:568
  339.3 35.9 %collective-permute-start.32 = (f32[512,128]{1,0:T(8,128)}, f32[512,128]{1,0:T(8,128)S(1)}, u32[]{:S(2)}, u32[]{:S(2)}) collective-permute-start(f32[512,128]{1,0:T(8,128)} %get-tuple-element.127), channel_id=1, source_target_pairs={{0,12},{4,8},{8,4},{12,0},{16,28},{20,24},{24,20},{28,16},{1,13},{... | collective-permute-start | bytes 786440 | tf_op jit(solution)/shard_map/ppermute | solution.py:504
  339.6 35.6 %collective-permute-start.33 = (f32[512,128]{1,0:T(8,128)}, f32[512,128]{1,0:T(8,128)S(1)}, u32[]{:S(2)}, u32[]{:S(2)}) collective-permute-start(f32[512,128]{1,0:T(8,128)} %get-tuple-element.128), channel_id=1, source_target_pairs={{0,16},{4,20},{8,24},{12,28},{16,0},{20,4},{24,8},{28,12},{1,17},{... | collective-permute-start | bytes 786440 | tf_op jit(solution)/shard_map/ppermute | solution.py:504
  341.0 34.3 %collective-permute-start.34 = (f32[512,128]{1,0:T(8,128)S(1)}, f32[512,128]{1,0:T(8,128)S(1)}, u32[]{:S(2)}, u32[]{:S(2)}) collective-permute-start(f32[512,128]{1,0:T(8,128)S(1)} %get-tuple-element.129), channel_id=1, source_target_pairs={{0,20},{4,16},{8,28},{12,24},{16,4},{20,0},{24,12},{28,8},{1,21},{... | collective-permute-start | bytes 786440 | tf_op jit(solution)/shard_map/ppermute | solution.py:504
  341.2 34.0 %collective-permute-start.35 = (f32[512,128]{1,0:T(8,128)S(1)}, f32[512,128]{1,0:T(8,128)S(1)}, u32[]{:S(2)}, u32[]{:S(2)}) collective-permute-start(f32[512,128]{1,0:T(8,128)S(1)} %get-tuple-element.130), channel_id=1, source_target_pairs={{0,24},{4,28},{8,16},{12,20},{16,8},{20,12},{24,0},{28,4},{1,25},{... | collective-permute-start | bytes 786440 | tf_op jit(solution)/shard_map/ppermute | solution.py:504
  352.4 25.4 %collective-permute-start.36 = (f32[512,128]{1,0:T(8,128)S(1)}, f32[512,128]{1,0:T(8,128)S(1)}, u32[]{:S(2)}, u32[]{:S(2)}) collective-permute-start(f32[512,128]{1,0:T(8,128)S(1)} %get-tuple-element.131), channel_id=1, source_target_pairs={{0,28},{4,24},{8,20},{12,16},{16,12},{20,8},{24,4},{28,0},{1,29},{... | collective-permute-start | bytes 786440 | tf_op jit(solution)/shard_map/ppermute | solution.py:504
  391.2 24.3 %collective-permute-start.41 = (f32[512,128]{1,0:T(8,128)S(1)}, f32[512,128]{1,0:T(8,128)S(1)}, u32[]{:S(2)}, u32[]{:S(2)}) collective-permute-start(f32[512,128]{1,0:T(8,128)S(1)} %get-tuple-element.146), channel_id=1, source_target_pairs={{0,20},{4,16},{8,28},{12,24},{16,4},{20,0},{24,12},{28,8},{1,21},{... | collective-permute-start | bytes 786440 | tf_op jit(solution)/shard_map/ppermute | solution.py:504
  392.3 23.2 %collective-permute-start.42 = (f32[512,128]{1,0:T(8,128)S(1)}, f32[512,128]{1,0:T(8,128)S(1)}, u32[]{:S(2)}, u32[]{:S(2)}) collective-permute-start(f32[512,128]{1,0:T(8,128)S(1)} %get-tuple-element.147), channel_id=1, source_target_pairs={{0,24},{4,28},{8,16},{12,20},{16,8},{20,12},{24,0},{28,4},{1,25},{... | collective-permute-start | bytes 786440 | tf_op jit(solution)/shard_map/ppermute | solution.py:504
  (64 other events, 813.4 us)

commit v4 on v3

--- a/solution.py
+++ b/solution.py
@@ -340,7 +340,7 @@
     low = lane < HALF
     step = 64
     first_row = first_row + pl.program_id(0) * height
-    for k in range(count):
+    for at, k in enumerate(far_first(count)):
         start = pl.multiple_of(jnp.bitwise_xor(me, k) * LANES, LANES)
         for row in range(0, height, step):
             rows = pl.ds(row, step)
@@ -348,7 +348,7 @@
             spec = spectrum_of(hyper, first_row + row, first_col + start, (step, LANES))
             inverse = 1.0 / (1.0 + spec * spec)
             spec = spec * (1.0 / NG)
-            one, two = blocks[k][rows, :], blocks[count + k][rows, :]
+            one, two = blocks[at][rows, :], blocks[count + at][rows, :]
             adjoint_real = jnp.where(low, one, pltpu.roll(two, HALF, 1))
             adjoint_imag = jnp.where(low, pltpu.roll(one, HALF, 1), two)
             step_real_ref[rows, lanes] = (spec * adjoint_real + real_ref[rows, lanes]) * inverse
@@ -369,6 +369,10 @@
 
 def cost(flops, nbytes):
     return pl.CostEstimate(flops=int(flops), bytes_accessed=int(nbytes), transcendentals=0)
+
+
+def far_first(count):
+    return sorted(range(count), key=lambda k: (-(k >> 1).bit_count(), -(k & 1), k))
 
 
 def call_scale(place, hyper, real, imag, n_rows, j):
@@ -486,6 +490,7 @@
     def kernel(*refs):
         final_kernel(n_rows, *refs)
 
+    blocks = [blocks[j * n_rows + k] for j in range(2) for k in far_first(n_rows)]
     wide = pl.BlockSpec((tile, width), lambda i: (i, 0))
     narrow = pl.BlockSpec((tile, LANES), lambda i: (i, 0))
     return pl.pallas_call(
@@ -544,20 +549,13 @@
             else:
                 partial = (call_second_axis(spots, tables, lines, partial, n_rows, n_cols),)
 
-        residuals, sums, own, far = [None] * n_cols, 0.0, latent[0], n_cols - 1
-        arrived = {0: own, far: send(latent[far], "cols", n_cols, far)}
-        for k in range(1, far):
-            if k > 1:
-                arrived[far], latent[k] = lax.optimization_barrier((arrived[far], latent[k]))
-            arrived[k] = send(latent[k], "cols", n_cols, k)
-        before = None
-        for k in (far, *range(1, far), 0):
-            values = arrived[k]
-            if before is not None:
-                values, _ = lax.optimization_barrier((values, residuals[before]))
-            residuals[k], part = call_cell(place, coefficients, values, covariates, counts, land_mask, k)
-            sums, before = sums + part, k
-        back = [residuals[0]] + [send(residuals[k], "cols", n_cols, k) for k in range(1, n_cols)]
+        latent = exchange(latent, "cols")
+        residuals, sums = [], 0.0
+        for k in range(n_cols):
+            residual, part = call_cell(place, coefficients, latent[k], covariates, counts, land_mask, k)
+            residuals.append(residual)
+            sums = sums + part
+        back = exchange(residuals, "cols")
         sums = jnp.sum(sums, axis=(1, 2))
         own_loss = sums[n_cov] + 0.5 * squares
         own = jnp.concatenate([sums[:n_cov], jnp.broadcast_to(own_loss, (LANES - n_cov,))])

time: 425 us -> 423 us (level)
    ppermute x44, starting transfers between devices: 54.9 us -> 45.3 us  [send(): return lax.ppermute(values, axis, [(i, i ^ k) for i in range(count)])]
    all_to_all x2, starting transfers between devices: 7.34 us -> 15.2 us  [run(): lines = lax.all_to_all(spread[j], ('rows', 'cols'), 0, 0).reshape(NG, LANES)]
  transfers between devices with their start and end apart: 48 -> 48, of which waited for: 19 -> 21; matrix products, arithmetic and copies ran while one was open for 1% -> 1% of each run, Pallas kernels for 12% -> 12%
where the time goes in v4:
time: 423 us; the launch traced here: 422 us
  waiting for transfers between devices  230 us (54%)
  Pallas kernels  90.5 us (21%)
  starting transfers between devices  69.8 us (17%)
  local copies, waits for them, and re-layouts  22 us (5%)
  between operations  6.2 us (1%)
    ppermute x44, waiting for transfers between devices, send(): return lax.ppermute(values, axis, [(i, i ^ k) for i in range(count)])  150 us
    all_to_all x2, waiting for transfers between devices, run(): lines = lax.all_to_all(spread, ('rows', 'cols'), 0, 0)  56.9 us
    ppermute x44, starting transfers between devices, send(): return lax.ppermute(values, axis, [(i, i ^ k) for i in range(count)])  45.3 us
    pallas_call x4, Pallas kernels, call_first_axis(): pl.pallas_call(kernel, name='first_axis', out_shape=[f32(NG // n_out, LAN...  31.2 us
    all_to_all x2, waiting for transfers between devices, run(): lines = lax.all_to_all(spread[j], ('rows', 'cols'), 0, 0).reshape(NG, LANES)  22.8 us
    unnamed x80, local copies, waits for them, and re-layouts  20.6 us
    pallas_call x4, Pallas kernels, call_cell(): pl.pallas_call(kernel, name='cell', out_shape=[f32(width, LANES), f32(n_c...  20.1 us
    all_to_all x2, starting transfers between devices, run(): lines = lax.all_to_all(spread[j], ('rows', 'cols'), 0, 0).reshape(NG, LANES)  15.2 us
  transfers between devices with their start and end apart: 48, of which 21 were waited for; matrix products, arithmetic and copies ran while one was open for 1% of the time, Pallas kernels for 12%

profile of v4, /device:TPU:0, one launch (start us, length us, event | category | flops | bytes accessed | tf_op | source)
XLA Modules:
  0.0 421.8 jit_solution(3029521750229036458)
XLA Ops:
  24.2 9.9 %collective-permute-done.11.refs_8_ = f32[512,128]{1,0:T(8,128)S(1)} collective-permute-done((f32[512,128]{1,0:T(8,128)}, f32[512,128]{1,0:T(8,128)S(1)}, u32[]{:S(2)}, u32[]{:S(2)}) %collective-permute-start.11) | collective-permute-done | bytes 262176 | tf_op jit(solution)/shard_map/ppermute | solution.py:509
  40.9 7.2 %first_axis.5 = f32[4096,128]{1,0:T(8,128)S(1)} custom-call(s32[2]{0:T(128)S(1)} %pad_add_fusion.1.refs_0_, bf16[256,1536]{1,0:T(8,128)(2,1)S(1)} %copy-done.9, f32[4,256,128]{2,1,0:T(8,128)S(1)} %broadcast_in_dim.2.refs_2_, f32[512,128]{1,0:T(8,128)S(1)} %copy-done.16, f32[512,128]{1,0:T(8,128)S(1)} %collective-permute-done.refs_4_, ...), custom_call_target="tpu_custom_call" | custom-call | flops 49999998976 | bytes 4194304 | tf_op jit(solution)/shard_map/first_axis/pallas_call | solution.py:406
  57.0 17.5 %collective-permute-done.5.refs_8_ = f32[512,128]{1,0:T(8,128)} collective-permute-done((f32[512,128]{1,0:T(8,128)}, f32[512,128]{1,0:T(8,128)}, u32[]{:S(2)}, u32[]{:S(2)}) %collective-permute-start.5) | collective-permute-done | bytes 262176 | tf_op jit(solution)/shard_map/ppermute | solution.py:509
  76.6 7.8 %first_axis.4 = f32[4096,128]{1,0:T(8,128)S(1)} custom-call(s32[2]{0:T(128)S(1)} %pad_add_fusion.1.refs_0_, bf16[256,1536]{1,0:T(8,128)(2,1)S(1)} %copy-done.10, f32[4,256,128]{2,1,0:T(8,128)S(1)} %broadcast_in_dim.2.refs_2_, f32[512,128]{1,0:T(8,128)S(1)} %copy-done.15, f32[512,128]{1,0:T(8,128)S(1)} %collective-permute-done.1.refs_4_, ...), custom_call_target="tpu_custom_call" | custom-call | flops 49999998976 | bytes 4194304 | tf_op jit(solution)/shard_map/first_axis/pallas_call | solution.py:406
  85.7 16.1 %all-to-all-done.1.refs_3_ = f32[32,128,128]{2,1,0:T(8,128)S(1)} async-done(((f32[32,128,128]{2,1,0:T(8,128)}), f32[32,128,128]{2,1,0:T(8,128)S(1)}, u32[]{:S(2)}, u32[]{:S(2)}) %all-to-all-start.1) | async-done | bytes 2097184 | tf_op jit(solution)/shard_map/all_to_all | solution.py:546
  112.1 40.9 %all-to-all-done.refs_3_ = f32[32,128,128]{2,1,0:T(8,128)} async-done(((f32[32,128,128]{2,1,0:T(8,128)}), f32[32,128,128]{2,1,0:T(8,128)}, u32[]{:S(2)}, u32[]{:S(2)}) %all-to-all-start) | async-done | bytes 2097184 | tf_op jit(solution)/shard_map/all_to_all | solution.py:546
  154.6 6.1 %second_axis.3 = (f32[1024,128]{1,0:T(8,128)S(1)}, f32[1024,128]{1,0:T(8,128)S(1)}, f32[1024,128]{1,0:T(8,128)S(1)}, f32[1024,128]{1,0:T(8,128)S(1)}) custom-call(s32[2]{0:T(128)S(1)} %pad_add_fusion.1.refs_0_, bf16[256,1536]{1,0:T(8,128)(2,1)S(1)} %copy-done.11, f32[4,256,128]{2,1,0:T(8,128)S(1)} %broadcast_in_dim.2.refs_2_, ...), custom_call_target="tpu_custom_call" | custom-call | flops 49999998976 | bytes 6291456 | tf_op jit(solution)/shard_map/second_axis/pallas_call | solution.py:425
  166.9 19.0 %collective-permute-done.14.refs_2_ = f32[1024,128]{1,0:T(8,128)S(1)} collective-permute-done((f32[1024,128]{1,0:T(8,128)S(1)}, f32[1024,128]{1,0:T(8,128)S(1)}, u32[]{:S(2)}, u32[]{:S(2)}) %collective-permute-start.14) | collective-permute-done | bytes 524320 | tf_op jit(solution)/shard_map/ppermute | solution.py:509
  185.9 5.8 %copy-done.6 = bf16[16,512,1024]{2,1,0:T(8,128)(2,1)S(1)} copy-done((bf16[16,512,1024]{2,1,0:T(8,128)(2,1)S(1)}, bf16[16,512,1024]{2,1,0:T(8,128)(2,1)}, u32[]{:S(2)}) %copy-start.6) | copy-done | bytes 16777240
  196.8 5.9 %collective-permute-done.16.refs_2_ = f32[1024,128]{1,0:T(8,128)S(1)} collective-permute-done((f32[1024,128]{1,0:T(8,128)S(1)}, f32[1024,128]{1,0:T(8,128)S(1)}, u32[]{:S(2)}, u32[]{:S(2)}) %collective-permute-start.16) | collective-permute-done | bytes 524320 | tf_op jit(solution)/shard_map/ppermute | solution.py:509
  202.7 5.0 %cell.6 = (f32[1024,128]{1,0:T(8,128)S(1)}, f32[17,8,128]{2,1,0:T(8,128)S(1)}) custom-call(s32[4]{0:T(128)S(1)} %copy-done.5, f32[16]{0:T(128)S(1)} %copy-done.3, f32[1024,128]{1,0:T(8,128)S(1)} %collective-permute-done.16.refs_2_, bf16[16,512,1024]{2,1,0:T(8,128)(2,1)S(1)} %copy-done.6, s32[512,1024]{1,0:T(8,128)S(1)} %copy-done.7, s32[512,1024]{1,0:T(8,128)S(1)} %copy-done.8), custom_call_target="tpu_custom_call" | custom-call | flops 20000000000 | bytes 6291456 | tf_op jit(solution)/shard_map/cell/pallas_call | solution.py:465
  207.8 5.0 %cell.7 = (f32[1024,128]{1,0:T(8,128)S(1)}, f32[17,8,128]{2,1,0:T(8,128)S(1)}) custom-call(s32[4]{0:T(128)S(1)} %copy-done.5, f32[16]{0:T(128)S(1)} %copy-done.3, f32[1024,128]{1,0:T(8,128)S(1)} %collective-permute-done.18.refs_2_, bf16[16,512,1024]{2,1,0:T(8,128)(2,1)S(1)} %copy-done.6, s32[512,1024]{1,0:T(8,128)S(1)} %copy-done.7, s32[512,1024]{1,0:T(8,128)S(1)} %copy-done.8), custom_call_target="tpu_custom_call" | custom-call | flops 20000000000 | bytes 6291456 | tf_op jit(solution)/shard_map/cell/pallas_call | solution.py:465
  213.5 5.0 %cell.4 = (f32[1024,128]{1,0:T(8,128)S(1)}, f32[17,8,128]{2,1,0:T(8,128)S(1)}) custom-call(s32[4]{0:T(128)S(1)} %copy-done.5, f32[16]{0:T(128)S(1)} %copy-done.3, f32[1024,128]{1,0:T(8,128)S(1)} %get-tuple-element.97.refs_2_, bf16[16,512,1024]{2,1,0:T(8,128)(2,1)S(1)} %copy-done.6, s32[512,1024]{1,0:T(8,128)S(1)} %copy-done.7, s32[512,1024]{1,0:T(8,128)S(1)} %copy-done.8), custom_call_target="tpu_custom_call" | custom-call | flops 20000000000 | bytes 6291456 | tf_op jit(solution)/shard_map/cell/pallas_call | solution.py:465
  218.5 29.1 %collective-permute-done.17.refs_5_ = f32[1024,128]{1,0:T(8,128)S(1)} collective-permute-done((f32[1024,128]{1,0:T(8,128)S(1)}, f32[1024,128]{1,0:T(8,128)S(1)}, u32[]{:S(2)}, u32[]{:S(2)}) %collective-permute-start.17) | collective-permute-done | bytes 524320 | tf_op jit(solution)/shard_map/ppermute | solution.py:509
  247.6 12.9 %second_axis_back.1 = (f32[32,128,128]{2,1,0:T(8,128)S(1)}, f32[32,128,128]{2,1,0:T(8,128)}) custom-call(s32[2]{0:T(128)S(1)} %pad_add_fusion.1.refs_0_, bf16[256,1536]{1,0:T(8,128)(2,1)S(1)} %copy-done.12, f32[4,256,128]{2,1,0:T(8,128)S(1)} %broadcast_in_dim.2.refs_2_, f32[1024,128]{1,0:T(8,128)S(1)} %get-tuple-element.98.refs_3_, ...), custom_call_target="tpu_custom_call" | custom-call | flops 49999998976 | bytes 6291456 | tf_op jit(solution)/shard_map/second_axis_back/pallas_call | solution.py:441
  261.9 11.5 %all-to-all-start.3 = ((f32[32,128,128]{2,1,0:T(8,128)}), f32[32,128,128]{2,1,0:T(8,128)S(1)}, u32[]{:S(2)}, u32[]{:S(2)}) async-start(f32[32,128,128]{2,1,0:T(8,128)} %copy-done), calls=%async_computation.3 | async-start | bytes 4194304 | tf_op jit(solution)/shard_map/all_to_all | solution.py:566
  283.6 6.3 %collective-permute-done.25 = f32[128]{0:T(128)S(1)} collective-permute-done((f32[128]{0:T(128)S(1)}, f32[128]{0:T(128)S(1)}, u32[]{:S(2)}, u32[]{:S(2)}) %collective-permute-start.25) | collective-permute-done | bytes 544 | tf_op jit(solution)/shard_map/ppermute | solution.py:509
  296.5 26.3 %collective-permute-done.28 = f32[128]{0:T(128)S(1)} collective-permute-done((f32[128]{0:T(128)S(1)}, f32[128]{0:T(128)S(1)}, u32[]{:S(2)}, u32[]{:S(2)}) %collective-permute-start.28) | collective-permute-done | bytes 544 | tf_op jit(solution)/shard_map/ppermute | solution.py:509
  327.7 8.0 %first_axis.6 = (f32[512,128]{1,0:T(8,128)S(1)}, f32[512,128]{1,0:T(8,128)S(1)}, f32[512,128]{1,0:T(8,128)S(1)}, f32[512,128]{1,0:T(8,128)}, f32[512,128]{1,0:T(...) custom-call(s32[2]{0:T(128)S(1)} %pad_add_fusion.1.refs_0_, ...), custom_call_target="tpu_custom_call" | custom-call | flops 49999998976 | bytes 4194304 | tf_op jit(solution)/shard_map/first_axis/pallas_call | solution.py:406
  342.3 8.0 %collective-permute-done.31.refs_8_ = f32[512,128]{1,0:T(8,128)S(1)} collective-permute-done((f32[512,128]{1,0:T(8,128)S(1)}, f32[512,128]{1,0:T(8,128)S(1)}, u32[]{:S(2)}, u32[]{:S(2)}) %collective-permute-start.31) | collective-permute-done | bytes 262176 | tf_op jit(solution)/shard_map/ppermute | solution.py:509
  350.9 22.8 %all-to-all-done.2 = f32[32,128,128]{2,1,0:T(8,128)} async-done(((f32[32,128,128]{2,1,0:T(8,128)}), f32[32,128,128]{2,1,0:T(8,128)}, u32[]{:S(2)}, u32[]{:S(2)}) %all-to-all-start.2) | async-done | bytes 2097184 | tf_op jit(solution)/shard_map/all_to_all | solution.py:566
  378.2 8.2 %first_axis.7 = (f32[512,128]{1,0:T(8,128)S(1)}, f32[512,128]{1,0:T(8,128)S(1)}, f32[512,128]{1,0:T(8,128)S(1)}, f32[512,128]{1,0:T(8,128)S(1)}, f32[512,128]{1,...) custom-call(s32[2]{0:T(128)S(1)} %pad_add_fusion.1.refs_0_, ...), custom_call_target="tpu_custom_call" | custom-call | flops 49999998976 | bytes 4194304 | tf_op jit(solution)/shard_map/first_axis/pallas_call | solution.py:406
  397.2 5.5 %collective-permute-done.38.refs_13_ = f32[512,128]{1,0:T(8,128)S(1)} collective-permute-done((f32[512,128]{1,0:T(8,128)S(1)}, f32[512,128]{1,0:T(8,128)S(1)}, u32[]{:S(2)}, u32[]{:S(2)}) %collective-permute-start.38) | collective-permute-done | bytes 262176 | tf_op jit(solution)/shard_map/ppermute | solution.py:509
  414.4 6.4 %final.1 = (f32[512,1024]{1,0:T(8,128)}, f32[512,1024]{1,0:T(8,128)}) custom-call(s32[4]{0:T(128)} %pad_add_fusion.refs_0_, f32[2]{0:T(128)} %refs_1_.20, f32[512,1024]{1,0:T(8,128)} %refs_2_.5, f32[512,1024]{1,0:T(8,128)} %refs_3_.13, f32[512,128]{1,0:T(8,128)} %copy-done.30, f32[512,128]{1,0:T(8,128)} %copy-done.29, f32[512,128]{1,0:T(8,128)} %copy-done.26, ...), custom_call_target="tpu_custom_call" | custom-call | flops 4000000000 | bytes 12582912 | tf_op jit(solution)/shard_map/final/pallas_call | solution.py:496
  (178 shorter events, 119.5 us)
Async XLA Ops:
  10.9 23.2 %collective-permute-start.11 = (f32[512,128]{1,0:T(8,128)}, f32[512,128]{1,0:T(8,128)S(1)}, u32[]{:S(2)}, u32[]{:S(2)}) collective-permute-start(f32[512,128]{1,0:T(8,128)} %get-tuple-element.94), channel_id=1, source_target_pairs={{0,20},{4,16},{8,28},{12,24},{16,4},{20,0},{24,12},{28,8},{1,21},{... | collective-permute-start | bytes 786440 | tf_op jit(solution)/shard_map/ppermute | solution.py:509
  36.2 20.8 %collective-permute-start.4 = (f32[512,128]{1,0:T(8,128)}, f32[512,128]{1,0:T(8,128)}, u32[]{:S(2)}, u32[]{:S(2)}) collective-permute-start(f32[512,128]{1,0:T(8,128)} %get-tuple-element.86), channel_id=1, source_target_pairs={{0,16},{4,20},{8,24},{12,28},{16,0},{20,4},{24,8},{28,12},{1,17},{... | collective-permute-start | bytes 786440 | tf_op jit(solution)/shard_map/ppermute | solution.py:509
  37.8 36.8 %collective-permute-start.5 = (f32[512,128]{1,0:T(8,128)}, f32[512,128]{1,0:T(8,128)}, u32[]{:S(2)}, u32[]{:S(2)}) collective-permute-start(f32[512,128]{1,0:T(8,128)} %get-tuple-element.87), channel_id=1, source_target_pairs={{0,20},{4,16},{8,28},{12,24},{16,4},{20,0},{24,12},{28,8},{1,21},{... | collective-permute-start | bytes 786440 | tf_op jit(solution)/shard_map/ppermute | solution.py:509
  37.8 36.8 %collective-permute-start.6 = (f32[512,128]{1,0:T(8,128)}, f32[512,128]{1,0:T(8,128)}, u32[]{:S(2)}, u32[]{:S(2)}) collective-permute-start(f32[512,128]{1,0:T(8,128)} %get-tuple-element.88), channel_id=1, source_target_pairs={{0,24},{4,28},{8,16},{12,20},{16,8},{20,12},{24,0},{28,4},{1,25},{... | collective-permute-start | bytes 786440 | tf_op jit(solution)/shard_map/ppermute | solution.py:509
  39.0 35.6 %collective-permute-start.7 = (f32[512,128]{1,0:T(8,128)}, f32[512,128]{1,0:T(8,128)}, u32[]{:S(2)}, u32[]{:S(2)}) collective-permute-start(f32[512,128]{1,0:T(8,128)} %get-tuple-element.89), channel_id=1, source_target_pairs={{0,28},{4,24},{8,20},{12,16},{16,12},{20,8},{24,4},{28,0},{1,29},{... | collective-permute-start | bytes 786440 | tf_op jit(solution)/shard_map/ppermute | solution.py:509
  49.4 52.4 %all-to-all-start.1 = ((f32[32,128,128]{2,1,0:T(8,128)}), f32[32,128,128]{2,1,0:T(8,128)S(1)}, u32[]{:S(2)}, u32[]{:S(2)}) async-start(f32[32,128,128]{2,1,0:T(8,128)} %bitcast.12), calls=%async_computation.1 | async-start | bytes 4194304 | tf_op jit(solution)/shard_map/all_to_all | solution.py:546
  101.8 51.2 %all-to-all-start = ((f32[32,128,128]{2,1,0:T(8,128)}), f32[32,128,128]{2,1,0:T(8,128)}, u32[]{:S(2)}, u32[]{:S(2)}) async-start(f32[32,128,128]{2,1,0:T(8,128)} %bitcast.13), calls=%async_computation | async-start | bytes 4194304 | tf_op jit(solution)/shard_map/all_to_all | solution.py:546
  160.7 25.2 %collective-permute-start.14 = (f32[1024,128]{1,0:T(8,128)S(1)}, f32[1024,128]{1,0:T(8,128)S(1)}, u32[]{:S(2)}, u32[]{:S(2)}) collective-permute-start(f32[1024,128]{1,0:T(8,128)S(1)} %get-tuple-element.99), channel_id=1, source_target_pairs={{0,1},{1,0},{2,3},{3,2},{4,5},{5,4},{6,7},{7,6},{8,9},{9,8},{10,11... | collective-permute-start | bytes 1572872 | tf_op jit(solution)/shard_map/ppermute | solution.py:509
  164.5 38.2 %collective-permute-start.16 = (f32[1024,128]{1,0:T(8,128)S(1)}, f32[1024,128]{1,0:T(8,128)S(1)}, u32[]{:S(2)}, u32[]{:S(2)}) collective-permute-start(f32[1024,128]{1,0:T(8,128)S(1)} %get-tuple-element.101), channel_id=1, source_target_pairs={{0,2},{1,3},{2,0},{3,1},{4,6},{5,7},{6,4},{7,5},{8,10},{9,11},{10,... | collective-permute-start | bytes 1572872 | tf_op jit(solution)/shard_map/ppermute | solution.py:509
  164.6 43.2 %collective-permute-start.18 = (f32[1024,128]{1,0:T(8,128)S(1)}, f32[1024,128]{1,0:T(8,128)S(1)}, u32[]{:S(2)}, u32[]{:S(2)}) collective-permute-start(f32[1024,128]{1,0:T(8,128)S(1)} %get-tuple-element.103), channel_id=1, source_target_pairs={{0,3},{1,2},{2,1},{3,0},{4,7},{5,6},{6,5},{7,4},{8,11},{9,10},{10,... | collective-permute-start | bytes 1572872 | tf_op jit(solution)/shard_map/ppermute | solution.py:509
  196.7 21.8 %collective-permute-start.15 = (f32[1024,128]{1,0:T(8,128)S(1)}, f32[1024,128]{1,0:T(8,128)S(1)}, u32[]{:S(2)}, u32[]{:S(2)}) collective-permute-start(f32[1024,128]{1,0:T(8,128)S(1)} %get-tuple-element.100), channel_id=1, source_target_pairs={{0,1},{1,0},{2,3},{3,2},{4,5},{5,4},{6,7},{7,6},{8,9},{9,8},{10,11... | collective-permute-start | bytes 1572872 | tf_op jit(solution)/shard_map/ppermute | solution.py:509
  207.7 39.9 %collective-permute-start.17 = (f32[1024,128]{1,0:T(8,128)S(1)}, f32[1024,128]{1,0:T(8,128)S(1)}, u32[]{:S(2)}, u32[]{:S(2)}) collective-permute-start(f32[1024,128]{1,0:T(8,128)S(1)} %get-tuple-element.102), channel_id=1, source_target_pairs={{0,2},{1,3},{2,0},{3,1},{4,6},{5,7},{6,4},{7,5},{8,10},{9,11},{10,... | collective-permute-start | bytes 1572872 | tf_op jit(solution)/shard_map/ppermute | solution.py:509
  212.8 34.8 %collective-permute-start.19 = (f32[1024,128]{1,0:T(8,128)S(1)}, f32[1024,128]{1,0:T(8,128)S(1)}, u32[]{:S(2)}, u32[]{:S(2)}) collective-permute-start(f32[1024,128]{1,0:T(8,128)S(1)} %get-tuple-element.104), channel_id=1, source_target_pairs={{0,3},{1,2},{2,1},{3,0},{4,7},{5,6},{6,5},{7,4},{8,11},{9,10},{10,... | collective-permute-start | bytes 1572872 | tf_op jit(solution)/shard_map/ppermute | solution.py:509
  261.9 60.9 %all-to-all-start.3 = ((f32[32,128,128]{2,1,0:T(8,128)}), f32[32,128,128]{2,1,0:T(8,128)S(1)}, u32[]{:S(2)}, u32[]{:S(2)}) async-start(f32[32,128,128]{2,1,0:T(8,128)} %copy-done), calls=%async_computation.3 | async-start | bytes 4194304 | tf_op jit(solution)/shard_map/all_to_all | solution.py:566
  292.9 29.9 %collective-permute-start.28 = (f32[128]{0:T(128)S(1)}, f32[128]{0:T(128)S(1)}, u32[]{:S(2)}, u32[]{:S(2)}) collective-permute-start(f32[128]{0:T(128)S(1)} %add_add_fusion.1), channel_id=1, source_target_pairs={{0,2},{1,3},{2,0},{3,1},{4,6},{5,7},{6,4},{7,5},{8,10},{9,11},{10,... | collective-permute-start | bytes 1544 | tf_op jit(solution)/shard_map/ppermute | solution.py:509
  293.0 29.8 %collective-permute-start.29 = (f32[128]{0:T(128)S(1)}, f32[128]{0:T(128)S(1)}, u32[]{:S(2)}, u32[]{:S(2)}) collective-permute-start(f32[128]{0:T(128)S(1)} %add_add_fusion.1), channel_id=1, source_target_pairs={{0,3},{1,2},{2,1},{3,0},{4,7},{5,6},{6,5},{7,4},{8,11},{9,10},{10,... | collective-permute-start | bytes 1544 | tf_op jit(solution)/shard_map/ppermute | solution.py:509
  295.5 27.3 %collective-permute-start.27 = (f32[128]{0:T(128)S(1)}, f32[128]{0:T(128)S(1)}, u32[]{:S(2)}, u32[]{:S(2)}) collective-permute-start(f32[128]{0:T(128)S(1)} %add_add_fusion.1), channel_id=1, source_target_pairs={{0,1},{1,0},{2,3},{3,2},{4,5},{5,4},{6,7},{7,6},{8,9},{9,8},{10,11... | collective-permute-start | bytes 1544 | tf_op jit(solution)/shard_map/ppermute | solution.py:509
  322.8 51.0 %all-to-all-start.2 = ((f32[32,128,128]{2,1,0:T(8,128)}), f32[32,128,128]{2,1,0:T(8,128)}, u32[]{:S(2)}, u32[]{:S(2)}) async-start(f32[32,128,128]{2,1,0:T(8,128)} %get-tuple-element.105), calls=%async_computation.2 | async-start | bytes 4194304 | tf_op jit(solution)/shard_map/all_to_all | solution.py:566
  337.8 35.9 %collective-permute-start.32 = (f32[512,128]{1,0:T(8,128)}, f32[512,128]{1,0:T(8,128)S(1)}, u32[]{:S(2)}, u32[]{:S(2)}) collective-permute-start(f32[512,128]{1,0:T(8,128)} %get-tuple-element.117), channel_id=1, source_target_pairs={{0,12},{4,8},{8,4},{12,0},{16,28},{20,24},{24,20},{28,16},{1,13},{... | collective-permute-start | bytes 786440 | tf_op jit(solution)/shard_map/ppermute | solution.py:509
  338.2 35.6 %collective-permute-start.33 = (f32[512,128]{1,0:T(8,128)}, f32[512,128]{1,0:T(8,128)S(1)}, u32[]{:S(2)}, u32[]{:S(2)}) collective-permute-start(f32[512,128]{1,0:T(8,128)} %get-tuple-element.118), channel_id=1, source_target_pairs={{0,16},{4,20},{8,24},{12,28},{16,0},{20,4},{24,8},{28,12},{1,17},{... | collective-permute-start | bytes 786440 | tf_op jit(solution)/shard_map/ppermute | solution.py:509
  339.6 34.2 %collective-permute-start.34 = (f32[512,128]{1,0:T(8,128)S(1)}, f32[512,128]{1,0:T(8,128)S(1)}, u32[]{:S(2)}, u32[]{:S(2)}) collective-permute-start(f32[512,128]{1,0:T(8,128)S(1)} %get-tuple-element.119), channel_id=1, source_target_pairs={{0,20},{4,16},{8,28},{12,24},{16,4},{20,0},{24,12},{28,8},{1,21},{... | collective-permute-start | bytes 786440 | tf_op jit(solution)/shard_map/ppermute | solution.py:509
  339.8 34.0 %collective-permute-start.35 = (f32[512,128]{1,0:T(8,128)S(1)}, f32[512,128]{1,0:T(8,128)S(1)}, u32[]{:S(2)}, u32[]{:S(2)}) collective-permute-start(f32[512,128]{1,0:T(8,128)S(1)} %get-tuple-element.120), channel_id=1, source_target_pairs={{0,24},{4,28},{8,16},{12,20},{16,8},{20,12},{24,0},{28,4},{1,25},{... | collective-permute-start | bytes 786440 | tf_op jit(solution)/shard_map/ppermute | solution.py:509
  350.9 25.4 %collective-permute-start.36 = (f32[512,128]{1,0:T(8,128)S(1)}, f32[512,128]{1,0:T(8,128)S(1)}, u32[]{:S(2)}, u32[]{:S(2)}) collective-permute-start(f32[512,128]{1,0:T(8,128)S(1)} %get-tuple-element.121), channel_id=1, source_target_pairs={{0,28},{4,24},{8,20},{12,16},{16,12},{20,8},{24,4},{28,0},{1,29},{... | collective-permute-start | bytes 786440 | tf_op jit(solution)/shard_map/ppermute | solution.py:509
  391.2 21.7 %collective-permute-start.41 = (f32[512,128]{1,0:T(8,128)S(1)}, f32[512,128]{1,0:T(8,128)S(1)}, u32[]{:S(2)}, u32[]{:S(2)}) collective-permute-start(f32[512,128]{1,0:T(8,128)S(1)} %get-tuple-element.135), channel_id=1, source_target_pairs={{0,8},{4,12},{8,0},{12,4},{16,24},{20,28},{24,16},{28,20},{1,9},{5... | collective-permute-start | bytes 786440 | tf_op jit(solution)/shard_map/ppermute | solution.py:509
  (64 other events, 818.1 us)
